TPU v7x, 128 devices: a whole 4x4x4 slice. The times are simulated.
128 devices in a mesh: blk: 64 (over z, x, y_lo, core), rep: 2 (over y_hi).
Axes of the slice: x: 4, y: 4 (y_hi: 2, y_lo: 2; y = y_hi * 2 + y_lo), z: 4, core: 2. Of those that a mesh axis runs over, the one named last changes fastest.
Arguments:
- tokens: int32 [32768, 69], P('blk'), may hold values from 0 to 63
- lengths: int32 [32768], P('blk'), may hold values from 16 to 69
- embed: bfloat16 [64, 256], replicated, may hold values from -6 to 6
- conv_w: bfloat16 [7, 32, 256], replicated, may hold values from -0.375 to 0.375
- conv_b: float32 [256], replicated, may hold values from -3 to 3
- inv_len: float32 [256], replicated, may hold values from 0.05 to 0.3
- hyper: float32 [2], replicated, may hold values from 0.5 to 2
- probes: bfloat16 [32768, 64], P('blk'), may hold values from -6 to 6
- prev_probes: bfloat16 [32768, 64], P(('blk', 'rep')), may hold values from -6 to 6
- coupling: float32 [64, 64], replicated, may hold values from -12 to 12
Outputs:
- block_a: float32 [64, 64], replicated
- block_r: float32 [64, 64], replicated
- next_probes: float32 [32768, 64], P(('blk', 'rep'))
All inputs are finite; a program needn't handle non-finite values.
Results may differ from a plain program's by a relative error of at most 0.0065.
Values may be sent and summed in bfloat16 or wider, within the bound.
No kernel may reach another device: no remote copies, remote signals or barrier semaphores. Data moves between devices by JAX's collectives and lax.ppermute only.
A program may use at most 128 MiB of HBM per device.

v0:
```python
import math

import jax
import jax.numpy as jnp
from jax import lax
from jax.sharding import PartitionSpec as P


def upper_factor(gram):
    order = gram.shape[0]
    index_row = jnp.arange(order, dtype=jnp.int32)

    def column_step(column, carry):
        work, lower = carry
        pivot = lax.dynamic_slice(work, (column, column), (1, 1))[0, 0]
        vector = lax.dynamic_slice_in_dim(work, column, 1, 1)[:, 0]
        vector = jnp.where(index_row >= column, vector * lax.rsqrt(pivot), 0.0)
        lower = lower + vector[:, None] * (index_row == column).astype(jnp.float32)[None, :]
        work = work - vector[:, None] * vector[None, :]
        return (work, lower)

    _, lower = lax.fori_loop(0, order, column_step, (gram, jnp.zeros_like(gram)))
    return lower.T


def upper_inverse(upper):
    order = upper.shape[0]
    index_row = jnp.arange(order, dtype=jnp.int32)

    def row_step(count, solved):
        row = order - 1 - count
        upper_row = lax.dynamic_slice_in_dim(upper, row, 1, 0)
        diag_value = lax.dynamic_slice(upper, (row, row), (1, 1))[0, 0]
        unit_row = (index_row == row).astype(jnp.float32)[None, :]
        product = jnp.dot(
            upper_row, solved, precision=lax.Precision.HIGHEST, preferred_element_type=jnp.float32
        )
        new_row = (unit_row - product) / diag_value
        return solved + (index_row == row).astype(jnp.float32)[:, None] * new_row

    return lax.fori_loop(0, order, row_step, jnp.zeros_like(upper))


def dense_taps(conv_w, channels):
    tap_count, group_width, _ = conv_w.shape
    group_count = channels // group_width
    tiled = jnp.tile(conv_w, (1, group_count, 1))
    in_group = jnp.arange(channels, dtype=jnp.int32) // group_width
    same_group = (in_group[:, None] == in_group[None, :]).astype(jnp.bfloat16)
    return tiled * same_group[None, :, :]


def conv_features(tokens, lengths, embed, conv_w, conv_b, inv_len):
    row_count, seq_len = tokens.shape
    vocab_size, channels = embed.shape
    tap_count = conv_w.shape[0]
    positions = (seq_len - tap_count) // 2 + 1
    block_rows = math.gcd(row_count, 256)
    block_count = row_count // block_rows
    tap_weights = dense_taps(conv_w, channels)
    vocab_ids = jnp.arange(vocab_size, dtype=jnp.int32)[None, :]

    def one_block(pair):
        tok_block, len_block = pair
        running = jnp.zeros((block_rows * positions, channels), jnp.float32)
        for tap_index in range(tap_count):
            tap_tokens = lax.slice(
                tok_block, (0, tap_index), (block_rows, tap_index + 2 * (positions - 1) + 1), (1, 2)
            )
            onehot = (tap_tokens.reshape(-1, 1) == vocab_ids).astype(jnp.bfloat16)
            embedded = jnp.dot(onehot, embed, preferred_element_type=jnp.float32).astype(
                jnp.bfloat16
            )
            running = running + jnp.dot(
                embedded, tap_weights[tap_index], preferred_element_type=jnp.float32
            )
        preact = running.reshape(block_rows, positions, channels) + conv_b
        counts = (len_block - tap_count) // 2 + 1
        valid_mask = (jnp.arange(positions, dtype=jnp.int32)[None, :] < counts[:, None]).astype(
            jnp.float32
        )
        activated = jax.nn.gelu(preact, approximate=True) * valid_mask[:, :, None]
        pooled = jnp.sum(activated, axis=1) / counts.astype(jnp.float32)[:, None]
        row_mean = jnp.mean(pooled, axis=1, keepdims=True)
        centered = pooled - row_mean
        row_var = jnp.mean(centered * centered, axis=1, keepdims=True)
        normed = centered * lax.rsqrt(row_var + 1e-05)
        return (normed * inv_len).astype(jnp.bfloat16)

    result = lax.map(
        one_block,
        (
            tokens.reshape(block_count, block_rows, seq_len),
            lengths.reshape(block_count, block_rows),
        ),
    )
    return result.reshape(row_count, channels)


def squares_of(feat_rows):
    wide = feat_rows.astype(jnp.float32)
    return jnp.sum(wide * wide, axis=1)


def kernel_block(rows_feat, rows_sq, amplitude, col_feat, col_probes):
    col_sq = squares_of(col_feat)
    inner_prod = lax.dot_general(
        rows_feat, col_feat, (((1,), (1,)), ((), ())), preferred_element_type=jnp.float32
    )
    distance = jnp.maximum(rows_sq[:, None] + col_sq[None, :] - 2.0 * inner_prod, 0.0)
    weights = (amplitude * jnp.exp(-0.5 * distance)).astype(jnp.bfloat16)
    return jnp.dot(weights, col_probes, preferred_element_type=jnp.float32)


def make_fold(rows_feat, amplitude):
    rows_sq = squares_of(rows_feat)

    def accumulate(running, piece, first_row):
        col_feat, col_probes = piece
        col_count = col_feat.shape[0]
        col_width = math.gcd(col_count, 1024)
        col_blocks = col_feat.reshape(col_count // col_width, col_width, col_feat.shape[1])
        probe_blocks = col_probes.reshape(col_count // col_width, col_width, col_probes.shape[1])

        def advance(partial_value, block_pair):
            return (
                partial_value
                + kernel_block(rows_feat, rows_sq, amplitude, block_pair[0], block_pair[1]),
                None,
            )

        result, _ = lax.scan(advance, running, (col_blocks, probe_blocks))
        return result

    return accumulate


def gram_of(left, right):
    return lax.dot_general(
        left,
        right,
        (((0,), (0,)), ((), ())),
        precision=lax.Precision.HIGHEST,
        preferred_element_type=jnp.float32,
    )


def per_device(
    tokens, lengths, embed, conv_w, conv_b, inv_len, hyper, probes, prev_probes, coupling
):
    feat = conv_features(tokens, lengths, embed, conv_w, conv_b, inv_len)
    row_count = feat.shape[0]
    probe_width = probes.shape[1]
    half_rows = row_count // lax.axis_size("rep")
    rep_index = lax.axis_index("rep")
    total_rows = row_count * lax.axis_size("blk")
    inv_root = 1.0 / math.sqrt(total_rows)
    amplitude = hyper[0]
    noise_var = hyper[1]
    own_feat = lax.dynamic_slice_in_dim(feat, rep_index * half_rows, half_rows, 0)
    own_probes = lax.dynamic_slice_in_dim(probes, rep_index * half_rows, half_rows, 0)
    accumulate = make_fold(own_feat, amplitude)
    initial = jnp.zeros((half_rows, probe_width), jnp.float32)
    applied = accumulate(
        initial,
        (
            lax.all_gather(feat, "blk", axis=0, tiled=True),
            lax.all_gather(probes, "blk", axis=0, tiled=True),
        ),
        jnp.int32(0),
    )
    own_wide = own_probes.astype(jnp.float32)
    applied = applied + noise_var * own_wide
    basis_half = own_wide * inv_root
    coupled = (
        jnp.dot(
            prev_probes.astype(jnp.float32),
            coupling.T,
            precision=lax.Precision.HIGHEST,
            preferred_element_type=jnp.float32,
        )
        * inv_root
    )
    image = applied * inv_root - coupled
    block_a = lax.psum(gram_of(basis_half, image), ("blk", "rep"))
    resid = image - jnp.dot(
        basis_half, block_a, precision=lax.Precision.HIGHEST, preferred_element_type=jnp.float32
    )
    gram = lax.psum(gram_of(resid, resid), ("blk", "rep"))
    upper = upper_factor(gram)
    inverse = upper_inverse(upper)
    next_probes = jnp.dot(
        resid, inverse, precision=lax.Precision.HIGHEST, preferred_element_type=jnp.float32
    ) * math.sqrt(total_rows)
    return (block_a, upper, next_probes)


def solution(mesh):
    return jax.shard_map(
        per_device,
        mesh=mesh,
        in_specs=(
            P("blk", None),
            P("blk"),
            P(),
            P(),
            P(),
            P(),
            P(),
            P("blk", None),
            P(("blk", "rep"), None),
            P(),
        ),
        out_specs=(P(), P(), P(("blk", "rep"), None)),
        check_vma=False,
    )
```

profile of v0, /device:TPU:2, one launch (start us, length us, event | category | flops | bytes accessed | tf_op | source)
XLA Modules:
  0.0 695.9 jit_solution(5124918440417495933)
XLA Ops:
  10.8 118.4 %while.58 = (s32[]{:T(128)}, bf16[2,256,256]{2,1,0:T(8,128)(2,1)S(1)}, s32[2,256,69]{2,1,0:T(8,128)S(1)}, bf16[64,256]{1,0:T(8,128)(2,1)}, bf16[7,256,256]{2,1,0...) while((s32[]{:T(128)}, ...), condition=%wide.region_4.5_spmd.clone.clone, body=%wide.region_0.4_spmd.clone.clone.sunk | while | flops 9449918464 | bytes 104601792 | solution.py:90
  12.2 6.5 fusion.163
  20.1 7.0 %convolution_add_fusion.11 = f32[8192,256]{1,0:T(8,128)} fusion(f32[8192,256]{1,0:T(8,128)} %fusion.163, bf16[64,256]{1,0:T(8,128)(2,1)S(1)} %copy-done.1, s32[8192]{0:T(1024)S(1)} %eq.424, bf16[7,256,256]{2,1,0:T(8,128)(2,1)S(1)} %get-tuple-element.697), kind=kOutput, calls=%fused_computation.9.clone.1 | convolution fusion | flops 1346895872 | bytes 16973824 | tf_op jit(solution)/shard_map/while/body/eval_jaxpr/dot_general | solution.py:74
  28.4 7.0 %convolution_add_fusion.12 = f32[8192,256]{1,0:T(8,128)} fusion(f32[8192,256]{1,0:T(8,128)} %convolution_add_fusion.11, bf16[64,256]{1,0:T(8,128)(2,1)S(1)} %copy-done.1, s32[8192]{0:T(1024)S(1)} %eq.425, bf16[7,256,256]{2,1,0:T(8,128)(2,1)S(1)} %get-tuple-element.697), kind=kOutput, calls=%fused_computation.8.clone.1 | convolution fusion | flops 1346895872 | bytes 16973824 | tf_op jit(solution)/shard_map/while/body/eval_jaxpr/dot_general | solution.py:74
  36.8 7.0 %convolution_add_fusion.13 = f32[8192,256]{1,0:T(8,128)} fusion(f32[8192,256]{1,0:T(8,128)} %convolution_add_fusion.12, bf16[64,256]{1,0:T(8,128)(2,1)S(1)} %copy-done.1, s32[8192]{0:T(1024)S(1)} %eq.426, bf16[7,256,256]{2,1,0:T(8,128)(2,1)S(1)} %get-tuple-element.697), kind=kOutput, calls=%fused_computation.7.clone.1 | convolution fusion | flops 1346895872 | bytes 16973824 | tf_op jit(solution)/shard_map/while/body/eval_jaxpr/dot_general | solution.py:74
  45.2 7.0 %convolution_add_fusion.14 = f32[8192,256]{1,0:T(8,128)} fusion(f32[8192,256]{1,0:T(8,128)} %convolution_add_fusion.13, bf16[64,256]{1,0:T(8,128)(2,1)S(1)} %copy-done.1, s32[8192]{0:T(1024)S(1)} %eq.427, bf16[7,256,256]{2,1,0:T(8,128)(2,1)S(1)} %get-tuple-element.697), kind=kOutput, calls=%fused_computation.6.clone.1 | convolution fusion | flops 1346895872 | bytes 16973824 | tf_op jit(solution)/shard_map/while/body/eval_jaxpr/dot_general | solution.py:74
  53.5 7.0 %convolution_add_fusion.15 = f32[8192,256]{1,0:T(8,128)} fusion(f32[8192,256]{1,0:T(8,128)} %convolution_add_fusion.14, bf16[64,256]{1,0:T(8,128)(2,1)S(1)} %copy-done.1, s32[8192]{0:T(1024)S(1)} %eq.428, bf16[7,256,256]{2,1,0:T(8,128)(2,1)S(1)} %get-tuple-element.697), kind=kOutput, calls=%fused_computation.5.clone.1 | convolution fusion | flops 1346895872 | bytes 16973824 | tf_op jit(solution)/shard_map/while/body/eval_jaxpr/dot_general | solution.py:74
  62.0 7.3 %fusion.164 = f32[256,256]{1,0:T(8,128)S(1)} fusion(f32[256,32]{1,0:T(8,128)S(1)} %fusion.162, f32[256]{0:T(256)S(1)} %copy-done.7, f32[8192,256]{1,0:T(8,128)} %convolution_add_fusion.15, bf16[7,256,256]{2,1,0:T(8,128)(2,1)S(1)} %get-tuple-element.697, bf16[64,256]{1,0:T(8,128)(2,1)S(1)} %copy-done.1, s32[8192]{0:T(1024)S(1)} %eq.429), kind=kOutput, calls=%fused_computation.32.clone.1 | convolution fusion | flops 1369899008 | bytes 8979456 | tf_op jit(solution)/shard_map/while/body/eval_jaxpr/dot_general | solution.py:74
  71.3 6.5 fusion.163
  79.2 7.0 %convolution_add_fusion.11 = f32[8192,256]{1,0:T(8,128)} fusion(f32[8192,256]{1,0:T(8,128)} %fusion.163, bf16[64,256]{1,0:T(8,128)(2,1)S(1)} %copy-done.1, s32[8192]{0:T(1024)S(1)} %eq.424, bf16[7,256,256]{2,1,0:T(8,128)(2,1)S(1)} %get-tuple-element.697), kind=kOutput, calls=%fused_computation.9.clone.1 | convolution fusion | flops 1346895872 | bytes 16973824 | tf_op jit(solution)/shard_map/while/body/eval_jaxpr/dot_general | solution.py:74
  87.6 7.0 %convolution_add_fusion.12 = f32[8192,256]{1,0:T(8,128)} fusion(f32[8192,256]{1,0:T(8,128)} %convolution_add_fusion.11, bf16[64,256]{1,0:T(8,128)(2,1)S(1)} %copy-done.1, s32[8192]{0:T(1024)S(1)} %eq.425, bf16[7,256,256]{2,1,0:T(8,128)(2,1)S(1)} %get-tuple-element.697), kind=kOutput, calls=%fused_computation.8.clone.1 | convolution fusion | flops 1346895872 | bytes 16973824 | tf_op jit(solution)/shard_map/while/body/eval_jaxpr/dot_general | solution.py:74
  95.9 7.0 %convolution_add_fusion.13 = f32[8192,256]{1,0:T(8,128)} fusion(f32[8192,256]{1,0:T(8,128)} %convolution_add_fusion.12, bf16[64,256]{1,0:T(8,128)(2,1)S(1)} %copy-done.1, s32[8192]{0:T(1024)S(1)} %eq.426, bf16[7,256,256]{2,1,0:T(8,128)(2,1)S(1)} %get-tuple-element.697), kind=kOutput, calls=%fused_computation.7.clone.1 | convolution fusion | flops 1346895872 | bytes 16973824 | tf_op jit(solution)/shard_map/while/body/eval_jaxpr/dot_general | solution.py:74
  104.3 7.0 %convolution_add_fusion.14 = f32[8192,256]{1,0:T(8,128)} fusion(f32[8192,256]{1,0:T(8,128)} %convolution_add_fusion.13, bf16[64,256]{1,0:T(8,128)(2,1)S(1)} %copy-done.1, s32[8192]{0:T(1024)S(1)} %eq.427, bf16[7,256,256]{2,1,0:T(8,128)(2,1)S(1)} %get-tuple-element.697), kind=kOutput, calls=%fused_computation.6.clone.1 | convolution fusion | flops 1346895872 | bytes 16973824 | tf_op jit(solution)/shard_map/while/body/eval_jaxpr/dot_general | solution.py:74
  112.6 7.0 %convolution_add_fusion.15 = f32[8192,256]{1,0:T(8,128)} fusion(f32[8192,256]{1,0:T(8,128)} %convolution_add_fusion.14, bf16[64,256]{1,0:T(8,128)(2,1)S(1)} %copy-done.1, s32[8192]{0:T(1024)S(1)} %eq.428, bf16[7,256,256]{2,1,0:T(8,128)(2,1)S(1)} %get-tuple-element.697), kind=kOutput, calls=%fused_computation.5.clone.1 | convolution fusion | flops 1346895872 | bytes 16973824 | tf_op jit(solution)/shard_map/while/body/eval_jaxpr/dot_general | solution.py:74
  121.1 7.3 %fusion.164 = f32[256,256]{1,0:T(8,128)S(1)} fusion(f32[256,32]{1,0:T(8,128)S(1)} %fusion.162, f32[256]{0:T(256)S(1)} %copy-done.7, f32[8192,256]{1,0:T(8,128)} %convolution_add_fusion.15, bf16[7,256,256]{2,1,0:T(8,128)(2,1)S(1)} %get-tuple-element.697, bf16[64,256]{1,0:T(8,128)(2,1)S(1)} %copy-done.1, s32[8192]{0:T(1024)S(1)} %eq.429), kind=kOutput, calls=%fused_computation.32.clone.1 | convolution fusion | flops 1369899008 | bytes 8979456 | tf_op jit(solution)/shard_map/while/body/eval_jaxpr/dot_general | solution.py:74
  131.6 8.4 %copy.20 = bf16[32768,64]{1,0:T(8,128)(2,1)} copy(bf16[32768,64]{0,1:T(8,128)(2,1)} %all-gather.5.cloned.1.call-done) | data formatting | bytes 8388608 | tf_op jit(solution)/shard_map/all_gather | solution.py:168
  140.0 113.7 %all-gather.3.cloned.1.call-done = bf16[32768,256]{1,0:T(8,128)(2,1)} async-done(((bf16[512,256]{1,0:T(8,128)(2,1)}), bf16[32768,256]{1,0:T(8,128)(2,1)}) %all-gather.3.cloned.1.call-update) | async-done | bytes 16777232 | tf_op jit(solution)/shard_map/all_gather | solution.py:167
  253.7 119.1 %while.59 = (s32[]{:T(128)}, f32[256,64]{0,1:T(8,128)S(1)}, f32[]{:T(128)}, f32[256]{0:T(256)S(1)}, bf16[32,1024,256]{2,1,0:T(8,128)(2,1)}, /*index=5*/bf16[256,...) while((s32[]{:T(128)}, f32[256,64]{0,1:T(8,128)S(1)}, f32[]{:T(128)}, ...), condition=%wide.region_8.9_spmd.clone, body=%wide.region_6.8_spmd.clone.sunk | while | flops 170425344 | bytes 1583723 | solution.py:132
  255.0 2.4 fusion.170
  258.8 2.4 fusion.170
  262.5 2.4 fusion.170
  266.2 2.4 fusion.170
  269.9 2.4 fusion.170
  273.7 2.4 fusion.170
  277.4 2.4 fusion.170
  281.1 2.4 fusion.170
  292.3 2.4 fusion.170
  296.0 2.4 fusion.170
  373.9 64.6 %psum.14 = f32[64,64]{1,0:T(8,128)S(1)} all-reduce(f32[64,64]{1,0:T(8,128)S(1)} %fusion.90), channel_id=1, replica_groups=mesh['blk'=64,'rep'=2] {'blk','rep'}, use_global_device_ids=true, to_apply=%region_9.10 | all-reduce | flops 4096 | bytes 32768 | tf_op jit(solution)/shard_map/psum | solution.py:185
  439.0 62.9 %psum.15 = f32[64,64]{1,0:T(8,128)S(1)} all-reduce(f32[64,64]{1,0:T(8,128)S(1)} %fusion.104), channel_id=1, replica_groups=mesh['blk'=64,'rep'=2] {'blk','rep'}, use_global_device_ids=true, to_apply=%region_10.11 | all-reduce | flops 4096 | bytes 32768 | tf_op jit(solution)/shard_map/psum | solution.py:189
  502.0 92.5 %while.61 = (s32[]{:T(128)}, f32[64,64]{0,1:T(8,128)S(1)}, f32[64,64]{0,1:T(8,128)S(1)}, s32[]{:T(128)}, s32[]{:T(128)}) while((s32[]{:T(128)}, f32[64,64]{0,1:T(8,128)S(1)}, f32[64,64]{0,1:T(8,128)S(1)}, s32[]{:T(128)}, s32[]{:T(128)}) %tuple.135), condition=%wide.region_12.13_spmd.clone.clone, body=%wide.region_11.12_spmd.clone.clone.sunk | while | flops 20995 | bytes 70751 | solution.py:22
  594.5 93.7 %while.60 = (s32[]{:T(128)}, f32[64,64]{1,0:T(8,128)S(1)}, f32[64,64]{1,0:T(8,128)S(1)}, s32[]{:T(128)}, s32[]{:T(128)}, /*index=5*/s32[]{:T(128)}, s32[]{:T(128)}) while((s32[]{:T(128)}, f32[64,64]{1,0:T(8,128)S(1)}, f32[64,64]{1,0:T(8,128)S(1)}, s32[]{:T(128)}, s32[]{:T(128)}, /*index=5*/s32[]{:T(128)}, s32[]{:T(128)}) %tuple.147), condition=%wide.region_14.15_spmd.clone, body=%wide.region_13.14_spmd.clone.sunk | while | flops 65927 | bytes 67234 | solution.py:41
  (724 shorter events, 261.1 us)
Async XLA Ops:
  7.2 365.7 %copy-start = (bf16[256,64]{0,1:T(8,128)(2,1)S(1)}, bf16[256,64]{0,1:T(8,128)(2,1)}, u32[]{:S(2)}) copy-start(bf16[256,64]{0,1:T(8,128)(2,1)} %param.26) | copy-start | bytes 98308
  7.2 124.5 %all-gather.5.cloned.1.call-start = ((), (), s32[]{:S(2)}) async-start(), calls=%async_computation.1 | async-start | bytes 4259840 | tf_op jit(solution)/shard_map/all_gather | solution.py:168
  7.9 245.8 %all-gather.3.cloned.1.call-start = ((), (), s32[]{:S(2)}) async-start(), calls=%async_computation | async-start | bytes 17039360 | tf_op jit(solution)/shard_map/all_gather | solution.py:167
  10.8 119.2 %copy-start.9 = (f32[2]{0:T(128)S(1)}, f32[2]{0:T(128)}, u32[]{:S(2)}) copy-start(f32[2]{0:T(128)} %param.24) | copy-start | bytes 28
  10.8 9.2 %copy-start.1 = (bf16[64,256]{1,0:T(8,128)(2,1)S(1)}, bf16[64,256]{1,0:T(8,128)(2,1)}, u32[]{:S(2)}) copy-start(bf16[64,256]{1,0:T(8,128)(2,1)} %get-tuple-element.696) | copy-start | bytes 98308 | tf_op jit(solution)/shard_map/while
  53.5 8.5 %copy-start.7 = (f32[256]{0:T(256)S(1)}, f32[256]{0:T(256)}, u32[]{:S(2)}) copy-start(f32[256]{0:T(256)} %get-tuple-element.698) | copy-start | bytes 3076 | tf_op jit(solution)/shard_map/while
  60.5 9.2 %copy-start.8 = (f32[256]{0:T(256)S(1)}, f32[256]{0:T(256)}, u32[]{:S(2)}) copy-start(f32[256]{0:T(256)} %get-tuple-element.700) | copy-start | bytes 3076 | tf_op jit(solution)/shard_map/while
  69.9 9.2 %copy-start.1 = (bf16[64,256]{1,0:T(8,128)(2,1)S(1)}, bf16[64,256]{1,0:T(8,128)(2,1)}, u32[]{:S(2)}) copy-start(bf16[64,256]{1,0:T(8,128)(2,1)} %get-tuple-element.696) | copy-start | bytes 98308 | tf_op jit(solution)/shard_map/while
  112.6 8.5 %copy-start.7 = (f32[256]{0:T(256)S(1)}, f32[256]{0:T(256)}, u32[]{:S(2)}) copy-start(f32[256]{0:T(256)} %get-tuple-element.698) | copy-start | bytes 3076 | tf_op jit(solution)/shard_map/while
  119.6 9.2 %copy-start.8 = (f32[256]{0:T(256)S(1)}, f32[256]{0:T(256)}, u32[]{:S(2)}) copy-start(f32[256]{0:T(256)} %get-tuple-element.700) | copy-start | bytes 3076 | tf_op jit(solution)/shard_map/while
  129.2 0.7 copy-start.3
  253.7 119.2 %copy-start.4 = (bf16[512,64]{0,1:T(8,128)(2,1)S(1)}, bf16[512,64]{0,1:T(8,128)(2,1)}, u32[]{:S(2)}) copy-start(bf16[512,64]{0,1:T(8,128)(2,1)} %param.25) | copy-start | bytes 196612
  253.7 119.2 %copy-start.6 = (f32[64,64]{1,0:T(8,128)S(1)}, f32[64,64]{1,0:T(8,128)}, u32[]{:S(2)}) copy-start(f32[64,64]{1,0:T(8,128)} %param.27) | copy-start | bytes 49156
  438.5 250.6 %copy-start.5 = (f32[64,64]{1,0:T(8,128)}, f32[64,64]{1,0:T(8,128)S(1)}, u32[]{:S(2)}) copy-start(f32[64,64]{1,0:T(8,128)S(1)} %psum.14) | copy-start | bytes 49156
  688.2 0.9 copy-start.2
Sparse Core Ops, SparseCore 0:
  9.7 106.8 all-gather.4
  130.1 123.6 all-gather.2
where the time goes:
time: 702 us; the launch traced here: 696 us
  matrix products  228 us (32%)
  blocking collectives  128 us (18%)
  waiting for transfers between devices  114 us (16%)
  local copies, waits for them, and re-layouts  106 us (15%)
  other arithmetic  56.5 us (8%)
  loops' own time  49.2 us (7%)
  between operations  14.2 us (2%)
    all_gather x1, waiting for transfers between devices, per_device(): lax.all_gather(feat, 'blk', axis=0, tiled=True)  114 us
    dot_general x14, matrix products, one_block(): jnp.dot(embedded, tap_weights[tap_index], preferred_element_type=jnp.floa...  97.4 us
    dot_general x32, matrix products, kernel_block(): return jnp.dot(weights, col_probes, preferred_element_type=jnp.float32)  77.9 us
    psum x1, blocking collectives, per_device(): block_a = lax.psum(gram_of(basis_half, image), ('blk', 'rep'))  64.6 us
    psum x1, blocking collectives, per_device(): gram = lax.psum(gram_of(resid, resid), ('blk', 'rep'))  62.9 us
    dot_general x64, matrix products, row_step(): jnp.dot(upper_row, solved, precision=lax.Precision.HIGHEST, preferred_ele...  50.1 us
    another operation x1, loops' own time, upper_factor(): lax.fori_loop(0, order, column_step, (gram, jnp.zeros_like(gram)))  47.4 us
    reduce_sum x33, other arithmetic, squares_of(): return jnp.sum(wide * wide, axis=1)  41.2 us
  transfers between devices with their start and end apart: 2, of which 1 were waited for; matrix products, arithmetic and copies ran while one was open for 19% of the time, Pallas kernels for 0%

commit v1 on v0

v1 whole, which is shorter than its diff:
```python
import functools
import math

import jax
import jax.numpy as jnp
from jax import lax
from jax.experimental import pallas as pl
from jax.experimental.pallas import tpu as pltpu
from jax.sharding import PartitionSpec as P

LOG2E = math.log2(math.e)
HIGHEST = lax.Precision.HIGHEST
AXES = ("blk", "rep")
RING = 4


def coords_of(index):
    rep, blk = index % 2, index // 2
    return blk // 16, (blk // 4) % 4, rep * 2 + (blk // 2) % 2, blk % 2


def index_of(z, x, y, core):
    return (((z * 4 + x) * 2 + y % 2) * 2 + core) * 2 + y // 2


def moved(move):
    return [(i, index_of(*move(*coords_of(i)))) for i in range(128)]


def core_swap():
    return moved(lambda z, x, y, c: (z, x, y, 1 - c))


def shift_y(step):
    return moved(lambda z, x, y, c: (z, x, (y + step) % RING, c))


def shift_z(step):
    return moved(lambda z, x, y, c: ((z + step) % RING, x, y, c))


def shift_x(step):
    return moved(lambda z, x, y, c: (z, (x + step) % RING, y, c))


def shift_by_core(step, core_of_z):
    def move(z, x, y, c):
        if c == core_of_z:
            return (z + step) % RING, x, y, c
        return z, (x + step) % RING, y, c

    return moved(move)


def send(value, perm):
    return lax.ppermute(value, AXES, perm)


def dot(left, right, dims, precision=None):
    return lax.dot_general(
        left, right, (dims, ((), ())), precision=precision, preferred_element_type=jnp.float32
    )


NN = ((1,), (0,))
NT = ((1,), (1,))
TN = ((0,), (0,))


def conv_kernel(
    taps, half_ref, tok_ref, len_ref, embed_ref, w_ref, bias_ref, inv_len_ref, probe_ref,
    cols_ref, rows_ref, table_ref, left_ref, onehot_ref, acc_ref,
):
    vocab, channels = embed_ref.shape
    width = w_ref.shape[1]
    seq, samples = tok_ref.shape
    outputs = (seq - taps) // 2 + 1
    depth = taps * vocab
    group_in = lax.broadcasted_iota(jnp.int32, (channels, channels), 0) // width
    group_out = lax.broadcasted_iota(jnp.int32, (channels, channels), 1) // width
    same = group_in == group_out
    embed = embed_ref[...]
    table_ref[...] = jnp.zeros_like(table_ref)
    for k in range(taps):
        tiled = jnp.concatenate([w_ref[k].astype(jnp.float32)] * (channels // width), axis=0)
        dense = jnp.where(same, tiled, 0.0).astype(jnp.bfloat16)
        entry = dot(embed, dense, NN)
        if k == 0:
            entry = entry + bias_ref[...]
        table_ref[k * vocab : (k + 1) * vocab, :] = entry
    table = table_ref[...].T
    high = table.astype(jnp.bfloat16)
    left_ref[:channels, :] = high
    left_ref[channels:, :] = (table - high.astype(jnp.float32)).astype(jnp.bfloat16)

    vocab_ids = lax.broadcasted_iota(jnp.int32, (vocab, samples), 0)

    def spread(s, carry):
        hit = tok_ref[pl.ds(s, 1), :] == vocab_ids
        onehot_ref[pl.ds(pl.multiple_of(s * vocab, vocab), vocab), :] = jnp.where(
            hit, 1.0, 0.0
        ).astype(jnp.bfloat16)
        return carry

    lax.fori_loop(0, seq, spread, 0, unroll=3)

    counts = (len_ref[...] - taps) // 2 + 1
    acc_ref[...] = jnp.zeros_like(acc_ref)
    root = math.sqrt(2.0 / math.pi)

    def position(t):
        start = pl.multiple_of(t * 2 * vocab, 2 * vocab)
        window = onehot_ref[pl.ds(start, depth), :]
        both = dot(left_ref[:, :depth], window, NN)
        pre = both[:channels] + both[channels:]
        inner = pre * (root + (root * 0.044715) * (pre * pre))
        active = pre + pre * jnp.tanh(inner)
        return jnp.where(t < counts, active, 0.0)

    def positions(step, carry):
        total = position(step * 2) + position(step * 2 + 1)
        acc_ref[...] += total
        return carry

    lax.fori_loop(0, outputs // 2, positions, 0)

    pooled = acc_ref[...] * (0.5 / counts.astype(jnp.float32))
    centered = pooled - jnp.mean(pooled, axis=0, keepdims=True)
    spread_sq = jnp.mean(centered * centered, axis=0, keepdims=True)
    normed = centered * lax.rsqrt(spread_sq + 1e-05)
    feat = (normed.T * inv_len_ref[...]).astype(jnp.bfloat16)
    cols_ref[:samples, :] = feat
    cols_ref[samples:, :] = probe_ref[...]
    rows_ref[...] = feat.astype(jnp.float32).T.astype(jnp.bfloat16)


def conv_features(tok_t, lengths, embed, conv_w, conv_b, inv_len, probes_t, half):
    seq, rows = tok_t.shape
    vocab, channels = embed.shape
    taps = conv_w.shape[0]
    samples = rows // 2
    width = probes_t.shape[0]
    depth = -(-taps * vocab // 128) * 128
    whole = lambda shape: pl.BlockSpec(shape, lambda i, h: (0,) * len(shape))
    part = lambda lead: pl.BlockSpec((lead, samples), lambda i, h: (0, h[0]))
    return pl.pallas_call(
        functools.partial(conv_kernel, taps),
        grid_spec=pltpu.PrefetchScalarGridSpec(
            num_scalar_prefetch=1,
            grid=(1,),
            in_specs=[
                part(seq),
                part(1),
                whole((vocab, channels)),
                whole(conv_w.shape),
                whole((1, channels)),
                whole((1, channels)),
                part(width),
            ],
            out_specs=[whole((samples + width, channels)), whole((channels, samples))],
            scratch_shapes=[
                pltpu.VMEM((depth, channels), jnp.float32),
                pltpu.VMEM((2 * channels, depth), jnp.bfloat16),
                pltpu.VMEM((seq * vocab, samples), jnp.bfloat16),
                pltpu.VMEM((channels, samples), jnp.float32),
            ],
        ),
        out_shape=[
            jax.ShapeDtypeStruct((samples + width, channels), jnp.bfloat16),
            jax.ShapeDtypeStruct((channels, samples), jnp.bfloat16),
        ],
        name="conv_features",
    )(
        half, tok_t, lengths.reshape(1, rows), embed, conv_w,
        conv_b.reshape(1, channels), inv_len.reshape(1, channels), probes_t,
    )


def apply_kernel(row_count, col_count, resume, hyper_ref, *refs):
    row_refs = refs[:row_count]
    col_refs = refs[row_count : row_count + col_count]
    rest = refs[row_count + col_count :]
    start_refs, out_refs, (half_ref,) = rest[: 2 * resume], rest[2 * resume : -1], rest[-1:]
    channels, samples = row_refs[0].shape
    half_rows = row_count // 2
    top = jnp.log2(jnp.full((1, 128), hyper_ref[0], jnp.float32))[:, :1]
    for i, row_ref in enumerate(row_refs):
        wide = row_ref[...].astype(jnp.float32)
        half_ref[i : i + 1, :] = (0.5 * LOG2E) * jnp.sum(wide * wide, axis=0, keepdims=True)
    for side in range(2):
        if resume:
            out_refs[side][...] = start_refs[side][...]
        else:
            out_refs[side][...] = jnp.zeros_like(out_refs[side])

    def block(col):
        feat = col[:samples, :]
        probes = col[samples:, :]
        wide = feat.astype(jnp.float32)
        bias = (0.5 * LOG2E) * jnp.sum(wide * wide, axis=1, keepdims=True) - top
        bias = jnp.broadcast_to(bias, (samples, samples))
        for i, row_ref in enumerate(row_refs):
            inner = dot(feat, row_ref[...], NN)
            power = jnp.minimum(inner * LOG2E - bias - half_ref[i : i + 1, :], top)
            weights = jnp.exp2(power).astype(jnp.bfloat16)
            out_refs[i // half_rows][i % half_rows] += dot(probes, weights, NN)

    for col_ref in col_refs:
        if len(col_ref.shape) == 2:
            block(col_ref[...])
        else:

            def step(j, carry, col_ref=col_ref):
                block(col_ref[j])
                return carry

            lax.fori_loop(0, col_ref.shape[0], step, 0)


def apply_rows(hyper, rows, cols, start=()):
    samples = rows[0].shape[1]
    width = cols[0].shape[-2] - samples
    half_rows = len(rows) // 2
    vmem = pl.BlockSpec(memory_space=pltpu.VMEM)
    blocks = sum(math.prod(c.shape[:-2]) for c in cols)
    pairs = blocks * len(rows) * samples * samples
    out = jax.ShapeDtypeStruct((half_rows, width, samples), jnp.float32)
    return pl.pallas_call(
        functools.partial(apply_kernel, len(rows), len(cols), 1 if start else 0),
        out_shape=[out, out],
        in_specs=[pl.BlockSpec(memory_space=pltpu.SMEM)]
        + [vmem] * (len(rows) + len(cols) + len(start)),
        out_specs=[vmem, vmem],
        scratch_shapes=[pltpu.VMEM((len(rows), samples), jnp.float32)],
        cost_estimate=pl.CostEstimate(
            flops=2 * pairs * (256 + 64), transcendentals=pairs, bytes_accessed=4 << 20
        ),
        name="apply_rows",
    )(hyper, *rows, *cols, *start)


def gram_kernel(
    inv_root, hyper_ref, own_ref, one_ref, two_ref, three_ref, half_ref, probe_ref, prev_ref,
    coupling_ref, image_ref, packed_ref,
):
    del half_ref
    probes = probe_ref[...].astype(jnp.float32)
    coupled = dot(coupling_ref[...], prev_ref[...].astype(jnp.float32), NN, HIGHEST) * inv_root
    applied = (own_ref[...] + two_ref[...]) + (one_ref[...] + three_ref[...])
    applied = applied + hyper_ref[1] * probes
    image = applied * inv_root - coupled
    basis = probes * inv_root
    image_ref[...] = image
    size = image.shape[0]
    packed_ref[:size, :size] = dot(basis, image, NT, HIGHEST)
    packed_ref[:size, size:] = dot(image, image, NT, HIGHEST)
    square = dot(basis, basis, NT, HIGHEST)
    packed_ref[size:, :size] = square[: size // 2]
    packed_ref[size:, size:] = square[size // 2 :]


def gram_stage(inv_root, hyper, parts, probes_t, prev_t, coupling, half):
    size, samples = parts[0].shape
    whole = lambda shape: pl.BlockSpec(shape, lambda i, h: (0,) * len(shape))

    def kernel(half_ref, hyper_ref, own, one, two, three, probe, prev, coup, image, packed):
        gram_kernel(
            inv_root, hyper_ref, own, one, two, three, half_ref, probe, prev, coup, image, packed
        )

    return pl.pallas_call(
        kernel,
        grid_spec=pltpu.PrefetchScalarGridSpec(
            num_scalar_prefetch=1,
            grid=(1,),
            in_specs=[pl.BlockSpec(memory_space=pltpu.SMEM)]
            + [whole((size, samples))] * 4
            + [
                pl.BlockSpec((size, samples), lambda i, h: (0, h[0])),
                whole((size, samples)),
                whole((size, size)),
            ],
            out_specs=[whole((size, samples)), whole((size * 3 // 2, 2 * size))],
        ),
        out_shape=[
            jax.ShapeDtypeStruct((size, samples), jnp.float32),
            jax.ShapeDtypeStruct((size * 3 // 2, 2 * size), jnp.float32),
        ],
        name="gram_stage",
    )(half, hyper, *parts, probes_t, prev_t, coupling)


def finish_kernel(inv_root, half_ref, packed_ref, image_ref, probe_ref, a_ref, r_ref, next_ref):
    size = image_ref.shape[0]
    block_a = packed_ref[:size, :size]
    image_sq = packed_ref[:size, size:]
    square = jnp.concatenate([packed_ref[size:, :size], packed_ref[size:, size:]], axis=0)
    twice = 2.0 * block_a - dot(square, block_a, NN, HIGHEST)
    gram = image_sq - dot(block_a, twice, TN, HIGHEST)
    basis = probe_ref[...].astype(jnp.float32) * inv_root
    resid = image_ref[...] - dot(block_a, basis, TN, HIGHEST)

    row_id = lax.broadcasted_iota(jnp.int32, (size, 2 * size), 0)
    lane_id = lax.broadcasted_iota(jnp.int32, (size, 2 * size), 1)
    unit = jnp.where(lane_id == row_id + size, 1.0, 0.0)
    work = jnp.concatenate([gram, jnp.zeros_like(gram)], axis=1) + unit
    tiles = [work[8 * i : 8 * i + 8, :] for i in range(size // 8)]
    sub_id = lax.broadcasted_iota(jnp.int32, (8, 2 * size), 0)
    for j in range(size):
        home, place = divmod(j, 8)
        row = jnp.broadcast_to(tiles[home][place : place + 1, :], (8, 2 * size))
        scale = lax.rsqrt(jnp.broadcast_to(row[:, j : j + 1], (8, 2 * size)))
        row = row * scale
        for i in range(home, size // 8):
            column = jnp.broadcast_to(tiles[i][:, j : j + 1], (8, 2 * size)) * scale
            if i == home:
                column = jnp.where(sub_id > place, column, 0.0)
            tiles[i] = tiles[i] - column * row
            if i == home:
                tiles[i] = jnp.where(sub_id == place, row, tiles[i])
    work = jnp.concatenate(tiles, axis=0)
    upper_rows = lax.broadcasted_iota(jnp.int32, (size, size), 0)
    upper_cols = lax.broadcasted_iota(jnp.int32, (size, size), 1)
    a_ref[...] = block_a
    r_ref[...] = jnp.where(upper_cols >= upper_rows, work[:, :size], 0.0)
    next_ref[...] = dot(work[:, size:], resid, NN, HIGHEST) * (1.0 / inv_root)


def finish(inv_root, packed, image, probes_t, half):
    size, samples = image.shape
    whole = lambda shape: pl.BlockSpec(shape, lambda i, h: (0,) * len(shape))
    return pl.pallas_call(
        functools.partial(finish_kernel, inv_root),
        grid_spec=pltpu.PrefetchScalarGridSpec(
            num_scalar_prefetch=1,
            grid=(1,),
            in_specs=[
                whole(packed.shape),
                whole(image.shape),
                pl.BlockSpec((size, samples), lambda i, h: (0, h[0])),
            ],
            out_specs=[whole((size, size)), whole((size, size)), whole((size, samples))],
        ),
        out_shape=[
            jax.ShapeDtypeStruct((size, size), jnp.float32),
            jax.ShapeDtypeStruct((size, size), jnp.float32),
            jax.ShapeDtypeStruct((size, samples), jnp.float32),
        ],
        name="finish",
    )(half, packed, image, probes_t)


def ring_sum(value, shift):
    one, two, three = (send(value, shift(s)) for s in (1, 2, 3))
    return (value + two) + (one + three)


def per_device(
    tokens, lengths, embed, conv_w, conv_b, inv_len, hyper, probes, prev_probes, coupling
):
    total_rows = tokens.shape[0] * lax.axis_size("blk")
    inv_root = 1.0 / math.sqrt(total_rows)
    half = lax.axis_index("rep").astype(jnp.int32).reshape(1)
    probes_t = probes.T
    cols, rows = conv_features(
        tokens.T, lengths, embed, conv_w, conv_b, inv_len, probes_t, half
    )
    near = [send(cols, shift_by_core(s, 0)) for s in (1, 2, 3)]
    own_rows = [rows] + [send(rows, shift_y(s)) for s in (1, 2, 3)]
    group = jnp.stack([cols] + near)
    far = [send(group, shift_by_core(s, 1)) for s in (1, 3, 2)]
    other_rows = [send(r, core_swap()) for r in own_rows]
    all_rows = own_rows + other_rows
    partial = apply_rows(hyper, all_rows, [group])
    for block in far:
        partial = apply_rows(hyper, all_rows, [block], partial)
    own, other = partial
    joint = own + send(other, core_swap())
    parts = [joint[0]] + [send(joint[s], shift_y(-s)) for s in (1, 2, 3)]
    image, packed = gram_stage(inv_root, hyper, parts, probes_t, prev_probes.T, coupling, half)
    packed = packed + send(packed, core_swap())
    for shift in (shift_z, shift_x, shift_y):
        packed = ring_sum(packed, shift)
    block_a, upper, next_t = finish(inv_root, packed, image, probes_t, half)
    return (block_a, upper, next_t.T)


def solution(mesh):
    return jax.shard_map(
        per_device,
        mesh=mesh,
        in_specs=(
            P("blk", None),
            P("blk"),
            P(),
            P(),
            P(),
            P(),
            P(),
            P("blk", None),
            P(("blk", "rep"), None),
            P(),
        ),
        out_specs=(P(), P(), P(("blk", "rep"), None)),
        check_vma=False,
    )
```

time: 702 us -> 142 us (0.20)
  matrix products: 228 us -> 0 us
  blocking collectives: 128 us -> 0 us
  local copies, waits for them, and re-layouts: 106 us -> 4.9 us
  waiting for transfers between devices: 114 us -> 39.4 us
  Pallas kernels: 0 us -> 65.7 us
  other arithmetic: 56.5 us -> 3.49 us
  loops' own time: 49.2 us -> 0 us
  starting transfers between devices: 0.08 us -> 27.3 us
  between operations: 14.2 us -> 0.75 us
    dot_general x115 -> x0, matrix products: 228 us -> none  [the longest x14 97.4 us: one_block(): jnp.dot(embedded, tap_weights[tap_index], preferred_element_type=jnp.floa...]
    psum x2 -> x0, blocking collectives: 128 us -> none  [the longest x1 64.6 us: per_device(): block_a = lax.psum(gram_of(basis_half, image), ('blk', 'rep'))]
    all_gather x2 -> x0, waiting for transfers between devices: 114 us -> none  [the longest x1 114 us: per_device(): lax.all_gather(feat, 'blk', axis=0, tiled=True)]
    dynamic_slice x128 -> x0, local copies, waits for them, and re-layouts: 75.7 us -> none  [the longest x64 38.1 us: row_step(): diag_value = lax.dynamic_slice(upper, (row, row), (1, 1))[0, 0]]
    pallas_call x0 -> x7, Pallas kernels: none -> 65.7 us  [the longest x4 41.3 us: apply_rows(): pl.pallas_call(functools.partial(apply_kernel, len(rows), len(cols), 1 if...]
    another operation x4 -> x0, loops' own time: 49.2 us -> none  [the longest x1 47.4 us: upper_factor(): lax.fori_loop(0, order, column_step, (gram, jnp.zeros_like(gram)))]
    reduce_sum x37 -> x0, other arithmetic: 42 us -> none  [the longest x33 41.2 us: squares_of(): return jnp.sum(wide * wide, axis=1)]
    ppermute x0 -> x27, waiting for transfers between devices: none -> 39.4 us  [send(): return lax.ppermute(value, AXES, perm)]
  transfers between devices with their start and end apart: 2 -> 27, of which waited for: 1 -> 19; matrix products, arithmetic and copies ran while one was open for 19% -> 0% of each run, Pallas kernels for 0% -> 22%
where the time goes in v1:
time: 142 us; the launch traced here: 141 us
  Pallas kernels  65.7 us (46%)
  waiting for transfers between devices  39.4 us (28%)
  starting transfers between devices  27.3 us (19%)
  local copies, waits for them, and re-layouts  4.9 us (3%)
  other arithmetic  3.49 us (2%)
    pallas_call x4, Pallas kernels, apply_rows(): pl.pallas_call(functools.partial(apply_kernel, len(rows), len(cols), 1 if...  41.3 us
    ppermute x27, waiting for transfers between devices, send(): return lax.ppermute(value, AXES, perm)  39.4 us
    ppermute x27, starting transfers between devices, send(): return lax.ppermute(value, AXES, perm)  27.3 us
    pallas_call x1, Pallas kernels, conv_features(): pl.pallas_call(functools.partial(conv_kernel, taps), grid_spec=pltpu.Pref...  11.5 us
    pallas_call x1, Pallas kernels, finish(): pl.pallas_call(functools.partial(finish_kernel, inv_root), grid_spec=pltp...  10.7 us
    unnamed x30, local copies, waits for them, and re-layouts  4.25 us
  transfers between devices with their start and end apart: 27, of which 19 were waited for; matrix products, arithmetic and copies ran while one was open for 0% of the time, Pallas kernels for 22%

profile of v1, /device:TPU:2, one launch (start us, length us, event | category | flops | bytes accessed | tf_op | source)
XLA Modules:
  0.0 141.5 jit_solution(12262427574412950706)
XLA Ops:
  0.6 11.5 %conv_features.1 = (bf16[320,256]{1,0:T(8,128)(2,1)}, bf16[256,256]{1,0:T(8,128)(2,1)}) custom-call(s32[1]{0:T(128)} %bitcast.half_ref, s32[69,512]{1,0:T(8,128)} %bitcast.27, s32[1,512]{1,0:T(1,128)} %bitcast.29, bf16[64,256]{1,0:T(8,128)(2,1)} %embed_ref.1, bf16[7,32,256]{2,1,0:T(8,128)(2,1)} %w_ref.1, f32[1,256]{1,0:T(1,128)} %bitcast.30, ...), custom_call_target="tpu_custom_call" | custom-call | tf_op jit(solution)/shard_map/conv_features/pallas_call | solution.py:146
  12.1 4.0 %collective-permute-start.9 = (bf16[320,256]{1,0:T(8,128)(2,1)}, bf16[320,256]{1,0:T(8,128)(2,1)S(1)}, u32[]{:S(2)}, u32[]{:S(2)}) collective-permute-start(bf16[320,256]{1,0:T(8,128)(2,1)} %get-tuple-element.19), channel_id=1, source_target_pairs={{0,96},{1,97},{2,26},{3,27},{4,100},{5,101},{6,30},{7,31},{8,104},... | collective-permute-start | bytes 491528 | tf_op jit(solution)/shard_map/ppermute | solution.py:56
  16.2 1.3 collective-permute-start.7
  17.4 3.7 %collective-permute-done.9 = bf16[320,256]{1,0:T(8,128)(2,1)S(1)} collective-permute-done((bf16[320,256]{1,0:T(8,128)(2,1)}, bf16[320,256]{1,0:T(8,128)(2,1)S(1)}, u32[]{:S(2)}, u32[]{:S(2)}) %collective-permute-start.9) | collective-permute-done | bytes 163872 | tf_op jit(solution)/shard_map/ppermute | solution.py:56
  21.1 2.2 %collective-permute-done.8 = bf16[320,256]{1,0:T(8,128)(2,1)S(1)} collective-permute-done((bf16[320,256]{1,0:T(8,128)(2,1)}, bf16[320,256]{1,0:T(8,128)(2,1)S(1)}, u32[]{:S(2)}, u32[]{:S(2)}) %collective-permute-start.8) | collective-permute-done | bytes 163872 | tf_op jit(solution)/shard_map/ppermute | solution.py:56
  23.3 1.4 collective-permute-done.7
  24.7 1.0 pad_maximum_fusion.refs_8_
  25.7 1.6 %collective-permute-start.12 = (bf16[4,320,256]{2,1,0:T(8,128)(2,1)S(1)}, bf16[4,320,256]{2,1,0:T(8,128)(2,1)S(1)}, u32[]{:S(2)}, u32[]{:S(2)}) collective-permute-start(bf16[4,320,256]{2,1,0:T(8,128)(2,1)S(1)} %pad_maximum_fusion.refs_8_), channel_id=1, source_target_pairs={{0,8},{1,9},{2,34},{3,35},{4,12},{5,13},{6,38},{7,39},{8,16},{9,17... | collective-permute-start | bytes 1966088 | tf_op jit(solution)/shard_map/ppermute | solution.py:56
  27.8 3.0 %collective-permute-start.2 = (bf16[256,256]{1,0:T(8,128)(2,1)S(1)}, bf16[256,256]{1,0:T(8,128)(2,1)S(1)}, u32[]{:S(2)}, u32[]{:S(2)}) collective-permute-start(bf16[256,256]{1,0:T(8,128)(2,1)S(1)} %copy-done.7), channel_id=1, source_target_pairs={{0,5},{1,4},{2,7},{3,6},{4,0},{5,1},{6,2},{7,3},{8,13},{9,12},{10,... | collective-permute-start | bytes 393224 | tf_op jit(solution)/shard_map/ppermute | solution.py:56
  31.5 2.1 %collective-permute-start.10 = (bf16[4,320,256]{2,1,0:T(8,128)(2,1)S(1)}, bf16[4,320,256]{2,1,0:T(8,128)(2,1)S(1)}, u32[]{:S(2)}, u32[]{:S(2)}) collective-permute-start(bf16[4,320,256]{2,1,0:T(8,128)(2,1)S(1)} %pad_maximum_fusion.refs_8_), channel_id=1, source_target_pairs={{0,16},{1,17},{2,66},{3,67},{4,20},{5,21},{6,70},{7,71},{8,24},{9,... | collective-permute-start | bytes 1966088 | tf_op jit(solution)/shard_map/ppermute | solution.py:56
  33.6 3.6 %collective-permute-done.2.refs_3_ = bf16[256,256]{1,0:T(8,128)(2,1)S(1)} collective-permute-done((bf16[256,256]{1,0:T(8,128)(2,1)S(1)}, bf16[256,256]{1,0:T(8,128)(2,1)S(1)}, u32[]{:S(2)}, u32[]{:S(2)}) %collective-permute-start.2) | collective-permute-done | bytes 131104 | tf_op jit(solution)/shard_map/ppermute | solution.py:56
  38.0 6.2 %collective-permute-done.refs_1_ = bf16[256,256]{1,0:T(8,128)(2,1)S(1)} collective-permute-done((bf16[256,256]{1,0:T(8,128)(2,1)S(1)}, bf16[256,256]{1,0:T(8,128)(2,1)S(1)}, u32[]{:S(2)}, u32[]{:S(2)}) %collective-permute-start) | collective-permute-done | bytes 131104 | tf_op jit(solution)/shard_map/ppermute | solution.py:56
  46.9 10.2 %apply_rows.4 = (f32[4,64,256]{2,1,0:T(8,128)}, f32[4,64,256]{2,1,0:T(8,128)}) custom-call(f32[2]{0:T(128)} %hyper_ref.9, bf16[256,256]{1,0:T(8,128)(2,1)} %get-tuple-element.18.refs_0_, bf16[256,256]{1,0:T(8,128)(2,1)} %copy-done.11, bf16[256,256]{1,0:T(8,128)(2,1)} %copy-done.10, bf16[256,256]{1,0:T(8,128)(2,1)} %copy-done.9, bf16[256,256]{1,0:T(8,128)(2,1)} %copy-done.8, ...), custom_call_target="tpu_custom_call" | custom-call | flops 1342177280 | bytes 4194304 | tf_op jit(solution)/shard_map/apply_rows/pallas_call | solution.py:228
  57.9 10.4 %apply_rows.5 = (f32[4,64,256]{2,1,0:T(8,128)}, f32[4,64,256]{2,1,0:T(8,128)}) custom-call(f32[2]{0:T(128)} %hyper_ref.9, bf16[256,256]{1,0:T(8,128)(2,1)} %get-tuple-element.18.refs_0_, bf16[256,256]{1,0:T(8,128)(2,1)} %copy-done.11, bf16[256,256]{1,0:T(8,128)(2,1)} %copy-done.10, bf16[256,256]{1,0:T(8,128)(2,1)} %copy-done.9, bf16[256,256]{1,0:T(8,128)(2,1)} %copy-done.8, ...), custom_call_target="tpu_custom_call" | custom-call | flops 1342177280 | bytes 4194304 | tf_op jit(solution)/shard_map/apply_rows/pallas_call | solution.py:228
  69.2 10.4 %apply_rows.6 = (f32[4,64,256]{2,1,0:T(8,128)}, f32[4,64,256]{2,1,0:T(8,128)}) custom-call(f32[2]{0:T(128)} %hyper_ref.9, bf16[256,256]{1,0:T(8,128)(2,1)} %get-tuple-element.18.refs_0_, bf16[256,256]{1,0:T(8,128)(2,1)} %copy-done.11, bf16[256,256]{1,0:T(8,128)(2,1)} %copy-done.10, bf16[256,256]{1,0:T(8,128)(2,1)} %copy-done.9, bf16[256,256]{1,0:T(8,128)(2,1)} %copy-done.8, ...), custom_call_target="tpu_custom_call" | custom-call | flops 1342177280 | bytes 4194304 | tf_op jit(solution)/shard_map/apply_rows/pallas_call | solution.py:228
  80.4 10.4 %apply_rows.7 = (f32[4,64,256]{2,1,0:T(8,128)}, f32[4,64,256]{2,1,0:T(8,128)}) custom-call(f32[2]{0:T(128)} %hyper_ref.9, bf16[256,256]{1,0:T(8,128)(2,1)} %get-tuple-element.18.refs_0_, bf16[256,256]{1,0:T(8,128)(2,1)} %copy-done.11, bf16[256,256]{1,0:T(8,128)(2,1)} %copy-done.10, bf16[256,256]{1,0:T(8,128)(2,1)} %copy-done.9, bf16[256,256]{1,0:T(8,128)(2,1)} %copy-done.8, ...), custom_call_target="tpu_custom_call" | custom-call | flops 1342177280 | bytes 4194304 | tf_op jit(solution)/shard_map/apply_rows/pallas_call | solution.py:228
  90.9 1.6 %collective-permute-done.13 = f32[4,64,256]{2,1,0:T(8,128)S(1)} collective-permute-done((f32[4,64,256]{2,1,0:T(8,128)}, f32[4,64,256]{2,1,0:T(8,128)S(1)}, u32[]{:S(2)}, u32[]{:S(2)}) %collective-permute-start.13) | collective-permute-done | bytes 262176 | tf_op jit(solution)/shard_map/ppermute | solution.py:56
  94.1 3.2 %collective-permute-start.15 = (f32[64,256]{1,0:T(8,128)S(1)}, f32[64,256]{1,0:T(8,128)S(1)}, u32[]{:S(2)}, u32[]{:S(2)}) collective-permute-start(f32[64,256]{1,0:T(8,128)S(1)} %get-tuple-element.34), channel_id=1, source_target_pairs={{0,1},{1,0},{2,3},{3,2},{4,5},{5,4},{6,7},{7,6},{8,9},{9,8},{10,11... | collective-permute-start | bytes 196616 | tf_op jit(solution)/shard_map/ppermute | solution.py:56
  97.5 3.4 %collective-permute-done.16.three = f32[64,256]{1,0:T(8,128)S(1)} collective-permute-done((f32[64,256]{1,0:T(8,128)S(1)}, f32[64,256]{1,0:T(8,128)S(1)}, u32[]{:S(2)}, u32[]{:S(2)}) %collective-permute-start.16) | collective-permute-done | bytes 65568 | tf_op jit(solution)/shard_map/ppermute | solution.py:56
  102.2 2.2 %gram_stage.1 = (f32[64,256]{1,0:T(8,128)}, f32[96,128]{1,0:T(8,128)}) custom-call(s32[1]{0:T(128)} %bitcast.half_ref, f32[2]{0:T(128)} %hyper_ref.9, f32[64,256]{1,0:T(8,128)} %get-tuple-element.36.own, f32[64,256]{1,0:T(8,128)} %copy-done.3, f32[64,256]{1,0:T(8,128)} %copy-done.2, f32[64,256]{1,0:T(8,128)} %copy-done.1, bf16[64,512]{1,0:T(8,128)(2,1)} %bitcast.21, ...), custom_call_target="tpu_custom_call" | custom-call | tf_op jit(solution)/shard_map/gram_stage/pallas_call | solution.py:271
  104.5 1.4 %collective-permute-done.17 = f32[96,128]{1,0:T(8,128)S(1)} collective-permute-done((f32[96,128]{1,0:T(8,128)}, f32[96,128]{1,0:T(8,128)S(1)}, u32[]{:S(2)}, u32[]{:S(2)}) %collective-permute-start.17) | collective-permute-done | bytes 49184 | tf_op jit(solution)/shard_map/ppermute | solution.py:56
  106.8 1.9 %collective-permute-start.19 = (f32[96,128]{1,0:T(8,128)S(1)}, f32[96,128]{1,0:T(8,128)S(1)}, u32[]{:S(2)}, u32[]{:S(2)}) collective-permute-start(f32[96,128]{1,0:T(8,128)S(1)} %add.34), channel_id=1, source_target_pairs={{0,32},{1,33},{2,34},{3,35},{4,36},{5,37},{6,38},{7,39},{8,40},{9,... | collective-permute-start | bytes 147464 | tf_op jit(solution)/shard_map/ppermute | solution.py:56
  108.7 2.1 %collective-permute-done.20 = f32[96,128]{1,0:T(8,128)S(1)} collective-permute-done((f32[96,128]{1,0:T(8,128)S(1)}, f32[96,128]{1,0:T(8,128)S(1)}, u32[]{:S(2)}, u32[]{:S(2)}) %collective-permute-start.20) | collective-permute-done | bytes 49184 | tf_op jit(solution)/shard_map/ppermute | solution.py:56
  110.8 1.3 collective-permute-done.19
  112.1 2.2 %collective-permute-done.18 = f32[96,128]{1,0:T(8,128)S(1)} collective-permute-done((f32[96,128]{1,0:T(8,128)S(1)}, f32[96,128]{1,0:T(8,128)S(1)}, u32[]{:S(2)}, u32[]{:S(2)}) %collective-permute-start.18) | collective-permute-done | bytes 49184 | tf_op jit(solution)/shard_map/ppermute | solution.py:56
  114.8 1.7 %collective-permute-start.22 = (f32[96,128]{1,0:T(8,128)S(1)}, f32[96,128]{1,0:T(8,128)S(1)}, u32[]{:S(2)}, u32[]{:S(2)}) collective-permute-start(f32[96,128]{1,0:T(8,128)S(1)} %add_add_fusion.2), channel_id=1, source_target_pairs={{0,8},{1,9},{2,10},{3,11},{4,12},{5,13},{6,14},{7,15},{8,16},{9,17... | collective-permute-start | bytes 147464 | tf_op jit(solution)/shard_map/ppermute | solution.py:56
  116.4 2.1 %collective-permute-start.21 = (f32[96,128]{1,0:T(8,128)S(1)}, f32[96,128]{1,0:T(8,128)S(1)}, u32[]{:S(2)}, u32[]{:S(2)}) collective-permute-start(f32[96,128]{1,0:T(8,128)S(1)} %add_add_fusion.2), channel_id=1, source_target_pairs={{0,16},{1,17},{2,18},{3,19},{4,20},{5,21},{6,22},{7,23},{8,24},{9,... | collective-permute-start | bytes 147464 | tf_op jit(solution)/shard_map/ppermute | solution.py:56
  119.0 3.0 %collective-permute-done.21 = f32[96,128]{1,0:T(8,128)S(1)} collective-permute-done((f32[96,128]{1,0:T(8,128)S(1)}, f32[96,128]{1,0:T(8,128)S(1)}, u32[]{:S(2)}, u32[]{:S(2)}) %collective-permute-start.21) | collective-permute-done | bytes 49184 | tf_op jit(solution)/shard_map/ppermute | solution.py:56
  122.0 2.3 %collective-permute-start.26 = (f32[96,128]{1,0:T(8,128)S(1)}, f32[96,128]{1,0:T(8,128)S(1)}, u32[]{:S(2)}, u32[]{:S(2)}) collective-permute-start(f32[96,128]{1,0:T(8,128)S(1)} %add_add_fusion.1), channel_id=1, source_target_pairs={{0,5},{1,4},{2,7},{3,6},{4,0},{5,1},{6,2},{7,3},{8,13},{9,12},{10,... | collective-permute-start | bytes 147464 | tf_op jit(solution)/shard_map/ppermute | solution.py:56
  124.3 1.5 %collective-permute-start.24 = (f32[96,128]{1,0:T(8,128)S(1)}, f32[96,128]{1,0:T(8,128)S(1)}, u32[]{:S(2)}, u32[]{:S(2)}) collective-permute-start(f32[96,128]{1,0:T(8,128)S(1)} %add_add_fusion.1), channel_id=1, source_target_pairs={{0,1},{1,0},{2,3},{3,2},{4,5},{5,4},{6,7},{7,6},{8,9},{9,8},{10,11... | collective-permute-start | bytes 147464 | tf_op jit(solution)/shard_map/ppermute | solution.py:56
  126.7 3.5 %collective-permute-done.25 = f32[96,128]{1,0:T(8,128)S(1)} collective-permute-done((f32[96,128]{1,0:T(8,128)S(1)}, f32[96,128]{1,0:T(8,128)S(1)}, u32[]{:S(2)}, u32[]{:S(2)}) %collective-permute-start.25) | collective-permute-done | bytes 49184 | tf_op jit(solution)/shard_map/ppermute | solution.py:56
  130.8 10.7 %finish.1 = (f32[64,64]{1,0:T(8,128)}, f32[64,64]{1,0:T(8,128)}, f32[64,256]{1,0:T(8,128)}) custom-call(s32[1]{0:T(128)} %bitcast.half_ref, f32[96,128]{1,0:T(8,128)} %add_add_fusion.packed_ref, f32[64,256]{1,0:T(8,128)} %get-tuple-element.29.image_ref, bf16[64,512]{1,0:T(8,128)(2,1)} %bitcast.22), custom_call_target="tpu_custom_call" | custom-call | tf_op jit(solution)/shard_map/finish/pallas_call | solution.py:332
  (66 shorter events, 13.8 us)
Async XLA Ops:
  12.1 9.0 %collective-permute-start.9 = (bf16[320,256]{1,0:T(8,128)(2,1)}, bf16[320,256]{1,0:T(8,128)(2,1)S(1)}, u32[]{:S(2)}, u32[]{:S(2)}) collective-permute-start(bf16[320,256]{1,0:T(8,128)(2,1)} %get-tuple-element.19), channel_id=1, source_target_pairs={{0,96},{1,97},{2,26},{3,27},{4,100},{5,101},{6,30},{7,31},{8,104},... | collective-permute-start | bytes 491528 | tf_op jit(solution)/shard_map/ppermute | solution.py:56
  16.2 7.1 %collective-permute-start.8 = (bf16[320,256]{1,0:T(8,128)(2,1)}, bf16[320,256]{1,0:T(8,128)(2,1)S(1)}, u32[]{:S(2)}, u32[]{:S(2)}) collective-permute-start(bf16[320,256]{1,0:T(8,128)(2,1)} %get-tuple-element.19), channel_id=1, source_target_pairs={{0,64},{1,65},{2,18},{3,19},{4,68},{5,69},{6,22},{7,23},{8,72},{9,... | collective-permute-start | bytes 491528 | tf_op jit(solution)/shard_map/ppermute | solution.py:56
  16.2 8.5 %collective-permute-start.7 = (bf16[320,256]{1,0:T(8,128)(2,1)}, bf16[320,256]{1,0:T(8,128)(2,1)S(1)}, u32[]{:S(2)}, u32[]{:S(2)}) collective-permute-start(bf16[320,256]{1,0:T(8,128)(2,1)} %get-tuple-element.19), channel_id=1, source_target_pairs={{0,32},{1,33},{2,10},{3,11},{4,36},{5,37},{6,14},{7,15},{8,40},{9,... | collective-permute-start | bytes 491528 | tf_op jit(solution)/shard_map/ppermute | solution.py:56
  24.7 2.6 %copy-start.7 = (bf16[256,256]{1,0:T(8,128)(2,1)S(1)}, bf16[256,256]{1,0:T(8,128)(2,1)}, u32[]{:S(2)}) copy-start(bf16[256,256]{1,0:T(8,128)(2,1)} %get-tuple-element.18.refs_0_) | copy-start | bytes 393220
  25.7 20.1 %copy-start = (bf16[4,320,256]{2,1,0:T(8,128)(2,1)}, bf16[4,320,256]{2,1,0:T(8,128)(2,1)S(1)}, u32[]{:S(2)}) copy-start(bf16[4,320,256]{2,1,0:T(8,128)(2,1)S(1)} %pad_maximum_fusion.refs_8_) | copy-start | bytes 1966084
  25.7 31.4 %collective-permute-start.12 = (bf16[4,320,256]{2,1,0:T(8,128)(2,1)S(1)}, bf16[4,320,256]{2,1,0:T(8,128)(2,1)S(1)}, u32[]{:S(2)}, u32[]{:S(2)}) collective-permute-start(bf16[4,320,256]{2,1,0:T(8,128)(2,1)S(1)} %pad_maximum_fusion.refs_8_), channel_id=1, source_target_pairs={{0,8},{1,9},{2,34},{3,35},{4,12},{5,13},{6,38},{7,39},{8,16},{9,17... | collective-permute-start | bytes 1966088 | tf_op jit(solution)/shard_map/ppermute | solution.py:56
  27.3 4.2 %collective-permute-start.3 = (bf16[256,256]{1,0:T(8,128)(2,1)S(1)}, bf16[256,256]{1,0:T(8,128)(2,1)S(1)}, u32[]{:S(2)}, u32[]{:S(2)}) collective-permute-start(bf16[256,256]{1,0:T(8,128)(2,1)S(1)} %copy-done.7), channel_id=1, source_target_pairs={{0,2},{1,3},{2,0},{3,1},{4,6},{5,7},{6,4},{7,5},{8,10},{9,11},{10,... | collective-permute-start | bytes 393224 | tf_op jit(solution)/shard_map/ppermute | solution.py:56
  27.3 41.0 %collective-permute-start.11 = (bf16[4,320,256]{2,1,0:T(8,128)(2,1)S(1)}, bf16[4,320,256]{2,1,0:T(8,128)(2,1)S(1)}, u32[]{:S(2)}, u32[]{:S(2)}) collective-permute-start(bf16[4,320,256]{2,1,0:T(8,128)(2,1)S(1)} %pad_maximum_fusion.refs_8_), channel_id=1, source_target_pairs={{0,24},{1,25},{2,98},{3,99},{4,28},{5,29},{6,102},{7,103},{8,0},{9... | collective-permute-start | bytes 1966088 | tf_op jit(solution)/shard_map/ppermute | solution.py:56
  27.8 9.3 %collective-permute-start.2 = (bf16[256,256]{1,0:T(8,128)(2,1)S(1)}, bf16[256,256]{1,0:T(8,128)(2,1)S(1)}, u32[]{:S(2)}, u32[]{:S(2)}) collective-permute-start(bf16[256,256]{1,0:T(8,128)(2,1)S(1)} %copy-done.7), channel_id=1, source_target_pairs={{0,5},{1,4},{2,7},{3,6},{4,0},{5,1},{6,2},{7,3},{8,13},{9,12},{10,... | collective-permute-start | bytes 393224 | tf_op jit(solution)/shard_map/ppermute | solution.py:56
  30.8 7.2 %collective-permute-start.1 = (bf16[256,256]{1,0:T(8,128)(2,1)S(1)}, bf16[256,256]{1,0:T(8,128)(2,1)S(1)}, u32[]{:S(2)}, u32[]{:S(2)}) collective-permute-start(bf16[256,256]{1,0:T(8,128)(2,1)S(1)} %copy-done.7), channel_id=1, source_target_pairs={{0,1},{1,0},{2,3},{3,2},{4,5},{5,4},{6,7},{7,6},{8,9},{9,8},{10,11... | collective-permute-start | bytes 393224 | tf_op jit(solution)/shard_map/ppermute | solution.py:56
  31.5 14.3 %copy-start.8 = (bf16[256,256]{1,0:T(8,128)(2,1)}, bf16[256,256]{1,0:T(8,128)(2,1)S(1)}, u32[]{:S(2)}) copy-start(bf16[256,256]{1,0:T(8,128)(2,1)S(1)} %collective-permute-done.3.refs_4_) | copy-start | bytes 393220
  31.5 48.0 %collective-permute-start.10 = (bf16[4,320,256]{2,1,0:T(8,128)(2,1)S(1)}, bf16[4,320,256]{2,1,0:T(8,128)(2,1)S(1)}, u32[]{:S(2)}, u32[]{:S(2)}) collective-permute-start(bf16[4,320,256]{2,1,0:T(8,128)(2,1)S(1)} %pad_maximum_fusion.refs_8_), channel_id=1, source_target_pairs={{0,16},{1,17},{2,66},{3,67},{4,20},{5,21},{6,70},{7,71},{8,24},{9,... | collective-permute-start | bytes 1966088 | tf_op jit(solution)/shard_map/ppermute | solution.py:56
  37.1 8.6 %copy-start.9 = (bf16[256,256]{1,0:T(8,128)(2,1)}, bf16[256,256]{1,0:T(8,128)(2,1)S(1)}, u32[]{:S(2)}) copy-start(bf16[256,256]{1,0:T(8,128)(2,1)S(1)} %collective-permute-done.2.refs_3_) | copy-start | bytes 393220
  37.1 7.1 %collective-permute-start = (bf16[256,256]{1,0:T(8,128)(2,1)S(1)}, bf16[256,256]{1,0:T(8,128)(2,1)S(1)}, u32[]{:S(2)}, u32[]{:S(2)}) collective-permute-start(bf16[256,256]{1,0:T(8,128)(2,1)S(1)} %copy-done.7), channel_id=1, source_target_pairs={{0,4},{1,5},{2,6},{3,7},{4,1},{5,0},{6,3},{7,2},{8,12},{9,13},{10,... | collective-permute-start | bytes 393224 | tf_op jit(solution)/shard_map/ppermute | solution.py:56
  38.0 7.7 %copy-start.10 = (bf16[256,256]{1,0:T(8,128)(2,1)}, bf16[256,256]{1,0:T(8,128)(2,1)S(1)}, u32[]{:S(2)}) copy-start(bf16[256,256]{1,0:T(8,128)(2,1)S(1)} %collective-permute-done.1.refs_2_) | copy-start | bytes 393220
  38.0 6.2 %collective-permute-start.6 = (bf16[256,256]{1,0:T(8,128)(2,1)S(1)}, bf16[256,256]{1,0:T(8,128)(2,1)S(1)}, u32[]{:S(2)}, u32[]{:S(2)}) collective-permute-start(bf16[256,256]{1,0:T(8,128)(2,1)S(1)} %collective-permute-done.2.refs_3_), channel_id=1, source_target_pairs={{0,2},{1,3},{2,0},{3,1},{4,6},{5,7},{6,4},{7,5},{8,10},{9,11},{10,... | collective-permute-start | bytes 393224 | tf_op jit(solution)/shard_map/ppermute | solution.py:56
  44.2 1.3 collective-permute-start.5
  44.2 1.5 %collective-permute-start.4 = (bf16[256,256]{1,0:T(8,128)(2,1)S(1)}, bf16[256,256]{1,0:T(8,128)(2,1)S(1)}, u32[]{:S(2)}, u32[]{:S(2)}) collective-permute-start(bf16[256,256]{1,0:T(8,128)(2,1)S(1)} %collective-permute-done.refs_1_), channel_id=1, source_target_pairs={{0,2},{1,3},{2,0},{3,1},{4,6},{5,7},{6,4},{7,5},{8,10},{9,11},{10,... | collective-permute-start | bytes 393224 | tf_op jit(solution)/shard_map/ppermute | solution.py:56
  90.7 1.7 %collective-permute-start.13 = (f32[4,64,256]{2,1,0:T(8,128)}, f32[4,64,256]{2,1,0:T(8,128)S(1)}, u32[]{:S(2)}, u32[]{:S(2)}) collective-permute-start(f32[4,64,256]{2,1,0:T(8,128)} %get-tuple-element.27), channel_id=1, source_target_pairs={{0,2},{1,3},{2,0},{3,1},{4,6},{5,7},{6,4},{7,5},{8,10},{9,11},{10,... | collective-permute-start | bytes 786440 | tf_op jit(solution)/shard_map/ppermute | solution.py:56
  94.1 6.8 %collective-permute-start.16 = (f32[64,256]{1,0:T(8,128)S(1)}, f32[64,256]{1,0:T(8,128)S(1)}, u32[]{:S(2)}, u32[]{:S(2)}) collective-permute-start(f32[64,256]{1,0:T(8,128)S(1)} %get-tuple-element.33), channel_id=1, source_target_pairs={{0,4},{1,5},{2,6},{3,7},{4,1},{5,0},{6,3},{7,2},{8,12},{9,13},{10,... | collective-permute-start | bytes 196616 | tf_op jit(solution)/shard_map/ppermute | solution.py:56
  94.1 6.8 %collective-permute-start.15 = (f32[64,256]{1,0:T(8,128)S(1)}, f32[64,256]{1,0:T(8,128)S(1)}, u32[]{:S(2)}, u32[]{:S(2)}) collective-permute-start(f32[64,256]{1,0:T(8,128)S(1)} %get-tuple-element.34), channel_id=1, source_target_pairs={{0,1},{1,0},{2,3},{3,2},{4,5},{5,4},{6,7},{7,6},{8,9},{9,8},{10,11... | collective-permute-start | bytes 196616 | tf_op jit(solution)/shard_map/ppermute | solution.py:56
  97.3 4.3 %collective-permute-start.14 = (f32[64,256]{1,0:T(8,128)S(1)}, f32[64,256]{1,0:T(8,128)S(1)}, u32[]{:S(2)}, u32[]{:S(2)}) collective-permute-start(f32[64,256]{1,0:T(8,128)S(1)} %get-tuple-element.35), channel_id=1, source_target_pairs={{0,5},{1,4},{2,7},{3,6},{4,0},{5,1},{6,2},{7,3},{8,13},{9,12},{10,... | collective-permute-start | bytes 196616 | tf_op jit(solution)/shard_map/ppermute | solution.py:56
  104.5 1.4 %collective-permute-start.17 = (f32[96,128]{1,0:T(8,128)}, f32[96,128]{1,0:T(8,128)S(1)}, u32[]{:S(2)}, u32[]{:S(2)}) collective-permute-start(f32[96,128]{1,0:T(8,128)} %get-tuple-element.28), channel_id=1, source_target_pairs={{0,2},{1,3},{2,0},{3,1},{4,6},{5,7},{6,4},{7,5},{8,10},{9,11},{10,... | collective-permute-start | bytes 147464 | tf_op jit(solution)/shard_map/ppermute | solution.py:56
  106.7 4.1 %collective-permute-start.20 = (f32[96,128]{1,0:T(8,128)S(1)}, f32[96,128]{1,0:T(8,128)S(1)}, u32[]{:S(2)}, u32[]{:S(2)}) collective-permute-start(f32[96,128]{1,0:T(8,128)S(1)} %add.34), channel_id=1, source_target_pairs={{0,96},{1,97},{2,98},{3,99},{4,100},{5,101},{6,102},{7,103},{8,104... | collective-permute-start | bytes 147464 | tf_op jit(solution)/shard_map/ppermute | solution.py:56
  106.8 5.3 %collective-permute-start.19 = (f32[96,128]{1,0:T(8,128)S(1)}, f32[96,128]{1,0:T(8,128)S(1)}, u32[]{:S(2)}, u32[]{:S(2)}) collective-permute-start(f32[96,128]{1,0:T(8,128)S(1)} %add.34), channel_id=1, source_target_pairs={{0,32},{1,33},{2,34},{3,35},{4,36},{5,37},{6,38},{7,39},{8,40},{9,... | collective-permute-start | bytes 147464 | tf_op jit(solution)/shard_map/ppermute | solution.py:56
  108.7 5.6 %collective-permute-start.18 = (f32[96,128]{1,0:T(8,128)S(1)}, f32[96,128]{1,0:T(8,128)S(1)}, u32[]{:S(2)}, u32[]{:S(2)}) collective-permute-start(f32[96,128]{1,0:T(8,128)S(1)} %add.34), channel_id=1, source_target_pairs={{0,64},{1,65},{2,66},{3,67},{4,68},{5,69},{6,70},{7,71},{8,72},{9,... | collective-permute-start | bytes 147464 | tf_op jit(solution)/shard_map/ppermute | solution.py:56
  114.3 4.2 %collective-permute-start.23 = (f32[96,128]{1,0:T(8,128)S(1)}, f32[96,128]{1,0:T(8,128)S(1)}, u32[]{:S(2)}, u32[]{:S(2)}) collective-permute-start(f32[96,128]{1,0:T(8,128)S(1)} %add_add_fusion.2), channel_id=1, source_target_pairs={{0,24},{1,25},{2,26},{3,27},{4,28},{5,29},{6,30},{7,31},{8,0},{9,1... | collective-permute-start | bytes 147464 | tf_op jit(solution)/shard_map/ppermute | solution.py:56
  114.8 4.3 %collective-permute-start.22 = (f32[96,128]{1,0:T(8,128)S(1)}, f32[96,128]{1,0:T(8,128)S(1)}, u32[]{:S(2)}, u32[]{:S(2)}) collective-permute-start(f32[96,128]{1,0:T(8,128)S(1)} %add_add_fusion.2), channel_id=1, source_target_pairs={{0,8},{1,9},{2,10},{3,11},{4,12},{5,13},{6,14},{7,15},{8,16},{9,17... | collective-permute-start | bytes 147464 | tf_op jit(solution)/shard_map/ppermute | solution.py:56
  116.4 5.6 %collective-permute-start.21 = (f32[96,128]{1,0:T(8,128)S(1)}, f32[96,128]{1,0:T(8,128)S(1)}, u32[]{:S(2)}, u32[]{:S(2)}) collective-permute-start(f32[96,128]{1,0:T(8,128)S(1)} %add_add_fusion.2), channel_id=1, source_target_pairs={{0,16},{1,17},{2,18},{3,19},{4,20},{5,21},{6,22},{7,23},{8,24},{9,... | collective-permute-start | bytes 147464 | tf_op jit(solution)/shard_map/ppermute | solution.py:56
  122.0 4.7 %collective-permute-start.26 = (f32[96,128]{1,0:T(8,128)S(1)}, f32[96,128]{1,0:T(8,128)S(1)}, u32[]{:S(2)}, u32[]{:S(2)}) collective-permute-start(f32[96,128]{1,0:T(8,128)S(1)} %add_add_fusion.1), channel_id=1, source_target_pairs={{0,5},{1,4},{2,7},{3,6},{4,0},{5,1},{6,2},{7,3},{8,13},{9,12},{10,... | collective-permute-start | bytes 147464 | tf_op jit(solution)/shard_map/ppermute | solution.py:56
  124.3 5.8 %collective-permute-start.25 = (f32[96,128]{1,0:T(8,128)S(1)}, f32[96,128]{1,0:T(8,128)S(1)}, u32[]{:S(2)}, u32[]{:S(2)}) collective-permute-start(f32[96,128]{1,0:T(8,128)S(1)} %add_add_fusion.1), channel_id=1, source_target_pairs={{0,4},{1,5},{2,6},{3,7},{4,1},{5,0},{6,3},{7,2},{8,12},{9,13},{10,... | collective-permute-start | bytes 147464 | tf_op jit(solution)/shard_map/ppermute | solution.py:56
  124.3 5.8 %collective-permute-start.24 = (f32[96,128]{1,0:T(8,128)S(1)}, f32[96,128]{1,0:T(8,128)S(1)}, u32[]{:S(2)}, u32[]{:S(2)}) collective-permute-start(f32[96,128]{1,0:T(8,128)S(1)} %add_add_fusion.1), channel_id=1, source_target_pairs={{0,1},{1,0},{2,3},{3,2},{4,5},{5,4},{6,7},{7,6},{8,9},{9,8},{10,11... | collective-permute-start | bytes 147464 | tf_op jit(solution)/shard_map/ppermute | solution.py:56
  (10 other events, 9.1 us)

commit v2 on v1

--- a/solution.py
+++ b/solution.py
@@ -7,6 +7,7 @@
 from jax.experimental import pallas as pl
 from jax.experimental.pallas import tpu as pltpu
 from jax.sharding import PartitionSpec as P
+
 
 LOG2E = math.log2(math.e)
 HIGHEST = lax.Precision.HIGHEST
@@ -177,63 +178,49 @@
 
 
 def apply_kernel(row_count, col_count, resume, hyper_ref, *refs):
-    row_refs = refs[:row_count]
-    col_refs = refs[row_count : row_count + col_count]
+    rows = refs[:row_count]
+    cols = refs[row_count : row_count + col_count]
     rest = refs[row_count + col_count :]
-    start_refs, out_refs, (half_ref,) = rest[: 2 * resume], rest[2 * resume : -1], rest[-1:]
-    channels, samples = row_refs[0].shape
-    half_rows = row_count // 2
+    start_refs, (out_ref, half_ref) = rest[:resume], rest[resume:]
+    _, samples = rows[0].shape
+    depth = cols[0].shape[0]
     top = jnp.log2(jnp.full((1, 128), hyper_ref[0], jnp.float32))[:, :1]
-    for i, row_ref in enumerate(row_refs):
-        wide = row_ref[...].astype(jnp.float32)
+    if resume:
+        out_ref[...] = start_refs[0][...]
+    else:
+        out_ref[...] = jnp.zeros_like(out_ref)
+    for i in range(row_count):
+        wide = rows[i][...].astype(jnp.float32)
         half_ref[i : i + 1, :] = (0.5 * LOG2E) * jnp.sum(wide * wide, axis=0, keepdims=True)
-    for side in range(2):
-        if resume:
-            out_refs[side][...] = start_refs[side][...]
-        else:
-            out_refs[side][...] = jnp.zeros_like(out_refs[side])
-
-    def block(col):
-        feat = col[:samples, :]
-        probes = col[samples:, :]
+    for g in range(col_count):
+        feat = jnp.concatenate([cols[g][d, :samples, :] for d in range(depth)], axis=0)
+        probes = jnp.concatenate([cols[g][d, samples:, :] for d in range(depth)], axis=1)
         wide = feat.astype(jnp.float32)
         bias = (0.5 * LOG2E) * jnp.sum(wide * wide, axis=1, keepdims=True) - top
-        bias = jnp.broadcast_to(bias, (samples, samples))
-        for i, row_ref in enumerate(row_refs):
-            inner = dot(feat, row_ref[...], NN)
+        bias = jnp.broadcast_to(bias, (depth * samples, samples))
+        for i in range(row_count):
+            inner = dot(feat, rows[i][...], NN)
             power = jnp.minimum(inner * LOG2E - bias - half_ref[i : i + 1, :], top)
             weights = jnp.exp2(power).astype(jnp.bfloat16)
-            out_refs[i // half_rows][i % half_rows] += dot(probes, weights, NN)
-
-    for col_ref in col_refs:
-        if len(col_ref.shape) == 2:
-            block(col_ref[...])
-        else:
-
-            def step(j, carry, col_ref=col_ref):
-                block(col_ref[j])
-                return carry
-
-            lax.fori_loop(0, col_ref.shape[0], step, 0)
+            out_ref[i] += dot(probes, weights, NN)
 
 
 def apply_rows(hyper, rows, cols, start=()):
-    samples = rows[0].shape[1]
-    width = cols[0].shape[-2] - samples
-    half_rows = len(rows) // 2
+    channels, samples = rows[0].shape
+    depth, tall, _ = cols[0].shape
+    width = tall - samples
     vmem = pl.BlockSpec(memory_space=pltpu.VMEM)
-    blocks = sum(math.prod(c.shape[:-2]) for c in cols)
-    pairs = blocks * len(rows) * samples * samples
-    out = jax.ShapeDtypeStruct((half_rows, width, samples), jnp.float32)
+    pairs = len(cols) * depth * len(rows) * samples * samples
     return pl.pallas_call(
-        functools.partial(apply_kernel, len(rows), len(cols), 1 if start else 0),
-        out_shape=[out, out],
+        functools.partial(apply_kernel, len(rows), len(cols), len(start)),
+        out_shape=jax.ShapeDtypeStruct((len(rows), width, samples), jnp.float32),
         in_specs=[pl.BlockSpec(memory_space=pltpu.SMEM)]
         + [vmem] * (len(rows) + len(cols) + len(start)),
-        out_specs=[vmem, vmem],
+        out_specs=vmem,
         scratch_shapes=[pltpu.VMEM((len(rows), samples), jnp.float32)],
+        compiler_params=pltpu.CompilerParams(vmem_limit_bytes=24 << 20),
         cost_estimate=pl.CostEstimate(
-            flops=2 * pairs * (256 + 64), transcendentals=pairs, bytes_accessed=4 << 20
+            flops=2 * pairs * (channels + width), transcendentals=pairs, bytes_accessed=4 << 20
         ),
         name="apply_rows",
     )(hyper, *rows, *cols, *start)
@@ -253,10 +240,14 @@
     image_ref[...] = image
     size = image.shape[0]
     packed_ref[:size, :size] = dot(basis, image, NT, HIGHEST)
-    packed_ref[:size, size:] = dot(image, image, NT, HIGHEST)
-    square = dot(basis, basis, NT, HIGHEST)
-    packed_ref[size:, :size] = square[: size // 2]
-    packed_ref[size:, size:] = square[size // 2 :]
+    image_sq = dot(image, image, NT, HIGHEST)
+    basis_sq = dot(basis, basis, NT, HIGHEST)
+    down = lax.broadcasted_iota(jnp.int32, (size, size), 0)
+    across = lax.broadcasted_iota(jnp.int32, (size, size), 1)
+    packed_ref[:size, size:] = jnp.where(across >= down, image_sq, basis_sq)
+    diagonal = jnp.sum(jnp.where(across == down, basis_sq, 0.0), axis=0, keepdims=True)
+    packed_ref[size:, :size] = jnp.broadcast_to(diagonal, (8, size))
+    packed_ref[size:, size:] = jnp.zeros((8, size), jnp.float32)
 
 
 def gram_stage(inv_root, hyper, parts, probes_t, prev_t, coupling, half):
@@ -280,49 +271,81 @@
                 whole((size, samples)),
                 whole((size, size)),
             ],
-            out_specs=[whole((size, samples)), whole((size * 3 // 2, 2 * size))],
+            out_specs=[whole((size, samples)), whole((size + 8, 2 * size))],
         ),
         out_shape=[
             jax.ShapeDtypeStruct((size, samples), jnp.float32),
-            jax.ShapeDtypeStruct((size * 3 // 2, 2 * size), jnp.float32),
+            jax.ShapeDtypeStruct((size + 8, 2 * size), jnp.float32),
         ],
         name="gram_stage",
     )(half, hyper, *parts, probes_t, prev_t, coupling)
 
 
+PANEL = 4
+
+
 def finish_kernel(inv_root, half_ref, packed_ref, image_ref, probe_ref, a_ref, r_ref, next_ref):
     size = image_ref.shape[0]
     block_a = packed_ref[:size, :size]
-    image_sq = packed_ref[:size, size:]
-    square = jnp.concatenate([packed_ref[size:, :size], packed_ref[size:, size:]], axis=0)
+    mixed = packed_ref[:size, size:]
+    mixed_t = mixed.T
+    diagonal = packed_ref[size : size + 1, :size]
+    down = lax.broadcasted_iota(jnp.int32, (size, size), 0)
+    across = lax.broadcasted_iota(jnp.int32, (size, size), 1)
+    image_sq = jnp.where(across >= down, mixed, mixed_t)
+    square = jnp.where(across == down, diagonal, jnp.where(across < down, mixed, mixed_t))
     twice = 2.0 * block_a - dot(square, block_a, NN, HIGHEST)
     gram = image_sq - dot(block_a, twice, TN, HIGHEST)
     basis = probe_ref[...].astype(jnp.float32) * inv_root
     resid = image_ref[...] - dot(block_a, basis, TN, HIGHEST)
 
-    row_id = lax.broadcasted_iota(jnp.int32, (size, 2 * size), 0)
-    lane_id = lax.broadcasted_iota(jnp.int32, (size, 2 * size), 1)
-    unit = jnp.where(lane_id == row_id + size, 1.0, 0.0)
-    work = jnp.concatenate([gram, jnp.zeros_like(gram)], axis=1) + unit
+    unit = jnp.where(across == down, 1.0, 0.0)
+    work = jnp.concatenate([gram, unit], axis=1)
     tiles = [work[8 * i : 8 * i + 8, :] for i in range(size // 8)]
-    sub_id = lax.broadcasted_iota(jnp.int32, (8, 2 * size), 0)
-    for j in range(size):
+    wide = (8, 2 * size)
+    sub_id = lax.broadcasted_iota(jnp.int32, wide, 0)
+    for j in range(0, size, PANEL):
         home, place = divmod(j, 8)
-        row = jnp.broadcast_to(tiles[home][place : place + 1, :], (8, 2 * size))
-        scale = lax.rsqrt(jnp.broadcast_to(row[:, j : j + 1], (8, 2 * size)))
-        row = row * scale
+        rows = [
+            jnp.broadcast_to(tiles[home][place + a : place + a + 1, :], wide)
+            for a in range(PANEL)
+        ]
+        corner = [
+            [jnp.broadcast_to(rows[a][:, j + b : j + b + 1], wide) if b >= a else None
+             for b in range(PANEL)]
+            for a in range(PANEL)
+        ]
+        scales = []
+        for a in range(PANEL):
+            scale = lax.rsqrt(corner[a][a])
+            scales.append(scale)
+            rows[a] = rows[a] * scale
+            for b in range(a + 1, PANEL):
+                corner[a][b] = corner[a][b] * scale
+            for c in range(a + 1, PANEL):
+                rows[c] = rows[c] - corner[a][c] * rows[a]
+                for b in range(c, PANEL):
+                    corner[c][b] = corner[c][b] - corner[a][c] * corner[a][b]
         for i in range(home, size // 8):
-            column = jnp.broadcast_to(tiles[i][:, j : j + 1], (8, 2 * size)) * scale
+            if i == home and place + PANEL == 8:
+                continue
+            columns = []
+            for b in range(PANEL):
+                column = jnp.broadcast_to(tiles[i][:, j + b : j + b + 1], wide)
+                for a in range(b):
+                    column = column - columns[a] * corner[a][b]
+                columns.append(column * scales[b])
+            lowered = tiles[i]
+            for b in range(PANEL):
+                lowered = lowered - columns[b] * rows[b]
             if i == home:
-                column = jnp.where(sub_id > place, column, 0.0)
-            tiles[i] = tiles[i] - column * row
-            if i == home:
-                tiles[i] = jnp.where(sub_id == place, row, tiles[i])
+                lowered = jnp.where(sub_id >= place + PANEL, lowered, tiles[i])
+            tiles[i] = lowered
+        for a in range(PANEL):
+            tiles[home] = jnp.where(sub_id == place + a, rows[a], tiles[home])
     work = jnp.concatenate(tiles, axis=0)
-    upper_rows = lax.broadcasted_iota(jnp.int32, (size, size), 0)
-    upper_cols = lax.broadcasted_iota(jnp.int32, (size, size), 1)
     a_ref[...] = block_a
-    r_ref[...] = jnp.where(upper_cols >= upper_rows, work[:, :size], 0.0)
+    r_ref[...] = jnp.where(across >= down, work[:, :size], 0.0)
     next_ref[...] = dot(work[:, size:], resid, NN, HIGHEST) * (1.0 / inv_root)
 
 
@@ -355,7 +378,7 @@
     return (value + two) + (one + three)
 
 
-def per_device(
+def lanczos_step(
     tokens, lengths, embed, conv_w, conv_b, inv_len, hyper, probes, prev_probes, coupling
 ):
     total_rows = tokens.shape[0] * lax.axis_size("blk")
@@ -366,17 +389,20 @@
         tokens.T, lengths, embed, conv_w, conv_b, inv_len, probes_t, half
     )
     near = [send(cols, shift_by_core(s, 0)) for s in (1, 2, 3)]
-    own_rows = [rows] + [send(rows, shift_y(s)) for s in (1, 2, 3)]
+    all_rows = [rows] + [send(rows, shift_y(s)) for s in (1, 2, 3)]
     group = jnp.stack([cols] + near)
     far = [send(group, shift_by_core(s, 1)) for s in (1, 3, 2)]
-    other_rows = [send(r, core_swap()) for r in own_rows]
-    all_rows = own_rows + other_rows
-    partial = apply_rows(hyper, all_rows, [group])
-    for block in far:
-        partial = apply_rows(hyper, all_rows, [block], partial)
-    own, other = partial
-    joint = own + send(other, core_swap())
-    parts = [joint[0]] + [send(joint[s], shift_y(-s)) for s in (1, 2, 3)]
+    swap = core_swap()
+
+    def apply(blocks, start=()):
+        return apply_rows(hyper, all_rows, blocks, start)
+
+    partial = apply([group, send(group, swap)])
+    partial = apply([far[0], far[1]], [partial])
+    swapped = [send(far[0], swap), send(far[1], swap)]
+    partial = apply(swapped + [far[2]], [partial])
+    partial = apply([send(far[2], swap)], [partial])
+    parts = [partial[0]] + [send(partial[s], shift_y(-s)) for s in (1, 2, 3)]
     image, packed = gram_stage(inv_root, hyper, parts, probes_t, prev_probes.T, coupling, half)
     packed = packed + send(packed, core_swap())
     for shift in (shift_z, shift_x, shift_y):
@@ -387,7 +413,7 @@
 
 def solution(mesh):
     return jax.shard_map(
-        per_device,
+        lanczos_step,
         mesh=mesh,
         in_specs=(
             P("blk", None),

time: 142 us -> 123 us (0.87)
  Pallas kernels: 65.7 us -> 35.5 us
  starting transfers between devices: 27.3 us -> 44.5 us
  local copies, waits for them, and re-layouts: 4.9 us -> 1.28 us
  waiting for transfers between devices: 39.4 us -> 37.7 us
    pallas_call x4, Pallas kernels: 41.3 us -> 16.9 us  [apply_rows(): pl.pallas_call(functools.partial(apply_kernel, len(rows), len(cols), len(...]
    ppermute x27 -> x26, starting transfers between devices: 27.3 us -> 44.5 us  [send(): return lax.ppermute(value, AXES, perm)]
    pallas_call x1, Pallas kernels: 10.7 us -> 4.87 us  [finish(): pl.pallas_call(functools.partial(finish_kernel, inv_root), grid_spec=pltp...]
    unnamed x30 -> x10, local copies, waits for them, and re-layouts: 4.25 us -> 0.63 us
    ppermute x27 -> x26, waiting for transfers between devices: 39.4 us -> 37.7 us  [send(): return lax.ppermute(value, AXES, perm)]
  transfers between devices with their start and end apart: 27 -> 26, of which waited for: 19 -> 18; matrix products, arithmetic and copies ran while one was open for 0% -> 0% of each run, Pallas kernels for 22% -> 12%
where the time goes in v2:
time: 123 us; the launch traced here: 122 us
  starting transfers between devices  44.5 us (36%)
  waiting for transfers between devices  37.7 us (31%)
  Pallas kernels  35.5 us (29%)
  other arithmetic  2.46 us (2%)
  local copies, waits for them, and re-layouts  1.28 us (1%)
    ppermute x26, starting transfers between devices, send(): return lax.ppermute(value, AXES, perm)  44.5 us
    ppermute x26, waiting for transfers between devices, send(): return lax.ppermute(value, AXES, perm)  37.7 us
    pallas_call x4, Pallas kernels, apply_rows(): pl.pallas_call(functools.partial(apply_kernel, len(rows), len(cols), len(...  16.9 us
    pallas_call x1, Pallas kernels, conv_features(): pl.pallas_call(functools.partial(conv_kernel, taps), grid_spec=pltpu.Pref...  11.5 us
    pallas_call x1, Pallas kernels, finish(): pl.pallas_call(functools.partial(finish_kernel, inv_root), grid_spec=pltp...  4.87 us
  transfers between devices with their start and end apart: 26, of which 18 were waited for; matrix products, arithmetic and copies ran while one was open for 0% of the time, Pallas kernels for 12%

profile of v2, /device:TPU:2, one launch (start us, length us, event | category | flops | bytes accessed | tf_op | source)
XLA Modules:
  0.0 122.2 jit_solution(4674544318045470422)
XLA Ops:
  0.6 11.5 %conv_features.1 = (bf16[320,256]{1,0:T(8,128)(2,1)}, bf16[256,256]{1,0:T(8,128)(2,1)}) custom-call(s32[1]{0:T(128)} %bitcast.half_ref, s32[69,512]{1,0:T(8,128)} %bitcast.27, s32[1,512]{1,0:T(1,128)} %bitcast.29, bf16[64,256]{1,0:T(8,128)(2,1)} %embed_ref.1, bf16[7,32,256]{2,1,0:T(8,128)(2,1)} %w_ref.1, f32[1,256]{1,0:T(1,128)} %bitcast.30, ...), custom_call_target="tpu_custom_call" | custom-call | tf_op jit(solution)/shard_map/conv_features/pallas_call | solution.py:147
  12.1 1.9 %collective-permute-start.3 = (bf16[320,256]{1,0:T(8,128)(2,1)}, bf16[320,256]{1,0:T(8,128)(2,1)S(1)}, u32[]{:S(2)}, u32[]{:S(2)}) collective-permute-start(bf16[320,256]{1,0:T(8,128)(2,1)} %get-tuple-element.11), channel_id=1, source_target_pairs={{0,32},{1,33},{2,10},{3,11},{4,36},{5,37},{6,14},{7,15},{8,40},{9,... | collective-permute-start | bytes 491528 | tf_op jit(solution)/shard_map/ppermute | solution.py:57
  14.0 3.6 %collective-permute-start.4 = (bf16[320,256]{1,0:T(8,128)(2,1)}, bf16[320,256]{1,0:T(8,128)(2,1)S(1)}, u32[]{:S(2)}, u32[]{:S(2)}) collective-permute-start(bf16[320,256]{1,0:T(8,128)(2,1)} %get-tuple-element.11), channel_id=1, source_target_pairs={{0,64},{1,65},{2,18},{3,19},{4,68},{5,69},{6,22},{7,23},{8,72},{9,... | collective-permute-start | bytes 491528 | tf_op jit(solution)/shard_map/ppermute | solution.py:57
  19.7 3.2 %collective-permute-done.4 = bf16[320,256]{1,0:T(8,128)(2,1)S(1)} collective-permute-done((bf16[320,256]{1,0:T(8,128)(2,1)}, bf16[320,256]{1,0:T(8,128)(2,1)S(1)}, u32[]{:S(2)}, u32[]{:S(2)}) %collective-permute-start.4) | collective-permute-done | bytes 163872 | tf_op jit(solution)/shard_map/ppermute | solution.py:57
  26.3 3.3 %collective-permute-start.6 = (bf16[4,320,256]{2,1,0:T(8,128)(2,1)S(1)}, bf16[4,320,256]{2,1,0:T(8,128)(2,1)S(1)}, u32[]{:S(2)}, u32[]{:S(2)}) collective-permute-start(bf16[4,320,256]{2,1,0:T(8,128)(2,1)S(1)} %pad_maximum_fusion.refs_4_), channel_id=1, source_target_pairs={{0,16},{1,17},{2,66},{3,67},{4,20},{5,21},{6,70},{7,71},{8,24},{9,... | collective-permute-start | bytes 1966088 | tf_op jit(solution)/shard_map/ppermute | solution.py:57
  29.6 5.2 %collective-permute-done.10.refs_5_ = bf16[4,320,256]{2,1,0:T(8,128)(2,1)S(1)} collective-permute-done((bf16[4,320,256]{2,1,0:T(8,128)(2,1)S(1)}, bf16[4,320,256]{2,1,0:T(8,128)(2,1)S(1)}, u32[]{:S(2)}, u32[]{:S(2)}) %collective-permute-start.10) | collective-permute-done | bytes 655392 | tf_op jit(solution)/shard_map/ppermute | solution.py:57
  34.8 5.0 %collective-permute-start.11 = (bf16[4,320,256]{2,1,0:T(8,128)(2,1)S(1)}, bf16[4,320,256]{2,1,0:T(8,128)(2,1)S(1)}, u32[]{:S(2)}, u32[]{:S(2)}) collective-permute-start(bf16[4,320,256]{2,1,0:T(8,128)(2,1)S(1)} %collective-permute-done.10.refs_5_), channel_id=1, source_target_pairs={{0,2},{1,3},{2,0},{3,1},{4,6},{5,7},{6,4},{7,5},{8,10},{9,11},{10,... | collective-permute-start | bytes 1966088 | tf_op jit(solution)/shard_map/ppermute | solution.py:57
  39.9 3.1 %collective-permute-start.9 = (bf16[4,320,256]{2,1,0:T(8,128)(2,1)S(1)}, bf16[4,320,256]{2,1,0:T(8,128)(2,1)S(1)}, u32[]{:S(2)}, u32[]{:S(2)}) collective-permute-start(bf16[4,320,256]{2,1,0:T(8,128)(2,1)S(1)} %collective-permute-done.8.refs_4_), channel_id=1, source_target_pairs={{0,2},{1,3},{2,0},{3,1},{4,6},{5,7},{6,4},{7,5},{8,10},{9,11},{10,... | collective-permute-start | bytes 1966088 | tf_op jit(solution)/shard_map/ppermute | solution.py:57
  43.0 1.6 %collective-permute-start = (bf16[256,256]{1,0:T(8,128)(2,1)S(1)}, bf16[256,256]{1,0:T(8,128)(2,1)S(1)}, u32[]{:S(2)}, u32[]{:S(2)}) collective-permute-start(bf16[256,256]{1,0:T(8,128)(2,1)S(1)} %copy-done.1), channel_id=1, source_target_pairs={{0,4},{1,5},{2,6},{3,7},{4,1},{5,0},{6,3},{7,2},{8,12},{9,13},{10,... | collective-permute-start | bytes 393224 | tf_op jit(solution)/shard_map/ppermute | solution.py:57
  44.5 5.1 %collective-permute-done.refs_1_ = bf16[256,256]{1,0:T(8,128)(2,1)S(1)} collective-permute-done((bf16[256,256]{1,0:T(8,128)(2,1)S(1)}, bf16[256,256]{1,0:T(8,128)(2,1)S(1)}, u32[]{:S(2)}, u32[]{:S(2)}) %collective-permute-start) | collective-permute-done | bytes 131104 | tf_op jit(solution)/shard_map/ppermute | solution.py:57
  49.6 1.9 %collective-permute-start.1 = (bf16[256,256]{1,0:T(8,128)(2,1)S(1)}, bf16[256,256]{1,0:T(8,128)(2,1)S(1)}, u32[]{:S(2)}, u32[]{:S(2)}) collective-permute-start(bf16[256,256]{1,0:T(8,128)(2,1)S(1)} %copy-done.1), channel_id=1, source_target_pairs={{0,1},{1,0},{2,3},{3,2},{4,5},{5,4},{6,7},{7,6},{8,9},{9,8},{10,11... | collective-permute-start | bytes 393224 | tf_op jit(solution)/shard_map/ppermute | solution.py:57
  51.6 4.5 %collective-permute-done.1.refs_2_ = bf16[256,256]{1,0:T(8,128)(2,1)S(1)} collective-permute-done((bf16[256,256]{1,0:T(8,128)(2,1)S(1)}, bf16[256,256]{1,0:T(8,128)(2,1)S(1)}, u32[]{:S(2)}, u32[]{:S(2)}) %collective-permute-start.1) | collective-permute-done | bytes 131104 | tf_op jit(solution)/shard_map/ppermute | solution.py:57
  56.1 1.7 %collective-permute-start.2 = (bf16[256,256]{1,0:T(8,128)(2,1)S(1)}, bf16[256,256]{1,0:T(8,128)(2,1)S(1)}, u32[]{:S(2)}, u32[]{:S(2)}) collective-permute-start(bf16[256,256]{1,0:T(8,128)(2,1)S(1)} %copy-done.1), channel_id=1, source_target_pairs={{0,5},{1,4},{2,7},{3,6},{4,0},{5,1},{6,2},{7,3},{8,13},{9,12},{10,... | collective-permute-start | bytes 393224 | tf_op jit(solution)/shard_map/ppermute | solution.py:57
  57.9 3.2 %collective-permute-done.2.refs_3_ = bf16[256,256]{1,0:T(8,128)(2,1)S(1)} collective-permute-done((bf16[256,256]{1,0:T(8,128)(2,1)S(1)}, bf16[256,256]{1,0:T(8,128)(2,1)S(1)}, u32[]{:S(2)}, u32[]{:S(2)}) %collective-permute-start.2) | collective-permute-done | bytes 131104 | tf_op jit(solution)/shard_map/ppermute | solution.py:57
  61.1 4.2 %apply_rows.4.refs_6_ = f32[4,64,256]{2,1,0:T(8,128)S(1)} custom-call(f32[2]{0:T(128)S(1)} %copy-done, bf16[256,256]{1,0:T(8,128)(2,1)S(1)} %copy-done.1, bf16[256,256]{1,0:T(8,128)(2,1)S(1)} %collective-permute-done.refs_1_, bf16[256,256]{1,0:T(8,128)(2,1)S(1)} %collective-permute-done.1.refs_2_, bf16[256,256]{1,0:T(8,128)(2,1)S(1)} %collective-permute-done.2.refs_3_, ...), custom_call_target="tpu_custom_call" | custom-call | flops 1342177280 | bytes 4194304 | tf_op jit(solution)/shard_map/apply_rows/pallas_call | solution.py:214
  65.3 4.2 %apply_rows.5.refs_7_ = f32[4,64,256]{2,1,0:T(8,128)S(1)} custom-call(f32[2]{0:T(128)S(1)} %copy-done, bf16[256,256]{1,0:T(8,128)(2,1)S(1)} %copy-done.1, bf16[256,256]{1,0:T(8,128)(2,1)S(1)} %collective-permute-done.refs_1_, bf16[256,256]{1,0:T(8,128)(2,1)S(1)} %collective-permute-done.1.refs_2_, bf16[256,256]{1,0:T(8,128)(2,1)S(1)} %collective-permute-done.2.refs_3_, ...), custom_call_target="tpu_custom_call" | custom-call | flops 1342177280 | bytes 4194304 | tf_op jit(solution)/shard_map/apply_rows/pallas_call | solution.py:214
  69.6 6.0 %apply_rows.6.refs_5_ = f32[4,64,256]{2,1,0:T(8,128)S(1)} custom-call(f32[2]{0:T(128)S(1)} %copy-done, bf16[256,256]{1,0:T(8,128)(2,1)S(1)} %copy-done.1, bf16[256,256]{1,0:T(8,128)(2,1)S(1)} %collective-permute-done.refs_1_, bf16[256,256]{1,0:T(8,128)(2,1)S(1)} %collective-permute-done.1.refs_2_, bf16[256,256]{1,0:T(8,128)(2,1)S(1)} %collective-permute-done.2.refs_3_, ...), custom_call_target="tpu_custom_call" | custom-call | flops 2013265920 | bytes 4194304 | tf_op jit(solution)/shard_map/apply_rows/pallas_call | solution.py:214
  75.6 2.5 %apply_rows.7 = f32[4,64,256]{2,1,0:T(8,128)S(1)} custom-call(f32[2]{0:T(128)S(1)} %copy-done, bf16[256,256]{1,0:T(8,128)(2,1)S(1)} %copy-done.1, bf16[256,256]{1,0:T(8,128)(2,1)S(1)} %collective-permute-done.refs_1_, bf16[256,256]{1,0:T(8,128)(2,1)S(1)} %collective-permute-done.1.refs_2_, bf16[256,256]{1,0:T(8,128)(2,1)S(1)} %collective-permute-done.2.refs_3_, ...), custom_call_target="tpu_custom_call" | custom-call | flops 671088640 | bytes 4194304 | tf_op jit(solution)/shard_map/apply_rows/pallas_call | solution.py:214
  78.7 3.0 %collective-permute-start.13 = (f32[64,256]{1,0:T(8,128)S(1)}, f32[64,256]{1,0:T(8,128)S(1)}, u32[]{:S(2)}, u32[]{:S(2)}) collective-permute-start(f32[64,256]{1,0:T(8,128)S(1)} %get-tuple-element.19), channel_id=1, source_target_pairs={{0,5},{1,4},{2,7},{3,6},{4,0},{5,1},{6,2},{7,3},{8,13},{9,12},{10,... | collective-permute-start | bytes 196616 | tf_op jit(solution)/shard_map/ppermute | solution.py:57
  82.5 1.7 %collective-permute-done.13.one = f32[64,256]{1,0:T(8,128)S(1)} collective-permute-done((f32[64,256]{1,0:T(8,128)S(1)}, f32[64,256]{1,0:T(8,128)S(1)}, u32[]{:S(2)}, u32[]{:S(2)}) %collective-permute-start.13) | collective-permute-done | bytes 65568 | tf_op jit(solution)/shard_map/ppermute | solution.py:57
  84.2 3.3 %collective-permute-done.14.two = f32[64,256]{1,0:T(8,128)S(1)} collective-permute-done((f32[64,256]{1,0:T(8,128)S(1)}, f32[64,256]{1,0:T(8,128)S(1)}, u32[]{:S(2)}, u32[]{:S(2)}) %collective-permute-start.14) | collective-permute-done | bytes 65568 | tf_op jit(solution)/shard_map/ppermute | solution.py:57
  88.5 2.2 %gram_stage.1 = (f32[64,256]{1,0:T(8,128)}, f32[72,128]{1,0:T(8,128)}) custom-call(s32[1]{0:T(128)} %bitcast.half_ref, f32[2]{0:T(128)} %hyper_ref.9, f32[64,256]{1,0:T(8,128)} %get-tuple-element.20.own, f32[64,256]{1,0:T(8,128)} %copy-done.2, f32[64,256]{1,0:T(8,128)} %copy-done.3, f32[64,256]{1,0:T(8,128)} %copy-done.4, bf16[64,512]{1,0:T(8,128)(2,1)} %bitcast.21, ...), custom_call_target="tpu_custom_call" | custom-call | tf_op jit(solution)/shard_map/gram_stage/pallas_call | solution.py:262
  92.9 1.8 %collective-permute-start.18 = (f32[72,128]{1,0:T(8,128)S(1)}, f32[72,128]{1,0:T(8,128)S(1)}, u32[]{:S(2)}, u32[]{:S(2)}) collective-permute-start(f32[72,128]{1,0:T(8,128)S(1)} %add.30), channel_id=1, source_target_pairs={{0,32},{1,33},{2,34},{3,35},{4,36},{5,37},{6,38},{7,39},{8,40},{9,... | collective-permute-start | bytes 110600 | tf_op jit(solution)/shard_map/ppermute | solution.py:57
  94.7 1.5 %collective-permute-start.19 = (f32[72,128]{1,0:T(8,128)S(1)}, f32[72,128]{1,0:T(8,128)S(1)}, u32[]{:S(2)}, u32[]{:S(2)}) collective-permute-start(f32[72,128]{1,0:T(8,128)S(1)} %add.30), channel_id=1, source_target_pairs={{0,96},{1,97},{2,98},{3,99},{4,100},{5,101},{6,102},{7,103},{8,104... | collective-permute-start | bytes 110600 | tf_op jit(solution)/shard_map/ppermute | solution.py:57
  96.2 2.2 %collective-permute-done.17 = f32[72,128]{1,0:T(8,128)S(1)} collective-permute-done((f32[72,128]{1,0:T(8,128)S(1)}, f32[72,128]{1,0:T(8,128)S(1)}, u32[]{:S(2)}, u32[]{:S(2)}) %collective-permute-start.17) | collective-permute-done | bytes 36896 | tf_op jit(solution)/shard_map/ppermute | solution.py:57
  98.7 4.6 %collective-permute-start.20 = (f32[72,128]{1,0:T(8,128)S(1)}, f32[72,128]{1,0:T(8,128)S(1)}, u32[]{:S(2)}, u32[]{:S(2)}) collective-permute-start(f32[72,128]{1,0:T(8,128)S(1)} %add_add_fusion.2), channel_id=1, source_target_pairs={{0,16},{1,17},{2,18},{3,19},{4,20},{5,21},{6,22},{7,23},{8,24},{9,... | collective-permute-start | bytes 110600 | tf_op jit(solution)/shard_map/ppermute | solution.py:57
  103.2 2.6 %collective-permute-start.21 = (f32[72,128]{1,0:T(8,128)S(1)}, f32[72,128]{1,0:T(8,128)S(1)}, u32[]{:S(2)}, u32[]{:S(2)}) collective-permute-start(f32[72,128]{1,0:T(8,128)S(1)} %add_add_fusion.2), channel_id=1, source_target_pairs={{0,8},{1,9},{2,10},{3,11},{4,12},{5,13},{6,14},{7,15},{8,16},{9,17... | collective-permute-start | bytes 110600 | tf_op jit(solution)/shard_map/ppermute | solution.py:57
  105.9 1.6 %collective-permute-done.21 = f32[72,128]{1,0:T(8,128)S(1)} collective-permute-done((f32[72,128]{1,0:T(8,128)S(1)}, f32[72,128]{1,0:T(8,128)S(1)}, u32[]{:S(2)}, u32[]{:S(2)}) %collective-permute-start.21) | collective-permute-done | bytes 36896 | tf_op jit(solution)/shard_map/ppermute | solution.py:57
  107.5 2.3 %collective-permute-done.22 = f32[72,128]{1,0:T(8,128)S(1)} collective-permute-done((f32[72,128]{1,0:T(8,128)S(1)}, f32[72,128]{1,0:T(8,128)S(1)}, u32[]{:S(2)}, u32[]{:S(2)}) %collective-permute-start.22) | collective-permute-done | bytes 36896 | tf_op jit(solution)/shard_map/ppermute | solution.py:57
  109.8 1.7 %collective-permute-start.23 = (f32[72,128]{1,0:T(8,128)S(1)}, f32[72,128]{1,0:T(8,128)S(1)}, u32[]{:S(2)}, u32[]{:S(2)}) collective-permute-start(f32[72,128]{1,0:T(8,128)S(1)} %add_add_fusion.1), channel_id=1, source_target_pairs={{0,1},{1,0},{2,3},{3,2},{4,5},{5,4},{6,7},{7,6},{8,9},{9,8},{10,11... | collective-permute-start | bytes 110600 | tf_op jit(solution)/shard_map/ppermute | solution.py:57
  111.6 3.1 %collective-permute-start.25 = (f32[72,128]{1,0:T(8,128)S(1)}, f32[72,128]{1,0:T(8,128)S(1)}, u32[]{:S(2)}, u32[]{:S(2)}) collective-permute-start(f32[72,128]{1,0:T(8,128)S(1)} %add_add_fusion.1), channel_id=1, source_target_pairs={{0,5},{1,4},{2,7},{3,6},{4,0},{5,1},{6,2},{7,3},{8,13},{9,12},{10,... | collective-permute-start | bytes 110600 | tf_op jit(solution)/shard_map/ppermute | solution.py:57
  117.3 4.9 %finish.1 = (f32[64,64]{1,0:T(8,128)}, f32[64,64]{1,0:T(8,128)}, f32[64,256]{1,0:T(8,128)}) custom-call(s32[1]{0:T(128)} %bitcast.half_ref, f32[72,128]{1,0:T(8,128)} %add_add_fusion.packed_ref, f32[64,256]{1,0:T(8,128)} %get-tuple-element.13.image_ref, bf16[64,512]{1,0:T(8,128)(2,1)} %bitcast.22), custom_call_target="tpu_custom_call" | custom-call | tf_op jit(solution)/shard_map/finish/pallas_call | solution.py:355
  (43 shorter events, 13.1 us)
Async XLA Ops:
  12.1 7.5 %collective-permute-start.3 = (bf16[320,256]{1,0:T(8,128)(2,1)}, bf16[320,256]{1,0:T(8,128)(2,1)S(1)}, u32[]{:S(2)}, u32[]{:S(2)}) collective-permute-start(bf16[320,256]{1,0:T(8,128)(2,1)} %get-tuple-element.11), channel_id=1, source_target_pairs={{0,32},{1,33},{2,10},{3,11},{4,36},{5,37},{6,14},{7,15},{8,40},{9,... | collective-permute-start | bytes 491528 | tf_op jit(solution)/shard_map/ppermute | solution.py:57
  14.0 8.8 %collective-permute-start.4 = (bf16[320,256]{1,0:T(8,128)(2,1)}, bf16[320,256]{1,0:T(8,128)(2,1)S(1)}, u32[]{:S(2)}, u32[]{:S(2)}) collective-permute-start(bf16[320,256]{1,0:T(8,128)(2,1)} %get-tuple-element.11), channel_id=1, source_target_pairs={{0,64},{1,65},{2,18},{3,19},{4,68},{5,69},{6,22},{7,23},{8,72},{9,... | collective-permute-start | bytes 491528 | tf_op jit(solution)/shard_map/ppermute | solution.py:57
  17.6 5.5 %collective-permute-start.5 = (bf16[320,256]{1,0:T(8,128)(2,1)}, bf16[320,256]{1,0:T(8,128)(2,1)S(1)}, u32[]{:S(2)}, u32[]{:S(2)}) collective-permute-start(bf16[320,256]{1,0:T(8,128)(2,1)} %get-tuple-element.11), channel_id=1, source_target_pairs={{0,96},{1,97},{2,26},{3,27},{4,100},{5,101},{6,30},{7,31},{8,104},... | collective-permute-start | bytes 491528 | tf_op jit(solution)/shard_map/ppermute | solution.py:57
  23.1 19.8 %copy-start.1 = (bf16[256,256]{1,0:T(8,128)(2,1)S(1)}, bf16[256,256]{1,0:T(8,128)(2,1)}, u32[]{:S(2)}) copy-start(bf16[256,256]{1,0:T(8,128)(2,1)} %get-tuple-element.10.refs_0_) | copy-start | bytes 393220
  24.2 36.9 %copy-start = (f32[2]{0:T(128)S(1)}, f32[2]{0:T(128)}, u32[]{:S(2)}) copy-start(f32[2]{0:T(128)} %hyper_ref.9) | copy-start | bytes 28
  24.2 10.7 %collective-permute-start.10 = (bf16[4,320,256]{2,1,0:T(8,128)(2,1)S(1)}, bf16[4,320,256]{2,1,0:T(8,128)(2,1)S(1)}, u32[]{:S(2)}, u32[]{:S(2)}) collective-permute-start(bf16[4,320,256]{2,1,0:T(8,128)(2,1)S(1)} %pad_maximum_fusion.refs_4_), channel_id=1, source_target_pairs={{0,24},{1,25},{2,98},{3,99},{4,28},{5,29},{6,102},{7,103},{8,0},{9... | collective-permute-start | bytes 1966088 | tf_op jit(solution)/shard_map/ppermute | solution.py:57
  24.8 15.1 %collective-permute-start.8 = (bf16[4,320,256]{2,1,0:T(8,128)(2,1)S(1)}, bf16[4,320,256]{2,1,0:T(8,128)(2,1)S(1)}, u32[]{:S(2)}, u32[]{:S(2)}) collective-permute-start(bf16[4,320,256]{2,1,0:T(8,128)(2,1)S(1)} %pad_maximum_fusion.refs_4_), channel_id=1, source_target_pairs={{0,8},{1,9},{2,34},{3,35},{4,12},{5,13},{6,38},{7,39},{8,16},{9,17... | collective-permute-start | bytes 1966088 | tf_op jit(solution)/shard_map/ppermute | solution.py:57
  26.3 25.3 %collective-permute-start.6 = (bf16[4,320,256]{2,1,0:T(8,128)(2,1)S(1)}, bf16[4,320,256]{2,1,0:T(8,128)(2,1)S(1)}, u32[]{:S(2)}, u32[]{:S(2)}) collective-permute-start(bf16[4,320,256]{2,1,0:T(8,128)(2,1)S(1)} %pad_maximum_fusion.refs_4_), channel_id=1, source_target_pairs={{0,16},{1,17},{2,66},{3,67},{4,20},{5,21},{6,70},{7,71},{8,24},{9,... | collective-permute-start | bytes 1966088 | tf_op jit(solution)/shard_map/ppermute | solution.py:57
  29.6 31.5 %collective-permute-start.12 = (bf16[4,320,256]{2,1,0:T(8,128)(2,1)S(1)}, bf16[4,320,256]{2,1,0:T(8,128)(2,1)S(1)}, u32[]{:S(2)}, u32[]{:S(2)}) collective-permute-start(bf16[4,320,256]{2,1,0:T(8,128)(2,1)S(1)} %pad_maximum_fusion.refs_4_), channel_id=1, source_target_pairs={{0,2},{1,3},{2,0},{3,1},{4,6},{5,7},{6,4},{7,5},{8,10},{9,11},{10,... | collective-permute-start | bytes 1966088 | tf_op jit(solution)/shard_map/ppermute | solution.py:57
  34.8 34.7 %collective-permute-start.11 = (bf16[4,320,256]{2,1,0:T(8,128)(2,1)S(1)}, bf16[4,320,256]{2,1,0:T(8,128)(2,1)S(1)}, u32[]{:S(2)}, u32[]{:S(2)}) collective-permute-start(bf16[4,320,256]{2,1,0:T(8,128)(2,1)S(1)} %collective-permute-done.10.refs_5_), channel_id=1, source_target_pairs={{0,2},{1,3},{2,0},{3,1},{4,6},{5,7},{6,4},{7,5},{8,10},{9,11},{10,... | collective-permute-start | bytes 1966088 | tf_op jit(solution)/shard_map/ppermute | solution.py:57
  39.9 29.7 %collective-permute-start.9 = (bf16[4,320,256]{2,1,0:T(8,128)(2,1)S(1)}, bf16[4,320,256]{2,1,0:T(8,128)(2,1)S(1)}, u32[]{:S(2)}, u32[]{:S(2)}) collective-permute-start(bf16[4,320,256]{2,1,0:T(8,128)(2,1)S(1)} %collective-permute-done.8.refs_4_), channel_id=1, source_target_pairs={{0,2},{1,3},{2,0},{3,1},{4,6},{5,7},{6,4},{7,5},{8,10},{9,11},{10,... | collective-permute-start | bytes 1966088 | tf_op jit(solution)/shard_map/ppermute | solution.py:57
  43.0 6.7 %collective-permute-start = (bf16[256,256]{1,0:T(8,128)(2,1)S(1)}, bf16[256,256]{1,0:T(8,128)(2,1)S(1)}, u32[]{:S(2)}, u32[]{:S(2)}) collective-permute-start(bf16[256,256]{1,0:T(8,128)(2,1)S(1)} %copy-done.1), channel_id=1, source_target_pairs={{0,4},{1,5},{2,6},{3,7},{4,1},{5,0},{6,3},{7,2},{8,12},{9,13},{10,... | collective-permute-start | bytes 393224 | tf_op jit(solution)/shard_map/ppermute | solution.py:57
  49.6 6.5 %collective-permute-start.1 = (bf16[256,256]{1,0:T(8,128)(2,1)S(1)}, bf16[256,256]{1,0:T(8,128)(2,1)S(1)}, u32[]{:S(2)}, u32[]{:S(2)}) collective-permute-start(bf16[256,256]{1,0:T(8,128)(2,1)S(1)} %copy-done.1), channel_id=1, source_target_pairs={{0,1},{1,0},{2,3},{3,2},{4,5},{5,4},{6,7},{7,6},{8,9},{9,8},{10,11... | collective-permute-start | bytes 393224 | tf_op jit(solution)/shard_map/ppermute | solution.py:57
  51.6 24.0 %collective-permute-start.7 = (bf16[4,320,256]{2,1,0:T(8,128)(2,1)S(1)}, bf16[4,320,256]{2,1,0:T(8,128)(2,1)S(1)}, u32[]{:S(2)}, u32[]{:S(2)}) collective-permute-start(bf16[4,320,256]{2,1,0:T(8,128)(2,1)S(1)} %collective-permute-done.6.refs_6_), channel_id=1, source_target_pairs={{0,2},{1,3},{2,0},{3,1},{4,6},{5,7},{6,4},{7,5},{8,10},{9,11},{10,... | collective-permute-start | bytes 1966088 | tf_op jit(solution)/shard_map/ppermute | solution.py:57
  56.1 5.0 %collective-permute-start.2 = (bf16[256,256]{1,0:T(8,128)(2,1)S(1)}, bf16[256,256]{1,0:T(8,128)(2,1)S(1)}, u32[]{:S(2)}, u32[]{:S(2)}) collective-permute-start(bf16[256,256]{1,0:T(8,128)(2,1)S(1)} %copy-done.1), channel_id=1, source_target_pairs={{0,5},{1,4},{2,7},{3,6},{4,0},{5,1},{6,2},{7,3},{8,13},{9,12},{10,... | collective-permute-start | bytes 393224 | tf_op jit(solution)/shard_map/ppermute | solution.py:57
  78.7 5.5 %collective-permute-start.13 = (f32[64,256]{1,0:T(8,128)S(1)}, f32[64,256]{1,0:T(8,128)S(1)}, u32[]{:S(2)}, u32[]{:S(2)}) collective-permute-start(f32[64,256]{1,0:T(8,128)S(1)} %get-tuple-element.19), channel_id=1, source_target_pairs={{0,5},{1,4},{2,7},{3,6},{4,0},{5,1},{6,2},{7,3},{8,13},{9,12},{10,... | collective-permute-start | bytes 196616 | tf_op jit(solution)/shard_map/ppermute | solution.py:57
  81.7 5.9 %collective-permute-start.14 = (f32[64,256]{1,0:T(8,128)S(1)}, f32[64,256]{1,0:T(8,128)S(1)}, u32[]{:S(2)}, u32[]{:S(2)}) collective-permute-start(f32[64,256]{1,0:T(8,128)S(1)} %get-tuple-element.18), channel_id=1, source_target_pairs={{0,1},{1,0},{2,3},{3,2},{4,5},{5,4},{6,7},{7,6},{8,9},{9,8},{10,11... | collective-permute-start | bytes 196616 | tf_op jit(solution)/shard_map/ppermute | solution.py:57
  81.7 6.2 %collective-permute-start.15 = (f32[64,256]{1,0:T(8,128)S(1)}, f32[64,256]{1,0:T(8,128)S(1)}, u32[]{:S(2)}, u32[]{:S(2)}) collective-permute-start(f32[64,256]{1,0:T(8,128)S(1)} %get-tuple-element.17), channel_id=1, source_target_pairs={{0,4},{1,5},{2,6},{3,7},{4,1},{5,0},{6,3},{7,2},{8,12},{9,13},{10,... | collective-permute-start | bytes 196616 | tf_op jit(solution)/shard_map/ppermute | solution.py:57
  84.2 3.7 %copy-start.2 = (f32[64,256]{1,0:T(8,128)}, f32[64,256]{1,0:T(8,128)S(1)}, u32[]{:S(2)}) copy-start(f32[64,256]{1,0:T(8,128)S(1)} %collective-permute-done.13.one) | copy-start | bytes 196612
  87.6 0.6 copy-start.3
  87.9 0.6 copy-start.4
  90.7 1.4 %collective-permute-start.16 = (f32[72,128]{1,0:T(8,128)}, f32[72,128]{1,0:T(8,128)S(1)}, u32[]{:S(2)}, u32[]{:S(2)}) collective-permute-start(f32[72,128]{1,0:T(8,128)} %get-tuple-element.12), channel_id=1, source_target_pairs={{0,2},{1,3},{2,0},{3,1},{4,6},{5,7},{6,4},{7,5},{8,10},{9,11},{10,... | collective-permute-start | bytes 110600 | tf_op jit(solution)/shard_map/ppermute | solution.py:57
  92.9 5.5 %collective-permute-start.17 = (f32[72,128]{1,0:T(8,128)S(1)}, f32[72,128]{1,0:T(8,128)S(1)}, u32[]{:S(2)}, u32[]{:S(2)}) collective-permute-start(f32[72,128]{1,0:T(8,128)S(1)} %add.30), channel_id=1, source_target_pairs={{0,64},{1,65},{2,66},{3,67},{4,68},{5,69},{6,70},{7,71},{8,72},{9,... | collective-permute-start | bytes 110600 | tf_op jit(solution)/shard_map/ppermute | solution.py:57
  92.9 5.6 %collective-permute-start.18 = (f32[72,128]{1,0:T(8,128)S(1)}, f32[72,128]{1,0:T(8,128)S(1)}, u32[]{:S(2)}, u32[]{:S(2)}) collective-permute-start(f32[72,128]{1,0:T(8,128)S(1)} %add.30), channel_id=1, source_target_pairs={{0,32},{1,33},{2,34},{3,35},{4,36},{5,37},{6,38},{7,39},{8,40},{9,... | collective-permute-start | bytes 110600 | tf_op jit(solution)/shard_map/ppermute | solution.py:57
  94.7 4.0 %collective-permute-start.19 = (f32[72,128]{1,0:T(8,128)S(1)}, f32[72,128]{1,0:T(8,128)S(1)}, u32[]{:S(2)}, u32[]{:S(2)}) collective-permute-start(f32[72,128]{1,0:T(8,128)S(1)} %add.30), channel_id=1, source_target_pairs={{0,96},{1,97},{2,98},{3,99},{4,100},{5,101},{6,102},{7,103},{8,104... | collective-permute-start | bytes 110600 | tf_op jit(solution)/shard_map/ppermute | solution.py:57
  98.7 7.2 %collective-permute-start.20 = (f32[72,128]{1,0:T(8,128)S(1)}, f32[72,128]{1,0:T(8,128)S(1)}, u32[]{:S(2)}, u32[]{:S(2)}) collective-permute-start(f32[72,128]{1,0:T(8,128)S(1)} %add_add_fusion.2), channel_id=1, source_target_pairs={{0,16},{1,17},{2,18},{3,19},{4,20},{5,21},{6,22},{7,23},{8,24},{9,... | collective-permute-start | bytes 110600 | tf_op jit(solution)/shard_map/ppermute | solution.py:57
  103.2 4.3 %collective-permute-start.21 = (f32[72,128]{1,0:T(8,128)S(1)}, f32[72,128]{1,0:T(8,128)S(1)}, u32[]{:S(2)}, u32[]{:S(2)}) collective-permute-start(f32[72,128]{1,0:T(8,128)S(1)} %add_add_fusion.2), channel_id=1, source_target_pairs={{0,8},{1,9},{2,10},{3,11},{4,12},{5,13},{6,14},{7,15},{8,16},{9,17... | collective-permute-start | bytes 110600 | tf_op jit(solution)/shard_map/ppermute | solution.py:57
  105.9 4.0 %collective-permute-start.22 = (f32[72,128]{1,0:T(8,128)S(1)}, f32[72,128]{1,0:T(8,128)S(1)}, u32[]{:S(2)}, u32[]{:S(2)}) collective-permute-start(f32[72,128]{1,0:T(8,128)S(1)} %add_add_fusion.2), channel_id=1, source_target_pairs={{0,24},{1,25},{2,26},{3,27},{4,28},{5,29},{6,30},{7,31},{8,0},{9,1... | collective-permute-start | bytes 110600 | tf_op jit(solution)/shard_map/ppermute | solution.py:57
  109.8 5.5 %collective-permute-start.23 = (f32[72,128]{1,0:T(8,128)S(1)}, f32[72,128]{1,0:T(8,128)S(1)}, u32[]{:S(2)}, u32[]{:S(2)}) collective-permute-start(f32[72,128]{1,0:T(8,128)S(1)} %add_add_fusion.1), channel_id=1, source_target_pairs={{0,1},{1,0},{2,3},{3,2},{4,5},{5,4},{6,7},{7,6},{8,9},{9,8},{10,11... | collective-permute-start | bytes 110600 | tf_op jit(solution)/shard_map/ppermute | solution.py:57
  111.5 5.2 %collective-permute-start.24 = (f32[72,128]{1,0:T(8,128)S(1)}, f32[72,128]{1,0:T(8,128)S(1)}, u32[]{:S(2)}, u32[]{:S(2)}) collective-permute-start(f32[72,128]{1,0:T(8,128)S(1)} %add_add_fusion.1), channel_id=1, source_target_pairs={{0,4},{1,5},{2,6},{3,7},{4,1},{5,0},{6,3},{7,2},{8,12},{9,13},{10,... | collective-permute-start | bytes 110600 | tf_op jit(solution)/shard_map/ppermute | solution.py:57
  111.6 5.1 %collective-permute-start.25 = (f32[72,128]{1,0:T(8,128)S(1)}, f32[72,128]{1,0:T(8,128)S(1)}, u32[]{:S(2)}, u32[]{:S(2)}) collective-permute-start(f32[72,128]{1,0:T(8,128)S(1)} %add_add_fusion.1), channel_id=1, source_target_pairs={{0,5},{1,4},{2,7},{3,6},{4,0},{5,1},{6,2},{7,3},{8,13},{9,12},{10,... | collective-permute-start | bytes 110600 | tf_op jit(solution)/shard_map/ppermute | solution.py:57

commit v3 on v2

v3 whole, which is shorter than its diff:
```python
import functools
import math

import jax
import jax.numpy as jnp
from jax import lax
from jax.experimental import pallas as pl
from jax.experimental.pallas import tpu as pltpu
from jax.sharding import PartitionSpec as P


LOG2E = math.log2(math.e)
HIGHEST = lax.Precision.HIGHEST
AXES = ("blk", "rep")
RING = 4


def coords_of(index):
    rep, blk = index % 2, index // 2
    return blk // 16, (blk // 4) % 4, rep * 2 + (blk // 2) % 2, blk % 2


def index_of(z, x, y, core):
    return (((z * 4 + x) * 2 + y % 2) * 2 + core) * 2 + y // 2


def moved(move):
    return [(i, index_of(*move(*coords_of(i)))) for i in range(128)]


def core_swap():
    return moved(lambda z, x, y, c: (z, x, y, 1 - c))


def shift_y(step):
    return moved(lambda z, x, y, c: (z, x, (y + step) % RING, c))


def shift_z(step):
    return moved(lambda z, x, y, c: ((z + step) % RING, x, y, c))


def shift_x(step):
    return moved(lambda z, x, y, c: (z, (x + step) % RING, y, c))


def shift_by_core(step, core_of_z):
    def move(z, x, y, c):
        if c == core_of_z:
            return (z + step) % RING, x, y, c
        return z, (x + step) % RING, y, c

    return moved(move)


def send(value, perm):
    return lax.ppermute(value, AXES, perm)


def dot(left, right, dims, precision=None):
    return lax.dot_general(
        left, right, (dims, ((), ())), precision=precision, preferred_element_type=jnp.float32
    )


NN = ((1,), (0,))
NT = ((1,), (1,))
TN = ((0,), (0,))


CONV_STEP = 4


def conv_kernel(
    taps, half_ref, hyper_ref, tok_ref, len_ref, embed_ref, w_ref, bias_ref, inv_len_ref,
    probe_ref, prev_ref, coupling_ref, cols_ref, rows_ref, known_ref,
    high_ref, low_ref, onehot_ref, acc_ref,
):
    del half_ref
    vocab, channels = embed_ref.shape
    width = w_ref.shape[1]
    seq, samples = tok_ref.shape
    outputs = (seq - taps) // 2 + 1
    depth = high_ref.shape[0]
    lanes = 2 * vocab
    group_in = lax.broadcasted_iota(jnp.int32, (channels, channels), 0) // width
    group_out = lax.broadcasted_iota(jnp.int32, (channels, channels), 1) // width
    same = group_in == group_out
    embed = embed_ref[...]
    high_ref[taps * vocab :, :] = jnp.zeros((depth - taps * vocab, channels), jnp.bfloat16)
    low_ref[taps * vocab :, :] = jnp.zeros((depth - taps * vocab, channels), jnp.bfloat16)
    for k in range(taps):
        tiled = jnp.concatenate([w_ref[k].astype(jnp.float32)] * (channels // width), axis=0)
        dense = jnp.where(same, tiled, 0.0).astype(jnp.bfloat16)
        entry = dot(embed, dense, NN)
        if k == 0:
            entry = entry + bias_ref[...]
        high = entry.astype(jnp.bfloat16)
        high_ref[k * vocab : (k + 1) * vocab, :] = high
        low_ref[k * vocab : (k + 1) * vocab, :] = (
            entry - high.astype(jnp.float32)
        ).astype(jnp.bfloat16)

    known_ref[...] = hyper_ref[1] * probe_ref[...].astype(jnp.float32) - dot(
        coupling_ref[...], prev_ref[...].astype(jnp.float32), NN, HIGHEST
    )

    tokens = jnp.concatenate(
        [tok_ref[...], jnp.full((lanes - seq, samples), -1, jnp.int32)], axis=0
    ).astype(jnp.float32).T
    lane_id = lax.broadcasted_iota(jnp.int32, (samples, lanes), 1)
    left_half = lane_id < vocab
    vocab_id = jnp.where(left_half, lane_id, lane_id - vocab).astype(jnp.float32)
    for s in range(0, seq, 2):
        even = jnp.broadcast_to(tokens[:, s : s + 1], (samples, lanes))
        odd = jnp.broadcast_to(tokens[:, s + 1 : s + 2], (samples, lanes))
        hit = jnp.where(left_half, even, odd) == vocab_id
        onehot_ref[:, s * vocab : (s + 2) * vocab] = jnp.where(hit, 1.0, 0.0).astype(jnp.bfloat16)

    counts_row = (len_ref[...] - taps) // 2 + 1
    counts = jnp.broadcast_to(counts_row.astype(jnp.float32), (lanes, samples)).T
    counts = jnp.concatenate([counts] * (channels // lanes), axis=1)
    acc_ref[...] = jnp.zeros_like(acc_ref)
    root = math.sqrt(2.0 / math.pi)

    def positions(step, carry):
        base = step * CONV_STEP
        window = jnp.concatenate(
            [
                onehot_ref[:, pl.ds(pl.multiple_of((base + q) * lanes, lanes), depth)]
                for q in range(CONV_STEP)
            ],
            axis=0,
        )
        pre = dot(window, high_ref[...], NN) + dot(window, low_ref[...], NN)
        inner = pre * (root + (root * 0.044715) * (pre * pre))
        active = pre + pre * jnp.tanh(inner)
        total = acc_ref[...]
        for q in range(CONV_STEP):
            place = (base + q).astype(jnp.float32)
            part = active[q * samples : (q + 1) * samples, :]
            total = total + jnp.where(place < counts, part, 0.0)
        acc_ref[...] = total
        return carry

    lax.fori_loop(0, outputs // CONV_STEP, positions, 0)

    pooled = acc_ref[...] * (0.5 / counts)
    centered = pooled - jnp.mean(pooled, axis=1, keepdims=True)
    spread_sq = jnp.mean(centered * centered, axis=1, keepdims=True)
    normed = centered * lax.rsqrt(spread_sq + 1e-05)
    feat = (normed * inv_len_ref[...]).astype(jnp.bfloat16)
    cols_ref[:samples, :] = feat
    cols_ref[samples:, :] = probe_ref[...]
    rows_ref[...] = feat.astype(jnp.float32).T.astype(jnp.bfloat16)


def conv_features(
    hyper, tok_t, lengths, embed, conv_w, conv_b, inv_len, probes_t, prev_t, coupling, half
):
    seq, rows = tok_t.shape
    vocab, channels = embed.shape
    taps = conv_w.shape[0]
    samples = rows // 2
    width = probes_t.shape[0]
    depth = -(-taps * vocab // 128) * 128
    whole = lambda shape: pl.BlockSpec(shape, lambda i, h: (0,) * len(shape))
    part = lambda lead: pl.BlockSpec((lead, samples), lambda i, h: (0, h[0]))
    return pl.pallas_call(
        functools.partial(conv_kernel, taps),
        grid_spec=pltpu.PrefetchScalarGridSpec(
            num_scalar_prefetch=1,
            grid=(1,),
            in_specs=[
                pl.BlockSpec(memory_space=pltpu.SMEM),
                part(seq),
                part(1),
                whole((vocab, channels)),
                whole(conv_w.shape),
                whole((1, channels)),
                whole((1, channels)),
                part(width),
                whole((width, samples)),
                whole((width, width)),
            ],
            out_specs=[
                whole((samples + width, channels)),
                whole((channels, samples)),
                whole((width, samples)),
            ],
            scratch_shapes=[
                pltpu.VMEM((depth, channels), jnp.bfloat16),
                pltpu.VMEM((depth, channels), jnp.bfloat16),
                pltpu.VMEM((samples, (seq + 1) * vocab), jnp.bfloat16),
                pltpu.VMEM((samples, channels), jnp.float32),
            ],
        ),
        out_shape=[
            jax.ShapeDtypeStruct((samples + width, channels), jnp.bfloat16),
            jax.ShapeDtypeStruct((channels, samples), jnp.bfloat16),
            jax.ShapeDtypeStruct((width, samples), jnp.float32),
        ],
        name="conv_features",
    )(
        half, hyper, tok_t, lengths.reshape(1, rows), embed, conv_w,
        conv_b.reshape(1, channels), inv_len.reshape(1, channels), probes_t, prev_t, coupling,
    )


def apply_kernel(row_count, col_count, resume, last, hyper_ref, *refs):
    rows = refs[:row_count]
    cols = refs[row_count : row_count + col_count]
    rest = refs[row_count + col_count :]
    start_refs, rest = rest[:resume], rest[resume:]
    known_refs, out_refs, half_ref = rest[:last], rest[last:-1], rest[-1]
    totals = list(out_refs) if last else [out_refs[0].at[i] for i in range(row_count)]
    depth, _, _ = cols[0].shape
    samples = rows[0].shape[1]
    top = jnp.log2(jnp.full((1, 128), hyper_ref[0], jnp.float32))[:, :1]
    for i in range(row_count):
        total = start_refs[0][i] if resume else jnp.zeros(totals[i].shape, jnp.float32)
        totals[i][...] = total + known_refs[0][...] if last and i == 0 else total
        wide = rows[i][...].astype(jnp.float32)
        half_ref[i : i + 1, :] = (0.5 * LOG2E) * jnp.sum(wide * wide, axis=0, keepdims=True)
    for g in range(col_count):
        feat = jnp.concatenate([cols[g][d, :samples, :] for d in range(depth)], axis=0)
        probes = jnp.concatenate([cols[g][d, samples:, :] for d in range(depth)], axis=1)
        wide = feat.astype(jnp.float32)
        bias = (0.5 * LOG2E) * jnp.sum(wide * wide, axis=1, keepdims=True) - top
        bias = jnp.broadcast_to(bias, (depth * samples, samples))
        for i in range(row_count):
            inner = dot(feat, rows[i][...], NN)
            power = jnp.minimum(inner * LOG2E - bias - half_ref[i : i + 1, :], top)
            weights = jnp.exp2(power).astype(jnp.bfloat16)
            totals[i][...] += dot(probes, weights, NN)


def apply_rows(hyper, rows, cols, start=(), known=()):
    depth, tall, channels = cols[0].shape
    samples = rows[0].shape[1]
    width = tall - samples
    last = len(known)
    vmem = pl.BlockSpec(memory_space=pltpu.VMEM)
    pairs = len(cols) * depth * len(rows) * samples * samples
    shape = (len(rows), width, samples)
    return pl.pallas_call(
        functools.partial(apply_kernel, len(rows), len(cols), len(start), last),
        out_shape=[jax.ShapeDtypeStruct(shape[1:], jnp.float32)] * len(rows)
        if last
        else jax.ShapeDtypeStruct(shape, jnp.float32),
        in_specs=[pl.BlockSpec(memory_space=pltpu.SMEM)]
        + [vmem] * (len(rows) + len(cols) + len(start) + last),
        out_specs=[vmem] * len(rows) if last else vmem,
        scratch_shapes=[pltpu.VMEM((len(rows), samples), jnp.float32)],
        compiler_params=pltpu.CompilerParams(vmem_limit_bytes=24 << 20),
        cost_estimate=pl.CostEstimate(
            flops=2 * pairs * (channels + width), transcendentals=pairs, bytes_accessed=4 << 20
        ),
        name="apply_rows",
    )(hyper, *rows, *cols, *start, *known)


def gram_kernel(inv_root, own_ref, one_ref, two_ref, three_ref, col_ref, image_ref, packed_ref):
    size, samples = own_ref.shape
    image = ring_add([own_ref[...], one_ref[...], two_ref[...], three_ref[...]]) * inv_root
    image_ref[...] = image
    probes = col_ref[samples:, :]
    basis_sq = dot(probes, probes, NT) * (inv_root * inv_root)
    rest, projected = image, 0.0
    for _ in range(3):
        piece = rest.astype(jnp.bfloat16)
        rest = rest - piece.astype(jnp.float32)
        projected = projected + dot(probes, piece, NT)
    image_sq = dot(image, image, NT, HIGHEST)
    down = lax.broadcasted_iota(jnp.int32, (size, size), 0)
    across = lax.broadcasted_iota(jnp.int32, (size, size), 1)
    packed_ref[:size, :size] = projected * inv_root
    packed_ref[:size, size:] = jnp.where(across >= down, image_sq, basis_sq)
    diagonal = jnp.sum(jnp.where(across == down, basis_sq, 0.0), axis=0, keepdims=True)
    packed_ref[size:, :size] = jnp.broadcast_to(diagonal, (8, size))
    packed_ref[size:, size:] = jnp.zeros((8, size), jnp.float32)


def gram_stage(inv_root, parts, cols):
    size, samples = parts[0].shape
    vmem = pl.BlockSpec(memory_space=pltpu.VMEM)
    return pl.pallas_call(
        functools.partial(gram_kernel, inv_root),
        in_specs=[vmem] * (len(parts) + 1),
        out_specs=[vmem, vmem],
        out_shape=[
            jax.ShapeDtypeStruct((size, samples), jnp.float32),
            jax.ShapeDtypeStruct((size + 8, 2 * size), jnp.float32),
        ],
        name="gram_stage",
    )(*parts, cols)


PANEL = 4


def finish_kernel(
    inv_root, half_ref, own_ref, one_ref, two_ref, three_ref, image_ref, probe_ref,
    a_ref, r_ref, next_ref,
):
    size = image_ref.shape[0]
    packed = ring_add([own_ref[...], one_ref[...], two_ref[...], three_ref[...]])
    block_a = packed[:size, :size]
    mixed = packed[:size, size:]
    mixed_t = mixed.T
    diagonal = packed[size : size + 1, :size]
    down = lax.broadcasted_iota(jnp.int32, (size, size), 0)
    across = lax.broadcasted_iota(jnp.int32, (size, size), 1)
    image_sq = jnp.where(across >= down, mixed, mixed_t)
    square = jnp.where(across == down, diagonal, jnp.where(across < down, mixed, mixed_t))
    twice = 2.0 * block_a - dot(square, block_a, NN, HIGHEST)
    gram = image_sq - dot(block_a, twice, TN, HIGHEST)
    basis = probe_ref[...].astype(jnp.float32) * inv_root
    resid = image_ref[...] - dot(block_a, basis, TN, HIGHEST)

    unit = jnp.where(across == down, 1.0, 0.0)
    work = jnp.concatenate([gram, unit], axis=1)
    tiles = [work[8 * i : 8 * i + 8, :] for i in range(size // 8)]
    wide = (8, 2 * size)
    sub_id = lax.broadcasted_iota(jnp.int32, wide, 0)
    for j in range(0, size, PANEL):
        home, place = divmod(j, 8)
        rows = [
            jnp.broadcast_to(tiles[home][place + a : place + a + 1, :], wide)
            for a in range(PANEL)
        ]
        corner = [
            [jnp.broadcast_to(rows[a][:, j + b : j + b + 1], wide) if b >= a else None
             for b in range(PANEL)]
            for a in range(PANEL)
        ]
        scales = []
        for a in range(PANEL):
            scale = lax.rsqrt(corner[a][a])
            scales.append(scale)
            rows[a] = rows[a] * scale
            for b in range(a + 1, PANEL):
                corner[a][b] = corner[a][b] * scale
            for c in range(a + 1, PANEL):
                rows[c] = rows[c] - corner[a][c] * rows[a]
                for b in range(c, PANEL):
                    corner[c][b] = corner[c][b] - corner[a][c] * corner[a][b]
        for i in range(home, size // 8):
            if i == home and place + PANEL == 8:
                continue
            columns = []
            for b in range(PANEL):
                column = jnp.broadcast_to(tiles[i][:, j + b : j + b + 1], wide)
                for a in range(b):
                    column = column - columns[a] * corner[a][b]
                columns.append(column * scales[b])
            lowered = tiles[i]
            for b in range(PANEL):
                lowered = lowered - columns[b] * rows[b]
            if i == home:
                lowered = jnp.where(sub_id >= place + PANEL, lowered, tiles[i])
            tiles[i] = lowered
        for a in range(PANEL):
            tiles[home] = jnp.where(sub_id == place + a, rows[a], tiles[home])
    work = jnp.concatenate(tiles, axis=0)
    a_ref[...] = block_a
    r_ref[...] = jnp.where(across >= down, work[:, :size], 0.0)
    next_ref[...] = dot(work[:, size:], resid, NN, HIGHEST) * (1.0 / inv_root)


def finish(inv_root, packed, image, probes_t, half):
    size, samples = image.shape
    whole = lambda shape: pl.BlockSpec(shape, lambda i, h: (0,) * len(shape))
    return pl.pallas_call(
        functools.partial(finish_kernel, inv_root),
        grid_spec=pltpu.PrefetchScalarGridSpec(
            num_scalar_prefetch=1,
            grid=(1,),
            in_specs=[
                *[whole(part.shape) for part in packed],
                whole(image.shape),
                pl.BlockSpec((size, samples), lambda i, h: (0, h[0])),
            ],
            out_specs=[whole((size, size)), whole((size, size)), whole((size, samples))],
        ),
        out_shape=[
            jax.ShapeDtypeStruct((size, size), jnp.float32),
            jax.ShapeDtypeStruct((size, size), jnp.float32),
            jax.ShapeDtypeStruct((size, samples), jnp.float32),
        ],
        name="finish",
    )(half, *packed, image, probes_t)


def ring_parts(value, shift):
    return [value] + [send(value, shift(s)) for s in (1, 2, 3)]


def ring_add(parts):
    return (parts[0] + parts[2]) + (parts[1] + parts[3])


def lanczos_step(
    tokens, lengths, embed, conv_w, conv_b, inv_len, hyper, probes, prev_probes, coupling
):
    total_rows = tokens.shape[0] * lax.axis_size("blk")
    inv_root = 1.0 / math.sqrt(total_rows)
    half = lax.axis_index("rep").astype(jnp.int32).reshape(1)
    probes_t = probes.T
    cols, rows, known = conv_features(
        hyper, tokens.T, lengths, embed, conv_w, conv_b, inv_len, probes_t, prev_probes.T,
        coupling, half,
    )
    near = [send(cols, shift_by_core(s, 0)) for s in (1, 2, 3)]
    all_rows = [rows] + [send(rows, shift_y(s)) for s in (1, 2, 3)]
    group = jnp.stack([cols] + near)
    far = [send(group, shift_by_core(s, 1)) for s in (1, 3, 2)]
    swap = core_swap()

    def apply(blocks, start=(), known=()):
        return apply_rows(hyper, all_rows, blocks, start, known)

    partial = apply([group])
    partial = apply([send(group, swap)], [partial])
    partial = apply([far[0]], [partial])
    partial = apply([send(far[0], swap)], [partial])
    partial = apply([far[1]], [partial])
    partial = apply([send(far[1], swap)], [partial])
    partial = apply([far[2]], [partial])
    partial = apply([send(far[2], swap)], [partial], [known])
    parts = [partial[0]] + [send(partial[s], shift_y(-s)) for s in (1, 2, 3)]
    image, packed = gram_stage(inv_root, parts, cols)
    packed = packed + send(packed, core_swap())
    packed = ring_add(ring_parts(packed, shift_z))
    packed = ring_add(ring_parts(packed, shift_x))
    packed = ring_parts(packed, shift_y)
    block_a, upper, next_t = finish(inv_root, packed, image, probes_t, half)
    return (block_a, upper, next_t.T)


def solution(mesh):
    return jax.shard_map(
        lanczos_step,
        mesh=mesh,
        in_specs=(
            P("blk", None),
            P("blk"),
            P(),
            P(),
            P(),
            P(),
            P(),
            P("blk", None),
            P(("blk", "rep"), None),
            P(),
        ),
        out_specs=(P(), P(), P(("blk", "rep"), None)),
        check_vma=False,
    )
```

time: 123 us -> 121 us (0.984)
  starting transfers between devices: 44.5 us -> 35.9 us
  waiting for transfers between devices: 37.7 us -> 41.1 us
  Pallas kernels: 35.5 us -> 38 us
    ppermute x26, starting transfers between devices: 44.5 us -> 35.9 us  [send(): return lax.ppermute(value, AXES, perm)]
    ppermute x26, waiting for transfers between devices: 37.7 us -> 41.1 us  [send(): return lax.ppermute(value, AXES, perm)]
    pallas_call x4 -> x8, Pallas kernels: 16.9 us -> 19.8 us  [apply_rows(): pl.pallas_call(functools.partial(apply_kernel, len(rows), len(cols), len(...]
    unnamed x10 -> x22, local copies, waits for them, and re-layouts: 0.63 us -> 1.86 us
  transfers between devices with their start and end apart: 26 -> 26, of which waited for: 18 -> 17; matrix products, arithmetic and copies ran while one was open for 0% -> 0% of each run, Pallas kernels for 12% -> 14%
where the time goes in v3:
time: 121 us; the launch traced here: 120 us
  waiting for transfers between devices  41.1 us (34%)
  Pallas kernels  38 us (31%)
  starting transfers between devices  35.9 us (30%)
  local copies, waits for them, and re-layouts  1.86 us (2%)
  other arithmetic  1.83 us (2%)
    ppermute x26, waiting for transfers between devices, send(): return lax.ppermute(value, AXES, perm)  41.1 us
    ppermute x26, starting transfers between devices, send(): return lax.ppermute(value, AXES, perm)  35.9 us
    pallas_call x8, Pallas kernels, apply_rows(): pl.pallas_call(functools.partial(apply_kernel, len(rows), len(cols), len(...  19.8 us
    pallas_call x1, Pallas kernels, conv_features(): pl.pallas_call(functools.partial(conv_kernel, taps), grid_spec=pltpu.Pref...  11.2 us
    pallas_call x1, Pallas kernels, finish(): pl.pallas_call(functools.partial(finish_kernel, inv_root), grid_spec=pltp...  4.96 us
  transfers between devices with their start and end apart: 26, of which 17 were waited for; matrix products, arithmetic and copies ran while one was open for 0% of the time, Pallas kernels for 14%

profile of v3, /device:TPU:2, one launch (start us, length us, event | category | flops | bytes accessed | tf_op | source)
XLA Modules:
  0.0 119.5 jit_solution(501870250327110412)
XLA Ops:
  0.6 11.2 %conv_features.1 = (bf16[320,256]{1,0:T(8,128)(2,1)}, bf16[256,256]{1,0:T(8,128)(2,1)}, f32[64,256]{1,0:T(8,128)}) custom-call(s32[1]{0:T(128)} %bitcast.half_ref, f32[2]{0:T(128)} %hyper_ref.17, s32[69,512]{1,0:T(8,128)} %bitcast.18, s32[1,512]{1,0:T(1,128)} %bitcast.20, bf16[64,256]{1,0:T(8,128)(2,1)} %embed_ref.1, bf16[7,32,256]{2,1,0:T(8,128)(2,1)} %w_ref.1, ...), custom_call_target="tpu_custom_call" | custom-call | tf_op jit(solution)/shard_map/conv_features/pallas_call | solution.py:169
  11.8 4.0 %collective-permute-start.5 = (bf16[320,256]{1,0:T(8,128)(2,1)}, bf16[320,256]{1,0:T(8,128)(2,1)S(1)}, u32[]{:S(2)}, u32[]{:S(2)}) collective-permute-start(bf16[320,256]{1,0:T(8,128)(2,1)} %get-tuple-element.16.col_ref), channel_id=1, source_target_pairs={{0,96},{1,97},{2,26},{3,27},{4,100},{5,101},{6,30},{7,31},{8,104},... | collective-permute-start | bytes 491528 | tf_op jit(solution)/shard_map/ppermute | solution.py:57
  17.1 3.7 %collective-permute-done.5 = bf16[320,256]{1,0:T(8,128)(2,1)S(1)} collective-permute-done((bf16[320,256]{1,0:T(8,128)(2,1)}, bf16[320,256]{1,0:T(8,128)(2,1)S(1)}, u32[]{:S(2)}, u32[]{:S(2)}) %collective-permute-start.5) | collective-permute-done | bytes 163872 | tf_op jit(solution)/shard_map/ppermute | solution.py:57
  20.8 2.2 %collective-permute-done.4 = bf16[320,256]{1,0:T(8,128)(2,1)S(1)} collective-permute-done((bf16[320,256]{1,0:T(8,128)(2,1)}, bf16[320,256]{1,0:T(8,128)(2,1)S(1)}, u32[]{:S(2)}, u32[]{:S(2)}) %collective-permute-start.4) | collective-permute-done | bytes 163872 | tf_op jit(solution)/shard_map/ppermute | solution.py:57
  25.4 1.6 %collective-permute-start.10 = (bf16[4,320,256]{2,1,0:T(8,128)(2,1)S(1)}, bf16[4,320,256]{2,1,0:T(8,128)(2,1)S(1)}, u32[]{:S(2)}, u32[]{:S(2)}) collective-permute-start(bf16[4,320,256]{2,1,0:T(8,128)(2,1)S(1)} %pad_maximum_fusion.refs_4_), channel_id=1, source_target_pairs={{0,8},{1,9},{2,34},{3,35},{4,12},{5,13},{6,38},{7,39},{8,16},{9,17... | collective-permute-start | bytes 1966088 | tf_op jit(solution)/shard_map/ppermute | solution.py:57
  27.5 2.1 %collective-permute-start.6 = (bf16[4,320,256]{2,1,0:T(8,128)(2,1)S(1)}, bf16[4,320,256]{2,1,0:T(8,128)(2,1)S(1)}, u32[]{:S(2)}, u32[]{:S(2)}) collective-permute-start(bf16[4,320,256]{2,1,0:T(8,128)(2,1)S(1)} %pad_maximum_fusion.refs_4_), channel_id=1, source_target_pairs={{0,16},{1,17},{2,66},{3,67},{4,20},{5,21},{6,70},{7,71},{8,24},{9,... | collective-permute-start | bytes 1966088 | tf_op jit(solution)/shard_map/ppermute | solution.py:57
  29.6 6.4 %collective-permute-done.10.refs_4_ = bf16[4,320,256]{2,1,0:T(8,128)(2,1)S(1)} collective-permute-done((bf16[4,320,256]{2,1,0:T(8,128)(2,1)S(1)}, bf16[4,320,256]{2,1,0:T(8,128)(2,1)S(1)}, u32[]{:S(2)}, u32[]{:S(2)}) %collective-permute-start.10) | collective-permute-done | bytes 655392 | tf_op jit(solution)/shard_map/ppermute | solution.py:57
  36.1 3.0 %collective-permute-start.2 = (bf16[256,256]{1,0:T(8,128)(2,1)S(1)}, bf16[256,256]{1,0:T(8,128)(2,1)S(1)}, u32[]{:S(2)}, u32[]{:S(2)}) collective-permute-start(bf16[256,256]{1,0:T(8,128)(2,1)S(1)} %copy-done.2), channel_id=1, source_target_pairs={{0,5},{1,4},{2,7},{3,6},{4,0},{5,1},{6,2},{7,3},{8,13},{9,12},{10,... | collective-permute-start | bytes 393224 | tf_op jit(solution)/shard_map/ppermute | solution.py:57
  39.4 3.1 %collective-permute-done.2.refs_3_ = bf16[256,256]{1,0:T(8,128)(2,1)S(1)} collective-permute-done((bf16[256,256]{1,0:T(8,128)(2,1)S(1)}, bf16[256,256]{1,0:T(8,128)(2,1)S(1)}, u32[]{:S(2)}, u32[]{:S(2)}) %collective-permute-start.2) | collective-permute-done | bytes 131104 | tf_op jit(solution)/shard_map/ppermute | solution.py:57
  42.5 2.7 %collective-permute-start.1 = (bf16[256,256]{1,0:T(8,128)(2,1)S(1)}, bf16[256,256]{1,0:T(8,128)(2,1)S(1)}, u32[]{:S(2)}, u32[]{:S(2)}) collective-permute-start(bf16[256,256]{1,0:T(8,128)(2,1)S(1)} %copy-done.2), channel_id=1, source_target_pairs={{0,1},{1,0},{2,3},{3,2},{4,5},{5,4},{6,7},{7,6},{8,9},{9,8},{10,11... | collective-permute-start | bytes 393224 | tf_op jit(solution)/shard_map/ppermute | solution.py:57
  45.2 3.9 %collective-permute-done.1.refs_2_ = bf16[256,256]{1,0:T(8,128)(2,1)S(1)} collective-permute-done((bf16[256,256]{1,0:T(8,128)(2,1)S(1)}, bf16[256,256]{1,0:T(8,128)(2,1)S(1)}, u32[]{:S(2)}, u32[]{:S(2)}) %collective-permute-start.1) | collective-permute-done | bytes 131104 | tf_op jit(solution)/shard_map/ppermute | solution.py:57
  50.4 5.3 %collective-permute-done.refs_1_ = bf16[256,256]{1,0:T(8,128)(2,1)S(1)} collective-permute-done((bf16[256,256]{1,0:T(8,128)(2,1)S(1)}, bf16[256,256]{1,0:T(8,128)(2,1)S(1)}, u32[]{:S(2)}, u32[]{:S(2)}) %collective-permute-start) | collective-permute-done | bytes 131104 | tf_op jit(solution)/shard_map/ppermute | solution.py:57
  55.7 2.4 %apply_rows.8.refs_5_ = f32[4,64,256]{2,1,0:T(8,128)S(1)} custom-call(f32[2]{0:T(128)S(1)} %copy-done.1, bf16[256,256]{1,0:T(8,128)(2,1)S(1)} %copy-done.2, bf16[256,256]{1,0:T(8,128)(2,1)S(1)} %collective-permute-done.refs_1_, bf16[256,256]{1,0:T(8,128)(2,1)S(1)} %collective-permute-done.1.refs_2_, bf16[256,256]{1,0:T(8,128)(2,1)S(1)} %collective-permute-done.2.refs_3_, ...), custom_call_target="tpu_custom_call" | custom-call | flops 671088640 | bytes 4194304 | tf_op jit(solution)/shard_map/apply_rows/pallas_call | solution.py:246
  58.2 2.5 %apply_rows.9.refs_5_ = f32[4,64,256]{2,1,0:T(8,128)S(1)} custom-call(f32[2]{0:T(128)S(1)} %copy-done.1, bf16[256,256]{1,0:T(8,128)(2,1)S(1)} %copy-done.2, bf16[256,256]{1,0:T(8,128)(2,1)S(1)} %collective-permute-done.refs_1_, bf16[256,256]{1,0:T(8,128)(2,1)S(1)} %collective-permute-done.1.refs_2_, bf16[256,256]{1,0:T(8,128)(2,1)S(1)} %collective-permute-done.2.refs_3_, ...), custom_call_target="tpu_custom_call" | custom-call | flops 671088640 | bytes 4194304 | tf_op jit(solution)/shard_map/apply_rows/pallas_call | solution.py:246
  60.6 2.5 %apply_rows.10.refs_5_ = f32[4,64,256]{2,1,0:T(8,128)S(1)} custom-call(f32[2]{0:T(128)S(1)} %copy-done.1, bf16[256,256]{1,0:T(8,128)(2,1)S(1)} %copy-done.2, bf16[256,256]{1,0:T(8,128)(2,1)S(1)} %collective-permute-done.refs_1_, bf16[256,256]{1,0:T(8,128)(2,1)S(1)} %collective-permute-done.1.refs_2_, bf16[256,256]{1,0:T(8,128)(2,1)S(1)} %collective-permute-done.2.refs_3_, ...), custom_call_target="tpu_custom_call" | custom-call | flops 671088640 | bytes 4194304 | tf_op jit(solution)/shard_map/apply_rows/pallas_call | solution.py:246
  63.1 2.5 %apply_rows.11.refs_5_ = f32[4,64,256]{2,1,0:T(8,128)S(1)} custom-call(f32[2]{0:T(128)S(1)} %copy-done.1, bf16[256,256]{1,0:T(8,128)(2,1)S(1)} %copy-done.2, bf16[256,256]{1,0:T(8,128)(2,1)S(1)} %collective-permute-done.refs_1_, bf16[256,256]{1,0:T(8,128)(2,1)S(1)} %collective-permute-done.1.refs_2_, bf16[256,256]{1,0:T(8,128)(2,1)S(1)} %collective-permute-done.2.refs_3_, ...), custom_call_target="tpu_custom_call" | custom-call | flops 671088640 | bytes 4194304 | tf_op jit(solution)/shard_map/apply_rows/pallas_call | solution.py:246
  65.6 2.5 %apply_rows.12.refs_5_ = f32[4,64,256]{2,1,0:T(8,128)S(1)} custom-call(f32[2]{0:T(128)S(1)} %copy-done.1, bf16[256,256]{1,0:T(8,128)(2,1)S(1)} %copy-done.2, bf16[256,256]{1,0:T(8,128)(2,1)S(1)} %collective-permute-done.refs_1_, bf16[256,256]{1,0:T(8,128)(2,1)S(1)} %collective-permute-done.1.refs_2_, bf16[256,256]{1,0:T(8,128)(2,1)S(1)} %collective-permute-done.2.refs_3_, ...), custom_call_target="tpu_custom_call" | custom-call | flops 671088640 | bytes 4194304 | tf_op jit(solution)/shard_map/apply_rows/pallas_call | solution.py:246
  68.1 2.5 %apply_rows.13.refs_5_ = f32[4,64,256]{2,1,0:T(8,128)S(1)} custom-call(f32[2]{0:T(128)S(1)} %copy-done.1, bf16[256,256]{1,0:T(8,128)(2,1)S(1)} %copy-done.2, bf16[256,256]{1,0:T(8,128)(2,1)S(1)} %collective-permute-done.refs_1_, bf16[256,256]{1,0:T(8,128)(2,1)S(1)} %collective-permute-done.1.refs_2_, bf16[256,256]{1,0:T(8,128)(2,1)S(1)} %collective-permute-done.2.refs_3_, ...), custom_call_target="tpu_custom_call" | custom-call | flops 671088640 | bytes 4194304 | tf_op jit(solution)/shard_map/apply_rows/pallas_call | solution.py:246
  70.5 2.5 %apply_rows.14.refs_5_ = f32[4,64,256]{2,1,0:T(8,128)S(1)} custom-call(f32[2]{0:T(128)S(1)} %copy-done.1, bf16[256,256]{1,0:T(8,128)(2,1)S(1)} %copy-done.2, bf16[256,256]{1,0:T(8,128)(2,1)S(1)} %collective-permute-done.refs_1_, bf16[256,256]{1,0:T(8,128)(2,1)S(1)} %collective-permute-done.1.refs_2_, bf16[256,256]{1,0:T(8,128)(2,1)S(1)} %collective-permute-done.2.refs_3_, ...), custom_call_target="tpu_custom_call" | custom-call | flops 671088640 | bytes 4194304 | tf_op jit(solution)/shard_map/apply_rows/pallas_call | solution.py:246
  73.0 2.7 %apply_rows.15 = (f32[64,256]{1,0:T(8,128)S(1)}, f32[64,256]{1,0:T(8,128)S(1)}, f32[64,256]{1,0:T(8,128)S(1)}, f32[64,256]{1,0:T(8,128)S(1)}) custom-call(f32[2]{0:T(128)S(1)} %copy-done.1, bf16[256,256]{1,0:T(8,128)(2,1)S(1)} %copy-done.2, bf16[256,256]{1,0:T(8,128)(2,1)S(1)} %collective-permute-done.refs_1_, ...), custom_call_target="tpu_custom_call" | custom-call | flops 671088640 | bytes 4194304 | tf_op jit(solution)/shard_map/apply_rows/pallas_call | solution.py:246
  76.3 2.0 %collective-permute-start.13 = (f32[64,256]{1,0:T(8,128)S(1)}, f32[64,256]{1,0:T(8,128)S(1)}, u32[]{:S(2)}, u32[]{:S(2)}) collective-permute-start(f32[64,256]{1,0:T(8,128)S(1)} %get-tuple-element.19), channel_id=1, source_target_pairs={{0,5},{1,4},{2,7},{3,6},{4,0},{5,1},{6,2},{7,3},{8,13},{9,12},{10,... | collective-permute-start | bytes 196616 | tf_op jit(solution)/shard_map/ppermute | solution.py:57
  79.2 1.7 %collective-permute-done.13.one_ref = f32[64,256]{1,0:T(8,128)S(1)} collective-permute-done((f32[64,256]{1,0:T(8,128)S(1)}, f32[64,256]{1,0:T(8,128)S(1)}, u32[]{:S(2)}, u32[]{:S(2)}) %collective-permute-start.13) | collective-permute-done | bytes 65568 | tf_op jit(solution)/shard_map/ppermute | solution.py:57
  80.9 3.3 %collective-permute-done.14.two_ref = f32[64,256]{1,0:T(8,128)S(1)} collective-permute-done((f32[64,256]{1,0:T(8,128)S(1)}, f32[64,256]{1,0:T(8,128)S(1)}, u32[]{:S(2)}, u32[]{:S(2)}) %collective-permute-start.14) | collective-permute-done | bytes 65568 | tf_op jit(solution)/shard_map/ppermute | solution.py:57
  85.1 2.0 %gram_stage.1 = (f32[64,256]{1,0:T(8,128)}, f32[72,128]{1,0:T(8,128)}) custom-call(f32[64,256]{1,0:T(8,128)} %copy-done, f32[64,256]{1,0:T(8,128)} %copy-done.5, f32[64,256]{1,0:T(8,128)} %copy-done.6, f32[64,256]{1,0:T(8,128)} %copy-done.7, bf16[320,256]{1,0:T(8,128)(2,1)} %get-tuple-element.16.col_ref), custom_call_target="tpu_custom_call" | custom-call | tf_op jit(solution)/shard_map/gram_stage/pallas_call | solution.py:287
  90.2 1.6 %collective-permute-start.18 = (f32[72,128]{1,0:T(8,128)S(1)}, f32[72,128]{1,0:T(8,128)S(1)}, u32[]{:S(2)}, u32[]{:S(2)}) collective-permute-start(f32[72,128]{1,0:T(8,128)S(1)} %add.21), channel_id=1, source_target_pairs={{0,32},{1,33},{2,34},{3,35},{4,36},{5,37},{6,38},{7,39},{8,40},{9,... | collective-permute-start | bytes 110600 | tf_op jit(solution)/shard_map/ppermute | solution.py:57
  91.9 4.5 %collective-permute-start.17 = (f32[72,128]{1,0:T(8,128)S(1)}, f32[72,128]{1,0:T(8,128)S(1)}, u32[]{:S(2)}, u32[]{:S(2)}) collective-permute-start(f32[72,128]{1,0:T(8,128)S(1)} %add.21), channel_id=1, source_target_pairs={{0,64},{1,65},{2,66},{3,67},{4,68},{5,69},{6,70},{7,71},{8,72},{9,... | collective-permute-start | bytes 110600 | tf_op jit(solution)/shard_map/ppermute | solution.py:57
  96.8 1.9 %collective-permute-done.17 = f32[72,128]{1,0:T(8,128)S(1)} collective-permute-done((f32[72,128]{1,0:T(8,128)S(1)}, f32[72,128]{1,0:T(8,128)S(1)}, u32[]{:S(2)}, u32[]{:S(2)}) %collective-permute-start.17) | collective-permute-done | bytes 36896 | tf_op jit(solution)/shard_map/ppermute | solution.py:57
  98.7 2.5 %collective-permute-start.22 = (f32[72,128]{1,0:T(8,128)S(1)}, f32[72,128]{1,0:T(8,128)S(1)}, u32[]{:S(2)}, u32[]{:S(2)}) collective-permute-start(f32[72,128]{1,0:T(8,128)S(1)} %add_add_fusion.1), channel_id=1, source_target_pairs={{0,24},{1,25},{2,26},{3,27},{4,28},{5,29},{6,30},{7,31},{8,0},{9,1... | collective-permute-start | bytes 110600 | tf_op jit(solution)/shard_map/ppermute | solution.py:57
  101.2 3.9 %collective-permute-start.20 = (f32[72,128]{1,0:T(8,128)S(1)}, f32[72,128]{1,0:T(8,128)S(1)}, u32[]{:S(2)}, u32[]{:S(2)}) collective-permute-start(f32[72,128]{1,0:T(8,128)S(1)} %add_add_fusion.1), channel_id=1, source_target_pairs={{0,16},{1,17},{2,18},{3,19},{4,20},{5,21},{6,22},{7,23},{8,24},{9,... | collective-permute-start | bytes 110600 | tf_op jit(solution)/shard_map/ppermute | solution.py:57
  105.1 1.9 %collective-permute-done.20 = f32[72,128]{1,0:T(8,128)S(1)} collective-permute-done((f32[72,128]{1,0:T(8,128)S(1)}, f32[72,128]{1,0:T(8,128)S(1)}, u32[]{:S(2)}, u32[]{:S(2)}) %collective-permute-start.20) | collective-permute-done | bytes 36896 | tf_op jit(solution)/shard_map/ppermute | solution.py:57
  111.1 2.2 %collective-permute-done.24.two_ref = f32[72,128]{1,0:T(8,128)S(1)} collective-permute-done((f32[72,128]{1,0:T(8,128)S(1)}, f32[72,128]{1,0:T(8,128)S(1)}, u32[]{:S(2)}, u32[]{:S(2)}) %collective-permute-start.24) | collective-permute-done | bytes 36896 | tf_op jit(solution)/shard_map/ppermute | solution.py:57
  114.6 5.0 %finish.1 = (f32[64,64]{1,0:T(8,128)}, f32[64,64]{1,0:T(8,128)}, f32[64,256]{1,0:T(8,128)}) custom-call(s32[1]{0:T(128)} %bitcast.half_ref, f32[72,128]{1,0:T(8,128)} %copy-done.4, f32[72,128]{1,0:T(8,128)} %copy-done.10, f32[72,128]{1,0:T(8,128)} %copy-done.9, f32[72,128]{1,0:T(8,128)} %copy-done.8, f32[64,256]{1,0:T(8,128)} %get-tuple-element.23.image_ref, ...), custom_call_target="tpu_custom_call" | custom-call | tf_op jit(solution)/shard_map/finish/pallas_call | solution.py:374
  (57 shorter events, 17.2 us)
Async XLA Ops:
  11.8 9.0 %collective-permute-start.5 = (bf16[320,256]{1,0:T(8,128)(2,1)}, bf16[320,256]{1,0:T(8,128)(2,1)S(1)}, u32[]{:S(2)}, u32[]{:S(2)}) collective-permute-start(bf16[320,256]{1,0:T(8,128)(2,1)} %get-tuple-element.16.col_ref), channel_id=1, source_target_pairs={{0,96},{1,97},{2,26},{3,27},{4,100},{5,101},{6,30},{7,31},{8,104},... | collective-permute-start | bytes 491528 | tf_op jit(solution)/shard_map/ppermute | solution.py:57
  15.9 7.1 %collective-permute-start.4 = (bf16[320,256]{1,0:T(8,128)(2,1)}, bf16[320,256]{1,0:T(8,128)(2,1)S(1)}, u32[]{:S(2)}, u32[]{:S(2)}) collective-permute-start(bf16[320,256]{1,0:T(8,128)(2,1)} %get-tuple-element.16.col_ref), channel_id=1, source_target_pairs={{0,64},{1,65},{2,18},{3,19},{4,68},{5,69},{6,22},{7,23},{8,72},{9,... | collective-permute-start | bytes 491528 | tf_op jit(solution)/shard_map/ppermute | solution.py:57
  15.9 8.5 %collective-permute-start.3 = (bf16[320,256]{1,0:T(8,128)(2,1)}, bf16[320,256]{1,0:T(8,128)(2,1)S(1)}, u32[]{:S(2)}, u32[]{:S(2)}) collective-permute-start(bf16[320,256]{1,0:T(8,128)(2,1)} %get-tuple-element.16.col_ref), channel_id=1, source_target_pairs={{0,32},{1,33},{2,10},{3,11},{4,36},{5,37},{6,14},{7,15},{8,40},{9,... | collective-permute-start | bytes 491528 | tf_op jit(solution)/shard_map/ppermute | solution.py:57
  24.4 11.7 %copy-start.2 = (bf16[256,256]{1,0:T(8,128)(2,1)S(1)}, bf16[256,256]{1,0:T(8,128)(2,1)}, u32[]{:S(2)}) copy-start(bf16[256,256]{1,0:T(8,128)(2,1)} %get-tuple-element.15.refs_0_) | copy-start | bytes 393220
  25.4 30.3 %copy-start.1 = (f32[2]{0:T(128)S(1)}, f32[2]{0:T(128)}, u32[]{:S(2)}) copy-start(f32[2]{0:T(128)} %hyper_ref.17) | copy-start | bytes 28
  25.4 10.7 %collective-permute-start.10 = (bf16[4,320,256]{2,1,0:T(8,128)(2,1)S(1)}, bf16[4,320,256]{2,1,0:T(8,128)(2,1)S(1)}, u32[]{:S(2)}, u32[]{:S(2)}) collective-permute-start(bf16[4,320,256]{2,1,0:T(8,128)(2,1)S(1)} %pad_maximum_fusion.refs_4_), channel_id=1, source_target_pairs={{0,8},{1,9},{2,34},{3,35},{4,12},{5,13},{6,38},{7,39},{8,16},{9,17... | collective-permute-start | bytes 1966088 | tf_op jit(solution)/shard_map/ppermute | solution.py:57
  27.0 12.1 %collective-permute-start.8 = (bf16[4,320,256]{2,1,0:T(8,128)(2,1)S(1)}, bf16[4,320,256]{2,1,0:T(8,128)(2,1)S(1)}, u32[]{:S(2)}, u32[]{:S(2)}) collective-permute-start(bf16[4,320,256]{2,1,0:T(8,128)(2,1)S(1)} %pad_maximum_fusion.refs_4_), channel_id=1, source_target_pairs={{0,24},{1,25},{2,98},{3,99},{4,28},{5,29},{6,102},{7,103},{8,0},{9... | collective-permute-start | bytes 1966088 | tf_op jit(solution)/shard_map/ppermute | solution.py:57
  27.5 17.7 %collective-permute-start.6 = (bf16[4,320,256]{2,1,0:T(8,128)(2,1)S(1)}, bf16[4,320,256]{2,1,0:T(8,128)(2,1)S(1)}, u32[]{:S(2)}, u32[]{:S(2)}) collective-permute-start(bf16[4,320,256]{2,1,0:T(8,128)(2,1)S(1)} %pad_maximum_fusion.refs_4_), channel_id=1, source_target_pairs={{0,16},{1,17},{2,66},{3,67},{4,20},{5,21},{6,70},{7,71},{8,24},{9,... | collective-permute-start | bytes 1966088 | tf_op jit(solution)/shard_map/ppermute | solution.py:57
  29.6 28.5 %collective-permute-start.12 = (bf16[4,320,256]{2,1,0:T(8,128)(2,1)S(1)}, bf16[4,320,256]{2,1,0:T(8,128)(2,1)S(1)}, u32[]{:S(2)}, u32[]{:S(2)}) collective-permute-start(bf16[4,320,256]{2,1,0:T(8,128)(2,1)S(1)} %pad_maximum_fusion.refs_4_), channel_id=1, source_target_pairs={{0,2},{1,3},{2,0},{3,1},{4,6},{5,7},{6,4},{7,5},{8,10},{9,11},{10,... | collective-permute-start | bytes 1966088 | tf_op jit(solution)/shard_map/ppermute | solution.py:57
  36.1 27.0 %collective-permute-start.11 = (bf16[4,320,256]{2,1,0:T(8,128)(2,1)S(1)}, bf16[4,320,256]{2,1,0:T(8,128)(2,1)S(1)}, u32[]{:S(2)}, u32[]{:S(2)}) collective-permute-start(bf16[4,320,256]{2,1,0:T(8,128)(2,1)S(1)} %collective-permute-done.10.refs_4_), channel_id=1, source_target_pairs={{0,2},{1,3},{2,0},{3,1},{4,6},{5,7},{6,4},{7,5},{8,10},{9,11},{10,... | collective-permute-start | bytes 1966088 | tf_op jit(solution)/shard_map/ppermute | solution.py:57
  36.1 6.4 %collective-permute-start.2 = (bf16[256,256]{1,0:T(8,128)(2,1)S(1)}, bf16[256,256]{1,0:T(8,128)(2,1)S(1)}, u32[]{:S(2)}, u32[]{:S(2)}) collective-permute-start(bf16[256,256]{1,0:T(8,128)(2,1)S(1)} %copy-done.2), channel_id=1, source_target_pairs={{0,5},{1,4},{2,7},{3,6},{4,0},{5,1},{6,2},{7,3},{8,13},{9,12},{10,... | collective-permute-start | bytes 393224 | tf_op jit(solution)/shard_map/ppermute | solution.py:57
  39.1 28.9 %collective-permute-start.9 = (bf16[4,320,256]{2,1,0:T(8,128)(2,1)S(1)}, bf16[4,320,256]{2,1,0:T(8,128)(2,1)S(1)}, u32[]{:S(2)}, u32[]{:S(2)}) collective-permute-start(bf16[4,320,256]{2,1,0:T(8,128)(2,1)S(1)} %collective-permute-done.8.refs_4_), channel_id=1, source_target_pairs={{0,2},{1,3},{2,0},{3,1},{4,6},{5,7},{6,4},{7,5},{8,10},{9,11},{10,... | collective-permute-start | bytes 1966088 | tf_op jit(solution)/shard_map/ppermute | solution.py:57
  42.5 6.6 %collective-permute-start.1 = (bf16[256,256]{1,0:T(8,128)(2,1)S(1)}, bf16[256,256]{1,0:T(8,128)(2,1)S(1)}, u32[]{:S(2)}, u32[]{:S(2)}) collective-permute-start(bf16[256,256]{1,0:T(8,128)(2,1)S(1)} %copy-done.2), channel_id=1, source_target_pairs={{0,1},{1,0},{2,3},{3,2},{4,5},{5,4},{6,7},{7,6},{8,9},{9,8},{10,11... | collective-permute-start | bytes 393224 | tf_op jit(solution)/shard_map/ppermute | solution.py:57
  45.2 27.8 %collective-permute-start.7 = (bf16[4,320,256]{2,1,0:T(8,128)(2,1)S(1)}, bf16[4,320,256]{2,1,0:T(8,128)(2,1)S(1)}, u32[]{:S(2)}, u32[]{:S(2)}) collective-permute-start(bf16[4,320,256]{2,1,0:T(8,128)(2,1)S(1)} %collective-permute-done.6.refs_4_), channel_id=1, source_target_pairs={{0,2},{1,3},{2,0},{3,1},{4,6},{5,7},{6,4},{7,5},{8,10},{9,11},{10,... | collective-permute-start | bytes 1966088 | tf_op jit(solution)/shard_map/ppermute | solution.py:57
  49.1 6.6 %collective-permute-start = (bf16[256,256]{1,0:T(8,128)(2,1)S(1)}, bf16[256,256]{1,0:T(8,128)(2,1)S(1)}, u32[]{:S(2)}, u32[]{:S(2)}) collective-permute-start(bf16[256,256]{1,0:T(8,128)(2,1)S(1)} %copy-done.2), channel_id=1, source_target_pairs={{0,4},{1,5},{2,6},{3,7},{4,1},{5,0},{6,3},{7,2},{8,12},{9,13},{10,... | collective-permute-start | bytes 393224 | tf_op jit(solution)/shard_map/ppermute | solution.py:57
  70.5 2.5 %copy-start.3 = (f32[64,256]{1,0:T(8,128)S(1)}, f32[64,256]{1,0:T(8,128)}, u32[]{:S(2)}) copy-start(f32[64,256]{1,0:T(8,128)} %get-tuple-element.17.refs_6_) | copy-start | bytes 196612
  76.3 4.5 %collective-permute-start.13 = (f32[64,256]{1,0:T(8,128)S(1)}, f32[64,256]{1,0:T(8,128)S(1)}, u32[]{:S(2)}, u32[]{:S(2)}) collective-permute-start(f32[64,256]{1,0:T(8,128)S(1)} %get-tuple-element.19), channel_id=1, source_target_pairs={{0,5},{1,4},{2,7},{3,6},{4,0},{5,1},{6,2},{7,3},{8,13},{9,12},{10,... | collective-permute-start | bytes 196616 | tf_op jit(solution)/shard_map/ppermute | solution.py:57
  78.3 5.9 %collective-permute-start.14 = (f32[64,256]{1,0:T(8,128)S(1)}, f32[64,256]{1,0:T(8,128)S(1)}, u32[]{:S(2)}, u32[]{:S(2)}) collective-permute-start(f32[64,256]{1,0:T(8,128)S(1)} %get-tuple-element.20), channel_id=1, source_target_pairs={{0,1},{1,0},{2,3},{3,2},{4,5},{5,4},{6,7},{7,6},{8,9},{9,8},{10,11... | collective-permute-start | bytes 196616 | tf_op jit(solution)/shard_map/ppermute | solution.py:57
  78.3 6.2 %collective-permute-start.15 = (f32[64,256]{1,0:T(8,128)S(1)}, f32[64,256]{1,0:T(8,128)S(1)}, u32[]{:S(2)}, u32[]{:S(2)}) collective-permute-start(f32[64,256]{1,0:T(8,128)S(1)} %get-tuple-element.21), channel_id=1, source_target_pairs={{0,4},{1,5},{2,6},{3,7},{4,1},{5,0},{6,3},{7,2},{8,12},{9,13},{10,... | collective-permute-start | bytes 196616 | tf_op jit(solution)/shard_map/ppermute | solution.py:57
  80.9 3.7 %copy-start.5 = (f32[64,256]{1,0:T(8,128)}, f32[64,256]{1,0:T(8,128)S(1)}, u32[]{:S(2)}) copy-start(f32[64,256]{1,0:T(8,128)S(1)} %collective-permute-done.13.one_ref) | copy-start | bytes 196612
  87.1 1.4 %collective-permute-start.16 = (f32[72,128]{1,0:T(8,128)}, f32[72,128]{1,0:T(8,128)S(1)}, u32[]{:S(2)}, u32[]{:S(2)}) collective-permute-start(f32[72,128]{1,0:T(8,128)} %get-tuple-element.22), channel_id=1, source_target_pairs={{0,2},{1,3},{2,0},{3,1},{4,6},{5,7},{6,4},{7,5},{8,10},{9,11},{10,... | collective-permute-start | bytes 110600 | tf_op jit(solution)/shard_map/ppermute | solution.py:57
  89.3 7.0 %collective-permute-start.19 = (f32[72,128]{1,0:T(8,128)S(1)}, f32[72,128]{1,0:T(8,128)S(1)}, u32[]{:S(2)}, u32[]{:S(2)}) collective-permute-start(f32[72,128]{1,0:T(8,128)S(1)} %add.21), channel_id=1, source_target_pairs={{0,96},{1,97},{2,98},{3,99},{4,100},{5,101},{6,102},{7,103},{8,104... | collective-permute-start | bytes 110600 | tf_op jit(solution)/shard_map/ppermute | solution.py:57
  90.2 6.6 %collective-permute-start.18 = (f32[72,128]{1,0:T(8,128)S(1)}, f32[72,128]{1,0:T(8,128)S(1)}, u32[]{:S(2)}, u32[]{:S(2)}) collective-permute-start(f32[72,128]{1,0:T(8,128)S(1)} %add.21), channel_id=1, source_target_pairs={{0,32},{1,33},{2,34},{3,35},{4,36},{5,37},{6,38},{7,39},{8,40},{9,... | collective-permute-start | bytes 110600 | tf_op jit(solution)/shard_map/ppermute | solution.py:57
  91.9 6.8 %collective-permute-start.17 = (f32[72,128]{1,0:T(8,128)S(1)}, f32[72,128]{1,0:T(8,128)S(1)}, u32[]{:S(2)}, u32[]{:S(2)}) collective-permute-start(f32[72,128]{1,0:T(8,128)S(1)} %add.21), channel_id=1, source_target_pairs={{0,64},{1,65},{2,66},{3,67},{4,68},{5,69},{6,70},{7,71},{8,72},{9,... | collective-permute-start | bytes 110600 | tf_op jit(solution)/shard_map/ppermute | solution.py:57
  98.7 6.4 %collective-permute-start.22 = (f32[72,128]{1,0:T(8,128)S(1)}, f32[72,128]{1,0:T(8,128)S(1)}, u32[]{:S(2)}, u32[]{:S(2)}) collective-permute-start(f32[72,128]{1,0:T(8,128)S(1)} %add_add_fusion.1), channel_id=1, source_target_pairs={{0,24},{1,25},{2,26},{3,27},{4,28},{5,29},{6,30},{7,31},{8,0},{9,1... | collective-permute-start | bytes 110600 | tf_op jit(solution)/shard_map/ppermute | solution.py:57
  101.2 4.0 %collective-permute-start.21 = (f32[72,128]{1,0:T(8,128)S(1)}, f32[72,128]{1,0:T(8,128)S(1)}, u32[]{:S(2)}, u32[]{:S(2)}) collective-permute-start(f32[72,128]{1,0:T(8,128)S(1)} %add_add_fusion.1), channel_id=1, source_target_pairs={{0,8},{1,9},{2,10},{3,11},{4,12},{5,13},{6,14},{7,15},{8,16},{9,17... | collective-permute-start | bytes 110600 | tf_op jit(solution)/shard_map/ppermute | solution.py:57
  101.2 5.8 %collective-permute-start.20 = (f32[72,128]{1,0:T(8,128)S(1)}, f32[72,128]{1,0:T(8,128)S(1)}, u32[]{:S(2)}, u32[]{:S(2)}) collective-permute-start(f32[72,128]{1,0:T(8,128)S(1)} %add_add_fusion.1), channel_id=1, source_target_pairs={{0,16},{1,17},{2,18},{3,19},{4,20},{5,21},{6,22},{7,23},{8,24},{9,... | collective-permute-start | bytes 110600 | tf_op jit(solution)/shard_map/ppermute | solution.py:57
  107.0 6.9 %copy-start.4 = (f32[72,128]{1,0:T(8,128)}, f32[72,128]{1,0:T(8,128)S(1)}, u32[]{:S(2)}) copy-start(f32[72,128]{1,0:T(8,128)S(1)} %add_add_fusion.own_ref) | copy-start | bytes 110596
  107.1 4.0 %collective-permute-start.25 = (f32[72,128]{1,0:T(8,128)S(1)}, f32[72,128]{1,0:T(8,128)S(1)}, u32[]{:S(2)}, u32[]{:S(2)}) collective-permute-start(f32[72,128]{1,0:T(8,128)S(1)} %add_add_fusion.own_ref), channel_id=1, source_target_pairs={{0,5},{1,4},{2,7},{3,6},{4,0},{5,1},{6,2},{7,3},{8,13},{9,12},{10,... | collective-permute-start | bytes 110600 | tf_op jit(solution)/shard_map/ppermute | solution.py:57
  107.9 5.5 %collective-permute-start.24 = (f32[72,128]{1,0:T(8,128)S(1)}, f32[72,128]{1,0:T(8,128)S(1)}, u32[]{:S(2)}, u32[]{:S(2)}) collective-permute-start(f32[72,128]{1,0:T(8,128)S(1)} %add_add_fusion.own_ref), channel_id=1, source_target_pairs={{0,1},{1,0},{2,3},{3,2},{4,5},{5,4},{6,7},{7,6},{8,9},{9,8},{10,11... | collective-permute-start | bytes 110600 | tf_op jit(solution)/shard_map/ppermute | solution.py:57
  108.8 5.2 %collective-permute-start.23 = (f32[72,128]{1,0:T(8,128)S(1)}, f32[72,128]{1,0:T(8,128)S(1)}, u32[]{:S(2)}, u32[]{:S(2)}) collective-permute-start(f32[72,128]{1,0:T(8,128)S(1)} %add_add_fusion.own_ref), channel_id=1, source_target_pairs={{0,4},{1,5},{2,6},{3,7},{4,1},{5,0},{6,3},{7,2},{8,12},{9,13},{10,... | collective-permute-start | bytes 110600 | tf_op jit(solution)/shard_map/ppermute | solution.py:57
  111.1 2.9 %copy-start.8 = (f32[72,128]{1,0:T(8,128)}, f32[72,128]{1,0:T(8,128)S(1)}, u32[]{:S(2)}) copy-start(f32[72,128]{1,0:T(8,128)S(1)} %collective-permute-done.25.three_ref) | copy-start | bytes 110596
  (5 other events, 3.1 us)

commit v4 on v3

--- a/solution.py
+++ b/solution.py
@@ -69,26 +69,29 @@
 
 
 CONV_STEP = 4
+ONEHOT_TYPE = jnp.bfloat16
 
 
 def conv_kernel(
     taps, half_ref, hyper_ref, tok_ref, len_ref, embed_ref, w_ref, bias_ref, inv_len_ref,
     probe_ref, prev_ref, coupling_ref, cols_ref, rows_ref, known_ref,
-    high_ref, low_ref, onehot_ref, acc_ref,
+    table_ref, onehot_ref, acc_ref,
 ):
     del half_ref
     vocab, channels = embed_ref.shape
     width = w_ref.shape[1]
     seq, samples = tok_ref.shape
     outputs = (seq - taps) // 2 + 1
-    depth = high_ref.shape[0]
+    depth = table_ref.shape[0] // 2
     lanes = 2 * vocab
     group_in = lax.broadcasted_iota(jnp.int32, (channels, channels), 0) // width
     group_out = lax.broadcasted_iota(jnp.int32, (channels, channels), 1) // width
     same = group_in == group_out
     embed = embed_ref[...]
-    high_ref[taps * vocab :, :] = jnp.zeros((depth - taps * vocab, channels), jnp.bfloat16)
-    low_ref[taps * vocab :, :] = jnp.zeros((depth - taps * vocab, channels), jnp.bfloat16)
+    for base in (0, depth):
+        table_ref[base + taps * vocab : base + depth, :] = jnp.zeros(
+            (depth - taps * vocab, channels), jnp.bfloat16
+        )
     for k in range(taps):
         tiled = jnp.concatenate([w_ref[k].astype(jnp.float32)] * (channels // width), axis=0)
         dense = jnp.where(same, tiled, 0.0).astype(jnp.bfloat16)
@@ -96,26 +99,25 @@
         if k == 0:
             entry = entry + bias_ref[...]
         high = entry.astype(jnp.bfloat16)
-        high_ref[k * vocab : (k + 1) * vocab, :] = high
-        low_ref[k * vocab : (k + 1) * vocab, :] = (
-            entry - high.astype(jnp.float32)
-        ).astype(jnp.bfloat16)
+        low = (entry - high.astype(jnp.float32)).astype(jnp.bfloat16)
+        table_ref[k * vocab : (k + 1) * vocab, :] = high
+        table_ref[depth + k * vocab : depth + (k + 1) * vocab, :] = low
 
     known_ref[...] = hyper_ref[1] * probe_ref[...].astype(jnp.float32) - dot(
         coupling_ref[...], prev_ref[...].astype(jnp.float32), NN, HIGHEST
     )
 
-    tokens = jnp.concatenate(
-        [tok_ref[...], jnp.full((lanes - seq, samples), -1, jnp.int32)], axis=0
-    ).astype(jnp.float32).T
-    lane_id = lax.broadcasted_iota(jnp.int32, (samples, lanes), 1)
-    left_half = lane_id < vocab
-    vocab_id = jnp.where(left_half, lane_id, lane_id - vocab).astype(jnp.float32)
+    vocab_id = lax.broadcasted_iota(jnp.int32, (vocab, samples), 0)
+
+    def hits(s):
+        if s >= seq:
+            return jnp.zeros((vocab, samples), ONEHOT_TYPE)
+        hit = jnp.broadcast_to(tok_ref[s : s + 1, :], (vocab, samples)) == vocab_id
+        return jnp.where(hit, 1.0, 0.0).astype(ONEHOT_TYPE)
+
     for s in range(0, seq, 2):
-        even = jnp.broadcast_to(tokens[:, s : s + 1], (samples, lanes))
-        odd = jnp.broadcast_to(tokens[:, s + 1 : s + 2], (samples, lanes))
-        hit = jnp.where(left_half, even, odd) == vocab_id
-        onehot_ref[:, s * vocab : (s + 2) * vocab] = jnp.where(hit, 1.0, 0.0).astype(jnp.bfloat16)
+        pair = jnp.concatenate([hits(s), hits(s + 1)], axis=0)
+        onehot_ref[:, s * vocab : (s + 2) * vocab] = pair.T.astype(jnp.bfloat16)
 
     counts_row = (len_ref[...] - taps) // 2 + 1
     counts = jnp.broadcast_to(counts_row.astype(jnp.float32), (lanes, samples)).T
@@ -132,7 +134,7 @@
             ],
             axis=0,
         )
-        pre = dot(window, high_ref[...], NN) + dot(window, low_ref[...], NN)
+        pre = dot(jnp.concatenate([window, window], axis=1), table_ref[...], NN)
         inner = pre * (root + (root * 0.044715) * (pre * pre))
         active = pre + pre * jnp.tanh(inner)
         total = acc_ref[...]
@@ -189,8 +191,7 @@
                 whole((width, samples)),
             ],
             scratch_shapes=[
-                pltpu.VMEM((depth, channels), jnp.bfloat16),
-                pltpu.VMEM((depth, channels), jnp.bfloat16),
+                pltpu.VMEM((2 * depth, channels), jnp.bfloat16),
                 pltpu.VMEM((samples, (seq + 1) * vocab), jnp.bfloat16),
                 pltpu.VMEM((samples, channels), jnp.float32),
             ],
@@ -207,19 +208,18 @@
     )
 
 
-def apply_kernel(row_count, col_count, resume, last, hyper_ref, *refs):
-    rows = refs[:row_count]
-    cols = refs[row_count : row_count + col_count]
-    rest = refs[row_count + col_count :]
-    start_refs, rest = rest[:resume], rest[resume:]
-    known_refs, out_refs, half_ref = rest[:last], rest[last:-1], rest[-1]
-    totals = list(out_refs) if last else [out_refs[0].at[i] for i in range(row_count)]
+def apply_kernel(row_count, col_count, resume, known_count, hyper_ref, *refs):
+    rows, refs = refs[:row_count], refs[row_count:]
+    cols, refs = refs[:col_count], refs[col_count:]
+    starts, refs = refs[: row_count * resume], refs[row_count * resume :]
+    known_refs, refs = refs[:known_count], refs[known_count:]
+    totals, half_ref = refs[:row_count], refs[row_count]
     depth, _, _ = cols[0].shape
     samples = rows[0].shape[1]
     top = jnp.log2(jnp.full((1, 128), hyper_ref[0], jnp.float32))[:, :1]
     for i in range(row_count):
-        total = start_refs[0][i] if resume else jnp.zeros(totals[i].shape, jnp.float32)
-        totals[i][...] = total + known_refs[0][...] if last and i == 0 else total
+        total = starts[i][...] if resume else jnp.zeros(totals[i].shape, jnp.float32)
+        totals[i][...] = total + known_refs[0][...] if known_count and i == 0 else total
         wide = rows[i][...].astype(jnp.float32)
         half_ref[i : i + 1, :] = (0.5 * LOG2E) * jnp.sum(wide * wide, axis=0, keepdims=True)
     for g in range(col_count):
@@ -235,29 +235,25 @@
             totals[i][...] += dot(probes, weights, NN)
 
 
-def apply_rows(hyper, rows, cols, start=(), known=()):
+def apply_rows(hyper, rows, cols, starts=(), known=()):
     depth, tall, channels = cols[0].shape
     samples = rows[0].shape[1]
     width = tall - samples
-    last = len(known)
     vmem = pl.BlockSpec(memory_space=pltpu.VMEM)
     pairs = len(cols) * depth * len(rows) * samples * samples
-    shape = (len(rows), width, samples)
     return pl.pallas_call(
-        functools.partial(apply_kernel, len(rows), len(cols), len(start), last),
-        out_shape=[jax.ShapeDtypeStruct(shape[1:], jnp.float32)] * len(rows)
-        if last
-        else jax.ShapeDtypeStruct(shape, jnp.float32),
+        functools.partial(apply_kernel, len(rows), len(cols), 1 if starts else 0, len(known)),
+        out_shape=[jax.ShapeDtypeStruct((width, samples), jnp.float32)] * len(rows),
         in_specs=[pl.BlockSpec(memory_space=pltpu.SMEM)]
-        + [vmem] * (len(rows) + len(cols) + len(start) + last),
-        out_specs=[vmem] * len(rows) if last else vmem,
-        scratch_shapes=[pltpu.VMEM((len(rows), samples), jnp.float32)],
+        + [vmem] * (len(rows) + len(cols) + len(starts) + len(known)),
+        out_specs=[vmem] * len(rows),
+        scratch_shapes=[pltpu.VMEM((8, samples), jnp.float32)],
         compiler_params=pltpu.CompilerParams(vmem_limit_bytes=24 << 20),
         cost_estimate=pl.CostEstimate(
             flops=2 * pairs * (channels + width), transcendentals=pairs, bytes_accessed=4 << 20
         ),
         name="apply_rows",
-    )(hyper, *rows, *cols, *start, *known)
+    )(hyper, *rows, *cols, *starts, *known)
 
 
 def gram_kernel(inv_root, own_ref, one_ref, two_ref, three_ref, col_ref, image_ref, packed_ref):
@@ -296,7 +292,7 @@
     )(*parts, cols)
 
 
-PANEL = 4
+PANEL = 8
 
 
 def finish_kernel(
@@ -414,21 +410,29 @@
     near = [send(cols, shift_by_core(s, 0)) for s in (1, 2, 3)]
     all_rows = [rows] + [send(rows, shift_y(s)) for s in (1, 2, 3)]
     group = jnp.stack([cols] + near)
-    far = [send(group, shift_by_core(s, 1)) for s in (1, 3, 2)]
+    far = [send(group, shift_by_core(s, 1)) for s in (1, 3)]
+    far.append(send(far[0], shift_by_core(1, 1)))
     swap = core_swap()
 
-    def apply(blocks, start=(), known=()):
-        return apply_rows(hyper, all_rows, blocks, start, known)
-
-    partial = apply([group])
-    partial = apply([send(group, swap)], [partial])
-    partial = apply([far[0]], [partial])
-    partial = apply([send(far[0], swap)], [partial])
-    partial = apply([far[1]], [partial])
-    partial = apply([send(far[1], swap)], [partial])
-    partial = apply([far[2]], [partial])
-    partial = apply([send(far[2], swap)], [partial], [known])
-    parts = [partial[0]] + [send(partial[s], shift_y(-s)) for s in (1, 2, 3)]
+    def apply(at, blocks, starts=(), known=()):
+        return apply_rows(hyper, all_rows[at], blocks, starts, known)
+
+    own, others = slice(0, 1), slice(1, RING)
+    sums = apply(slice(0, RING), [group, send(group, swap)])
+    own_sum, sums = sums[:1], sums[1:]
+    plus, minus, opposite = far
+    sums = apply(others, [plus], sums)
+    plus_swapped = send(plus, swap)
+    sums = apply(others, [plus_swapped, minus], sums)
+    minus_swapped = send(minus, swap)
+    sums = apply(others, [minus_swapped], sums)
+    own_sum = apply(own, [plus, plus_swapped], own_sum)
+    sums = apply(others, [opposite], sums)
+    opposite_swapped = send(opposite, swap)
+    sums = apply(others, [opposite_swapped], sums)
+    parts = [send(sums[s - 1], shift_y(-s)) for s in (1, 2, 3)]
+    late = [minus, minus_swapped, opposite, opposite_swapped]
+    parts = list(apply(own, late, own_sum, [known])) + parts
     image, packed = gram_stage(inv_root, parts, cols)
     packed = packed + send(packed, core_swap())
     packed = ring_add(ring_parts(packed, shift_z))

time: 121 us -> 119 us (0.983)
  waiting for transfers between devices: 41.1 us -> 45.2 us
  Pallas kernels: 38 us -> 34.3 us
  starting transfers between devices: 35.9 us -> 32.9 us
    ppermute x26, waiting for transfers between devices: 41.1 us -> 45.2 us  [send(): return lax.ppermute(value, AXES, perm)]
    ppermute x26, starting transfers between devices: 35.9 us -> 32.9 us  [send(): return lax.ppermute(value, AXES, perm)]
    pallas_call x1, Pallas kernels: 11.2 us -> 9.46 us  [conv_features(): pl.pallas_call(functools.partial(conv_kernel, taps), grid_spec=pltpu.Pref...]
  transfers between devices with their start and end apart: 26 -> 26, of which waited for: 17 -> 16; matrix products, arithmetic and copies ran while one was open for 0% -> 0% of each run, Pallas kernels for 14% -> 14%
where the time goes in v4:
time: 119 us; the launch traced here: 117 us
  waiting for transfers between devices  45.2 us (38%)
  Pallas kernels  34.3 us (29%)
  starting transfers between devices  32.9 us (28%)
  local copies, waits for them, and re-layouts  1.91 us (2%)
  other arithmetic  1.83 us (2%)
    ppermute x26, waiting for transfers between devices, send(): return lax.ppermute(value, AXES, perm)  45.2 us
    ppermute x26, starting transfers between devices, send(): return lax.ppermute(value, AXES, perm)  32.9 us
    pallas_call x8, Pallas kernels, apply_rows(): pl.pallas_call(functools.partial(apply_kernel, len(rows), len(cols), 1 if...  18.7 us
    pallas_call x1, Pallas kernels, conv_features(): pl.pallas_call(functools.partial(conv_kernel, taps), grid_spec=pltpu.Pref...  9.46 us
    pallas_call x1, Pallas kernels, finish(): pl.pallas_call(functools.partial(finish_kernel, inv_root), grid_spec=pltp...  4.19 us
  transfers between devices with their start and end apart: 26, of which 16 were waited for; matrix products, arithmetic and copies ran while one was open for 0% of the time, Pallas kernels for 14%

profile of v4, /device:TPU:2, one launch (start us, length us, event | category | flops | bytes accessed | tf_op | source)
XLA Modules:
  0.0 117.0 jit_solution(18420664296501790613)
XLA Ops:
  0.6 9.5 %conv_features.1 = (bf16[320,256]{1,0:T(8,128)(2,1)}, bf16[256,256]{1,0:T(8,128)(2,1)}, f32[64,256]{1,0:T(8,128)}) custom-call(s32[1]{0:T(128)} %bitcast.half_ref, f32[2]{0:T(128)} %hyper_ref.17, s32[69,512]{1,0:T(8,128)} %bitcast.18, s32[1,512]{1,0:T(1,128)} %bitcast.20, bf16[64,256]{1,0:T(8,128)(2,1)} %embed_ref.1, bf16[7,32,256]{2,1,0:T(8,128)(2,1)} %w_ref.1, ...), custom_call_target="tpu_custom_call" | custom-call | tf_op jit(solution)/shard_map/conv_features/pallas_call | solution.py:171
  10.1 4.0 %collective-permute-start.2 = (bf16[320,256]{1,0:T(8,128)(2,1)}, bf16[320,256]{1,0:T(8,128)(2,1)S(1)}, u32[]{:S(2)}, u32[]{:S(2)}) collective-permute-start(bf16[320,256]{1,0:T(8,128)(2,1)} %get-tuple-element.31.col_ref), channel_id=1, source_target_pairs={{0,96},{1,97},{2,26},{3,27},{4,100},{5,101},{6,30},{7,31},{8,104},... | collective-permute-start | bytes 491528 | tf_op jit(solution)/shard_map/ppermute | solution.py:57
  15.4 3.7 %collective-permute-done.2 = bf16[320,256]{1,0:T(8,128)(2,1)S(1)} collective-permute-done((bf16[320,256]{1,0:T(8,128)(2,1)}, bf16[320,256]{1,0:T(8,128)(2,1)S(1)}, u32[]{:S(2)}, u32[]{:S(2)}) %collective-permute-start.2) | collective-permute-done | bytes 163872 | tf_op jit(solution)/shard_map/ppermute | solution.py:57
  19.1 2.2 %collective-permute-done.1 = bf16[320,256]{1,0:T(8,128)(2,1)S(1)} collective-permute-done((bf16[320,256]{1,0:T(8,128)(2,1)}, bf16[320,256]{1,0:T(8,128)(2,1)S(1)}, u32[]{:S(2)}, u32[]{:S(2)}) %collective-permute-start.1) | collective-permute-done | bytes 163872 | tf_op jit(solution)/shard_map/ppermute | solution.py:57
  23.7 1.6 %collective-permute-start.5 = (bf16[4,320,256]{2,1,0:T(8,128)(2,1)S(1)}, bf16[4,320,256]{2,1,0:T(8,128)(2,1)S(1)}, u32[]{:S(2)}, u32[]{:S(2)}) collective-permute-start(bf16[4,320,256]{2,1,0:T(8,128)(2,1)S(1)} %pad_maximum_fusion.refs_4_), channel_id=1, source_target_pairs={{0,8},{1,9},{2,34},{3,35},{4,12},{5,13},{6,38},{7,39},{8,16},{9,17... | collective-permute-start | bytes 1966088 | tf_op jit(solution)/shard_map/ppermute | solution.py:57
  25.8 8.6 %collective-permute-done.5.refs_1_.refs_3_ = bf16[4,320,256]{2,1,0:T(8,128)(2,1)S(1)} collective-permute-done((bf16[4,320,256]{2,1,0:T(8,128)(2,1)S(1)}, bf16[4,320,256]{2,1,0:T(8,128)(2,1)S(1)}, u32[]{:S(2)}, u32[]{:S(2)}) %collective-permute-start.5) | collective-permute-done | bytes 655392 | tf_op jit(solution)/shard_map/ppermute | solution.py:57
  34.3 1.5 %collective-permute-start.6 = (bf16[4,320,256]{2,1,0:T(8,128)(2,1)S(1)}, bf16[4,320,256]{2,1,0:T(8,128)(2,1)S(1)}, u32[]{:S(2)}, u32[]{:S(2)}) collective-permute-start(bf16[4,320,256]{2,1,0:T(8,128)(2,1)S(1)} %collective-permute-done.5.refs_1_.refs_3_), channel_id=1, source_target_pairs={{0,8},{1,9},{2,34},{3,35},{4,12},{5,13},{6,38},{7,39},{8,16},{9,17... | collective-permute-start | bytes 1966088 | tf_op jit(solution)/shard_map/ppermute | solution.py:57
  36.3 3.0 %collective-permute-start.11 = (bf16[256,256]{1,0:T(8,128)(2,1)S(1)}, bf16[256,256]{1,0:T(8,128)(2,1)S(1)}, u32[]{:S(2)}, u32[]{:S(2)}) collective-permute-start(bf16[256,256]{1,0:T(8,128)(2,1)S(1)} %copy-done), channel_id=1, source_target_pairs={{0,5},{1,4},{2,7},{3,6},{4,0},{5,1},{6,2},{7,3},{8,13},{9,12},{10,... | collective-permute-start | bytes 393224 | tf_op jit(solution)/shard_map/ppermute | solution.py:57
  39.4 5.6 %collective-permute-done.6.refs_3_ = bf16[4,320,256]{2,1,0:T(8,128)(2,1)S(1)} collective-permute-done((bf16[4,320,256]{2,1,0:T(8,128)(2,1)S(1)}, bf16[4,320,256]{2,1,0:T(8,128)(2,1)S(1)}, u32[]{:S(2)}, u32[]{:S(2)}) %collective-permute-start.6) | collective-permute-done | bytes 655392 | tf_op jit(solution)/shard_map/ppermute | solution.py:57
  44.9 3.2 %collective-permute-start.10 = (bf16[256,256]{1,0:T(8,128)(2,1)S(1)}, bf16[256,256]{1,0:T(8,128)(2,1)S(1)}, u32[]{:S(2)}, u32[]{:S(2)}) collective-permute-start(bf16[256,256]{1,0:T(8,128)(2,1)S(1)} %copy-done), channel_id=1, source_target_pairs={{0,1},{1,0},{2,3},{3,2},{4,5},{5,4},{6,7},{7,6},{8,9},{9,8},{10,11... | collective-permute-start | bytes 393224 | tf_op jit(solution)/shard_map/ppermute | solution.py:57
  48.1 4.2 %collective-permute-done.10.refs_2_.refs_1_ = bf16[256,256]{1,0:T(8,128)(2,1)S(1)} collective-permute-done((bf16[256,256]{1,0:T(8,128)(2,1)S(1)}, bf16[256,256]{1,0:T(8,128)(2,1)S(1)}, u32[]{:S(2)}, u32[]{:S(2)}) %collective-permute-start.10) | collective-permute-done | bytes 131104 | tf_op jit(solution)/shard_map/ppermute | solution.py:57
  52.4 1.6 %collective-permute-start.9 = (bf16[256,256]{1,0:T(8,128)(2,1)S(1)}, bf16[256,256]{1,0:T(8,128)(2,1)S(1)}, u32[]{:S(2)}, u32[]{:S(2)}) collective-permute-start(bf16[256,256]{1,0:T(8,128)(2,1)S(1)} %copy-done), channel_id=1, source_target_pairs={{0,4},{1,5},{2,6},{3,7},{4,1},{5,0},{6,3},{7,2},{8,12},{9,13},{10,... | collective-permute-start | bytes 393224 | tf_op jit(solution)/shard_map/ppermute | solution.py:57
  53.9 4.7 %collective-permute-done.9.refs_1_.refs_0_ = bf16[256,256]{1,0:T(8,128)(2,1)S(1)} collective-permute-done((bf16[256,256]{1,0:T(8,128)(2,1)S(1)}, bf16[256,256]{1,0:T(8,128)(2,1)S(1)}, u32[]{:S(2)}, u32[]{:S(2)}) %collective-permute-start.9) | collective-permute-done | bytes 131104 | tf_op jit(solution)/shard_map/ppermute | solution.py:57
  58.7 4.2 %apply_rows.8 = (f32[64,256]{1,0:T(8,128)S(1)}, f32[64,256]{1,0:T(8,128)S(1)}, f32[64,256]{1,0:T(8,128)S(1)}, f32[64,256]{1,0:T(8,128)S(1)}) custom-call(f32[2]{0:T(128)S(1)} %copy-done.3, bf16[256,256]{1,0:T(8,128)(2,1)S(1)} %copy-done, bf16[256,256]{1,0:T(8,128)(2,1)S(1)} %collective-permute-done.9.refs_1_.refs_0_, ...), custom_call_target="tpu_custom_call" | custom-call | flops 1342177280 | bytes 4194304 | tf_op jit(solution)/shard_map/apply_rows/pallas_call | solution.py:244
  62.9 2.0 %apply_rows.11 = (f32[64,256]{1,0:T(8,128)S(1)}, f32[64,256]{1,0:T(8,128)S(1)}, f32[64,256]{1,0:T(8,128)S(1)}) custom-call(f32[2]{0:T(128)S(1)} %copy-done.3, bf16[256,256]{1,0:T(8,128)(2,1)S(1)} %collective-permute-done.9.refs_1_.refs_0_, bf16[256,256]{1,0:T(8,128)(2,1)S(1)} %collective-permute-done.10.refs_2_.refs_1_, ...), custom_call_target="tpu_custom_call" | custom-call | flops 503316480 | bytes 4194304 | tf_op jit(solution)/shard_map/apply_rows/pallas_call | solution.py:244
  64.9 2.9 %apply_rows.12 = (f32[64,256]{1,0:T(8,128)S(1)}, f32[64,256]{1,0:T(8,128)S(1)}, f32[64,256]{1,0:T(8,128)S(1)}) custom-call(f32[2]{0:T(128)S(1)} %copy-done.3, bf16[256,256]{1,0:T(8,128)(2,1)S(1)} %collective-permute-done.9.refs_1_.refs_0_, bf16[256,256]{1,0:T(8,128)(2,1)S(1)} %collective-permute-done.10.refs_2_.refs_1_, ...), custom_call_target="tpu_custom_call" | custom-call | flops 1006632960 | bytes 4194304 | tf_op jit(solution)/shard_map/apply_rows/pallas_call | solution.py:244
  67.9 2.0 %apply_rows.13 = (f32[64,256]{1,0:T(8,128)S(1)}, f32[64,256]{1,0:T(8,128)S(1)}, f32[64,256]{1,0:T(8,128)S(1)}) custom-call(f32[2]{0:T(128)S(1)} %copy-done.3, bf16[256,256]{1,0:T(8,128)(2,1)S(1)} %collective-permute-done.9.refs_1_.refs_0_, bf16[256,256]{1,0:T(8,128)(2,1)S(1)} %collective-permute-done.10.refs_2_.refs_1_, ...), custom_call_target="tpu_custom_call" | custom-call | flops 503316480 | bytes 4194304 | tf_op jit(solution)/shard_map/apply_rows/pallas_call | solution.py:244
  69.8 2.0 %apply_rows.14 = (f32[64,256]{1,0:T(8,128)S(1)}, f32[64,256]{1,0:T(8,128)S(1)}, f32[64,256]{1,0:T(8,128)S(1)}) custom-call(f32[2]{0:T(128)S(1)} %copy-done.3, bf16[256,256]{1,0:T(8,128)(2,1)S(1)} %collective-permute-done.9.refs_1_.refs_0_, bf16[256,256]{1,0:T(8,128)(2,1)S(1)} %collective-permute-done.10.refs_2_.refs_1_, ...), custom_call_target="tpu_custom_call" | custom-call | flops 503316480 | bytes 4194304 | tf_op jit(solution)/shard_map/apply_rows/pallas_call | solution.py:244
  71.9 2.0 %apply_rows.15 = (f32[64,256]{1,0:T(8,128)S(1)}, f32[64,256]{1,0:T(8,128)S(1)}, f32[64,256]{1,0:T(8,128)S(1)}) custom-call(f32[2]{0:T(128)S(1)} %copy-done.3, bf16[256,256]{1,0:T(8,128)(2,1)S(1)} %collective-permute-done.9.refs_1_.refs_0_, bf16[256,256]{1,0:T(8,128)(2,1)S(1)} %collective-permute-done.10.refs_2_.refs_1_, ...), custom_call_target="tpu_custom_call" | custom-call | flops 503316480 | bytes 4194304 | tf_op jit(solution)/shard_map/apply_rows/pallas_call | solution.py:244
  73.8 1.8 %collective-permute-start.13 = (f32[64,256]{1,0:T(8,128)S(1)}, f32[64,256]{1,0:T(8,128)S(1)}, u32[]{:S(2)}, u32[]{:S(2)}) collective-permute-start(f32[64,256]{1,0:T(8,128)S(1)} %get-tuple-element.49), channel_id=1, source_target_pairs={{0,5},{1,4},{2,7},{3,6},{4,0},{5,1},{6,2},{7,3},{8,13},{9,12},{10,... | collective-permute-start | bytes 196616 | tf_op jit(solution)/shard_map/ppermute | solution.py:57
  77.3 1.4 %apply_rows.9.refs_5_ = f32[64,256]{1,0:T(8,128)S(1)} custom-call(f32[2]{0:T(128)S(1)} %copy-done.3, bf16[256,256]{1,0:T(8,128)(2,1)S(1)} %copy-done, bf16[4,320,256]{2,1,0:T(8,128)(2,1)S(1)} %collective-permute-done.5.refs_1_.refs_3_, bf16[4,320,256]{2,1,0:T(8,128)(2,1)S(1)} %collective-permute-done.8.refs_2_.refs_3_, f32[64,256]{1,0:T(8,128)S(1)} %get-tuple-element.32.refs_3_), custom_call_target="tpu_custom_call" | custom-call | flops 335544320 | bytes 4194304 | tf_op jit(solution)/shard_map/apply_rows/pallas_call | solution.py:244
  78.7 2.2 %apply_rows.10.own_ref = f32[64,256]{1,0:T(8,128)S(1)} custom-call(f32[2]{0:T(128)S(1)} %copy-done.3, bf16[256,256]{1,0:T(8,128)(2,1)S(1)} %copy-done, bf16[4,320,256]{2,1,0:T(8,128)(2,1)S(1)} %collective-permute-done.3.refs_1_.refs_4_, bf16[4,320,256]{2,1,0:T(8,128)(2,1)S(1)} %collective-permute-done.4.refs_2_.refs_3_, ...), custom_call_target="tpu_custom_call" | custom-call | flops 671088640 | bytes 4194304 | tf_op jit(solution)/shard_map/apply_rows/pallas_call | solution.py:244
  82.8 2.0 %gram_stage.1 = (f32[64,256]{1,0:T(8,128)}, f32[72,128]{1,0:T(8,128)}) custom-call(f32[64,256]{1,0:T(8,128)} %copy-done.1, f32[64,256]{1,0:T(8,128)} %copy-done.5, f32[64,256]{1,0:T(8,128)} %copy-done.6, f32[64,256]{1,0:T(8,128)} %copy-done.7, bf16[320,256]{1,0:T(8,128)(2,1)} %get-tuple-element.31.col_ref), custom_call_target="tpu_custom_call" | custom-call | tf_op jit(solution)/shard_map/gram_stage/pallas_call | solution.py:283
  90.9 2.5 %collective-permute-done.18 = f32[72,128]{1,0:T(8,128)S(1)} collective-permute-done((f32[72,128]{1,0:T(8,128)S(1)}, f32[72,128]{1,0:T(8,128)S(1)}, u32[]{:S(2)}, u32[]{:S(2)}) %collective-permute-start.18) | collective-permute-done | bytes 36896 | tf_op jit(solution)/shard_map/ppermute | solution.py:57
  94.5 3.0 %collective-permute-start.22 = (f32[72,128]{1,0:T(8,128)S(1)}, f32[72,128]{1,0:T(8,128)S(1)}, u32[]{:S(2)}, u32[]{:S(2)}) collective-permute-start(f32[72,128]{1,0:T(8,128)S(1)} %add_add_fusion.1), channel_id=1, source_target_pairs={{0,24},{1,25},{2,26},{3,27},{4,28},{5,29},{6,30},{7,31},{8,0},{9,1... | collective-permute-start | bytes 110600 | tf_op jit(solution)/shard_map/ppermute | solution.py:57
  97.5 2.4 %collective-permute-start.20 = (f32[72,128]{1,0:T(8,128)S(1)}, f32[72,128]{1,0:T(8,128)S(1)}, u32[]{:S(2)}, u32[]{:S(2)}) collective-permute-start(f32[72,128]{1,0:T(8,128)S(1)} %add_add_fusion.1), channel_id=1, source_target_pairs={{0,16},{1,17},{2,18},{3,19},{4,20},{5,21},{6,22},{7,23},{8,24},{9,... | collective-permute-start | bytes 110600 | tf_op jit(solution)/shard_map/ppermute | solution.py:57
  99.9 1.5 %collective-permute-done.21 = f32[72,128]{1,0:T(8,128)S(1)} collective-permute-done((f32[72,128]{1,0:T(8,128)S(1)}, f32[72,128]{1,0:T(8,128)S(1)}, u32[]{:S(2)}, u32[]{:S(2)}) %collective-permute-start.21) | collective-permute-done | bytes 36896 | tf_op jit(solution)/shard_map/ppermute | solution.py:57
  101.5 1.5 %collective-permute-done.20 = f32[72,128]{1,0:T(8,128)S(1)} collective-permute-done((f32[72,128]{1,0:T(8,128)S(1)}, f32[72,128]{1,0:T(8,128)S(1)}, u32[]{:S(2)}, u32[]{:S(2)}) %collective-permute-start.20) | collective-permute-done | bytes 36896 | tf_op jit(solution)/shard_map/ppermute | solution.py:57
  103.0 2.3 %collective-permute-start.25 = (f32[72,128]{1,0:T(8,128)S(1)}, f32[72,128]{1,0:T(8,128)S(1)}, u32[]{:S(2)}, u32[]{:S(2)}) collective-permute-start(f32[72,128]{1,0:T(8,128)S(1)} %add_add_fusion.own_ref), channel_id=1, source_target_pairs={{0,5},{1,4},{2,7},{3,6},{4,0},{5,1},{6,2},{7,3},{8,13},{9,12},{10,... | collective-permute-start | bytes 110600 | tf_op jit(solution)/shard_map/ppermute | solution.py:57
  105.3 1.7 %collective-permute-start.24 = (f32[72,128]{1,0:T(8,128)S(1)}, f32[72,128]{1,0:T(8,128)S(1)}, u32[]{:S(2)}, u32[]{:S(2)}) collective-permute-start(f32[72,128]{1,0:T(8,128)S(1)} %add_add_fusion.own_ref), channel_id=1, source_target_pairs={{0,1},{1,0},{2,3},{3,2},{4,5},{5,4},{6,7},{7,6},{8,9},{9,8},{10,11... | collective-permute-start | bytes 110600 | tf_op jit(solution)/shard_map/ppermute | solution.py:57
  107.3 3.5 %collective-permute-done.24.two_ref = f32[72,128]{1,0:T(8,128)S(1)} collective-permute-done((f32[72,128]{1,0:T(8,128)S(1)}, f32[72,128]{1,0:T(8,128)S(1)}, u32[]{:S(2)}, u32[]{:S(2)}) %collective-permute-start.24) | collective-permute-done | bytes 36896 | tf_op jit(solution)/shard_map/ppermute | solution.py:57
  112.8 4.2 %finish.1 = (f32[64,64]{1,0:T(8,128)}, f32[64,64]{1,0:T(8,128)}, f32[64,256]{1,0:T(8,128)}) custom-call(s32[1]{0:T(128)} %bitcast.half_ref, f32[72,128]{1,0:T(8,128)} %copy-done.4, f32[72,128]{1,0:T(8,128)} %copy-done.10, f32[72,128]{1,0:T(8,128)} %copy-done.9, f32[72,128]{1,0:T(8,128)} %copy-done.8, f32[64,256]{1,0:T(8,128)} %get-tuple-element.53.image_ref, ...), custom_call_target="tpu_custom_call" | custom-call | tf_op jit(solution)/shard_map/finish/pallas_call | solution.py:370
  (57 shorter events, 17.7 us)
Async XLA Ops:
  10.1 9.0 %collective-permute-start.2 = (bf16[320,256]{1,0:T(8,128)(2,1)}, bf16[320,256]{1,0:T(8,128)(2,1)S(1)}, u32[]{:S(2)}, u32[]{:S(2)}) collective-permute-start(bf16[320,256]{1,0:T(8,128)(2,1)} %get-tuple-element.31.col_ref), channel_id=1, source_target_pairs={{0,96},{1,97},{2,26},{3,27},{4,100},{5,101},{6,30},{7,31},{8,104},... | collective-permute-start | bytes 491528 | tf_op jit(solution)/shard_map/ppermute | solution.py:57
  14.1 7.1 %collective-permute-start.1 = (bf16[320,256]{1,0:T(8,128)(2,1)}, bf16[320,256]{1,0:T(8,128)(2,1)S(1)}, u32[]{:S(2)}, u32[]{:S(2)}) collective-permute-start(bf16[320,256]{1,0:T(8,128)(2,1)} %get-tuple-element.31.col_ref), channel_id=1, source_target_pairs={{0,64},{1,65},{2,18},{3,19},{4,68},{5,69},{6,22},{7,23},{8,72},{9,... | collective-permute-start | bytes 491528 | tf_op jit(solution)/shard_map/ppermute | solution.py:57
  14.1 8.5 %collective-permute-start = (bf16[320,256]{1,0:T(8,128)(2,1)}, bf16[320,256]{1,0:T(8,128)(2,1)S(1)}, u32[]{:S(2)}, u32[]{:S(2)}) collective-permute-start(bf16[320,256]{1,0:T(8,128)(2,1)} %get-tuple-element.31.col_ref), channel_id=1, source_target_pairs={{0,32},{1,33},{2,10},{3,11},{4,36},{5,37},{6,14},{7,15},{8,40},{9,... | collective-permute-start | bytes 491528 | tf_op jit(solution)/shard_map/ppermute | solution.py:57
  22.6 13.7 %copy-start = (bf16[256,256]{1,0:T(8,128)(2,1)S(1)}, bf16[256,256]{1,0:T(8,128)(2,1)}, u32[]{:S(2)}) copy-start(bf16[256,256]{1,0:T(8,128)(2,1)} %get-tuple-element.30.refs_0_) | copy-start | bytes 393220
  23.7 35.0 %copy-start.3 = (f32[2]{0:T(128)S(1)}, f32[2]{0:T(128)}, u32[]{:S(2)}) copy-start(f32[2]{0:T(128)} %hyper_ref.17) | copy-start | bytes 28
  23.7 10.7 %collective-permute-start.5 = (bf16[4,320,256]{2,1,0:T(8,128)(2,1)S(1)}, bf16[4,320,256]{2,1,0:T(8,128)(2,1)S(1)}, u32[]{:S(2)}, u32[]{:S(2)}) collective-permute-start(bf16[4,320,256]{2,1,0:T(8,128)(2,1)S(1)} %pad_maximum_fusion.refs_4_), channel_id=1, source_target_pairs={{0,8},{1,9},{2,34},{3,35},{4,12},{5,13},{6,38},{7,39},{8,16},{9,17... | collective-permute-start | bytes 1966088 | tf_op jit(solution)/shard_map/ppermute | solution.py:57
  25.2 14.1 %collective-permute-start.3 = (bf16[4,320,256]{2,1,0:T(8,128)(2,1)S(1)}, bf16[4,320,256]{2,1,0:T(8,128)(2,1)S(1)}, u32[]{:S(2)}, u32[]{:S(2)}) collective-permute-start(bf16[4,320,256]{2,1,0:T(8,128)(2,1)S(1)} %pad_maximum_fusion.refs_4_), channel_id=1, source_target_pairs={{0,24},{1,25},{2,98},{3,99},{4,28},{5,29},{6,102},{7,103},{8,0},{9... | collective-permute-start | bytes 1966088 | tf_op jit(solution)/shard_map/ppermute | solution.py:57
  34.3 10.6 %collective-permute-start.6 = (bf16[4,320,256]{2,1,0:T(8,128)(2,1)S(1)}, bf16[4,320,256]{2,1,0:T(8,128)(2,1)S(1)}, u32[]{:S(2)}, u32[]{:S(2)}) collective-permute-start(bf16[4,320,256]{2,1,0:T(8,128)(2,1)S(1)} %collective-permute-done.5.refs_1_.refs_3_), channel_id=1, source_target_pairs={{0,8},{1,9},{2,34},{3,35},{4,12},{5,13},{6,38},{7,39},{8,16},{9,17... | collective-permute-start | bytes 1966088 | tf_op jit(solution)/shard_map/ppermute | solution.py:57
  35.8 22.8 %collective-permute-start.12 = (bf16[4,320,256]{2,1,0:T(8,128)(2,1)S(1)}, bf16[4,320,256]{2,1,0:T(8,128)(2,1)S(1)}, u32[]{:S(2)}, u32[]{:S(2)}) collective-permute-start(bf16[4,320,256]{2,1,0:T(8,128)(2,1)S(1)} %pad_maximum_fusion.refs_4_), channel_id=1, source_target_pairs={{0,2},{1,3},{2,0},{3,1},{4,6},{5,7},{6,4},{7,5},{8,10},{9,11},{10,... | collective-permute-start | bytes 1966088 | tf_op jit(solution)/shard_map/ppermute | solution.py:57
  35.8 29.1 %collective-permute-start.8 = (bf16[4,320,256]{2,1,0:T(8,128)(2,1)S(1)}, bf16[4,320,256]{2,1,0:T(8,128)(2,1)S(1)}, u32[]{:S(2)}, u32[]{:S(2)}) collective-permute-start(bf16[4,320,256]{2,1,0:T(8,128)(2,1)S(1)} %collective-permute-done.5.refs_1_.refs_3_), channel_id=1, source_target_pairs={{0,2},{1,3},{2,0},{3,1},{4,6},{5,7},{6,4},{7,5},{8,10},{9,11},{10,... | collective-permute-start | bytes 1966088 | tf_op jit(solution)/shard_map/ppermute | solution.py:57
  36.3 8.6 %collective-permute-start.11 = (bf16[256,256]{1,0:T(8,128)(2,1)S(1)}, bf16[256,256]{1,0:T(8,128)(2,1)S(1)}, u32[]{:S(2)}, u32[]{:S(2)}) collective-permute-start(bf16[256,256]{1,0:T(8,128)(2,1)S(1)} %copy-done), channel_id=1, source_target_pairs={{0,5},{1,4},{2,7},{3,6},{4,0},{5,1},{6,2},{7,3},{8,13},{9,12},{10,... | collective-permute-start | bytes 393224 | tf_op jit(solution)/shard_map/ppermute | solution.py:57
  39.4 28.5 %collective-permute-start.4 = (bf16[4,320,256]{2,1,0:T(8,128)(2,1)S(1)}, bf16[4,320,256]{2,1,0:T(8,128)(2,1)S(1)}, u32[]{:S(2)}, u32[]{:S(2)}) collective-permute-start(bf16[4,320,256]{2,1,0:T(8,128)(2,1)S(1)} %collective-permute-done.3.refs_1_.refs_4_), channel_id=1, source_target_pairs={{0,2},{1,3},{2,0},{3,1},{4,6},{5,7},{6,4},{7,5},{8,10},{9,11},{10,... | collective-permute-start | bytes 1966088 | tf_op jit(solution)/shard_map/ppermute | solution.py:57
  44.9 26.9 %collective-permute-start.7 = (bf16[4,320,256]{2,1,0:T(8,128)(2,1)S(1)}, bf16[4,320,256]{2,1,0:T(8,128)(2,1)S(1)}, u32[]{:S(2)}, u32[]{:S(2)}) collective-permute-start(bf16[4,320,256]{2,1,0:T(8,128)(2,1)S(1)} %collective-permute-done.6.refs_3_), channel_id=1, source_target_pairs={{0,2},{1,3},{2,0},{3,1},{4,6},{5,7},{6,4},{7,5},{8,10},{9,11},{10,... | collective-permute-start | bytes 1966088 | tf_op jit(solution)/shard_map/ppermute | solution.py:57
  44.9 7.4 %collective-permute-start.10 = (bf16[256,256]{1,0:T(8,128)(2,1)S(1)}, bf16[256,256]{1,0:T(8,128)(2,1)S(1)}, u32[]{:S(2)}, u32[]{:S(2)}) collective-permute-start(bf16[256,256]{1,0:T(8,128)(2,1)S(1)} %copy-done), channel_id=1, source_target_pairs={{0,1},{1,0},{2,3},{3,2},{4,5},{5,4},{6,7},{7,6},{8,9},{9,8},{10,11... | collective-permute-start | bytes 393224 | tf_op jit(solution)/shard_map/ppermute | solution.py:57
  52.4 6.3 %collective-permute-start.9 = (bf16[256,256]{1,0:T(8,128)(2,1)S(1)}, bf16[256,256]{1,0:T(8,128)(2,1)S(1)}, u32[]{:S(2)}, u32[]{:S(2)}) collective-permute-start(bf16[256,256]{1,0:T(8,128)(2,1)S(1)} %copy-done), channel_id=1, source_target_pairs={{0,4},{1,5},{2,6},{3,7},{4,1},{5,0},{6,3},{7,2},{8,12},{9,13},{10,... | collective-permute-start | bytes 393224 | tf_op jit(solution)/shard_map/ppermute | solution.py:57
  73.8 7.7 %collective-permute-start.13 = (f32[64,256]{1,0:T(8,128)S(1)}, f32[64,256]{1,0:T(8,128)S(1)}, u32[]{:S(2)}, u32[]{:S(2)}) collective-permute-start(f32[64,256]{1,0:T(8,128)S(1)} %get-tuple-element.49), channel_id=1, source_target_pairs={{0,5},{1,4},{2,7},{3,6},{4,0},{5,1},{6,2},{7,3},{8,13},{9,12},{10,... | collective-permute-start | bytes 196616 | tf_op jit(solution)/shard_map/ppermute | solution.py:57
  75.7 5.9 %collective-permute-start.14 = (f32[64,256]{1,0:T(8,128)S(1)}, f32[64,256]{1,0:T(8,128)S(1)}, u32[]{:S(2)}, u32[]{:S(2)}) collective-permute-start(f32[64,256]{1,0:T(8,128)S(1)} %get-tuple-element.50), channel_id=1, source_target_pairs={{0,1},{1,0},{2,3},{3,2},{4,5},{5,4},{6,7},{7,6},{8,9},{9,8},{10,11... | collective-permute-start | bytes 196616 | tf_op jit(solution)/shard_map/ppermute | solution.py:57
  76.3 5.8 %collective-permute-start.15 = (f32[64,256]{1,0:T(8,128)S(1)}, f32[64,256]{1,0:T(8,128)S(1)}, u32[]{:S(2)}, u32[]{:S(2)}) collective-permute-start(f32[64,256]{1,0:T(8,128)S(1)} %get-tuple-element.51), channel_id=1, source_target_pairs={{0,4},{1,5},{2,6},{3,7},{4,1},{5,0},{6,3},{7,2},{8,12},{9,13},{10,... | collective-permute-start | bytes 196616 | tf_op jit(solution)/shard_map/ppermute | solution.py:57
  77.3 1.4 %copy-start.2 = (f32[64,256]{1,0:T(8,128)S(1)}, f32[64,256]{1,0:T(8,128)}, u32[]{:S(2)}) copy-start(f32[64,256]{1,0:T(8,128)} %get-tuple-element.33.refs_6_) | copy-start | bytes 196612
  84.8 1.4 %collective-permute-start.16 = (f32[72,128]{1,0:T(8,128)}, f32[72,128]{1,0:T(8,128)S(1)}, u32[]{:S(2)}, u32[]{:S(2)}) collective-permute-start(f32[72,128]{1,0:T(8,128)} %get-tuple-element.52), channel_id=1, source_target_pairs={{0,2},{1,3},{2,0},{3,1},{4,6},{5,7},{6,4},{7,5},{8,10},{9,11},{10,... | collective-permute-start | bytes 110600 | tf_op jit(solution)/shard_map/ppermute | solution.py:57
  87.0 4.0 %collective-permute-start.19 = (f32[72,128]{1,0:T(8,128)S(1)}, f32[72,128]{1,0:T(8,128)S(1)}, u32[]{:S(2)}, u32[]{:S(2)}) collective-permute-start(f32[72,128]{1,0:T(8,128)S(1)} %add.21), channel_id=1, source_target_pairs={{0,96},{1,97},{2,98},{3,99},{4,100},{5,101},{6,102},{7,103},{8,104... | collective-permute-start | bytes 110600 | tf_op jit(solution)/shard_map/ppermute | solution.py:57
  87.9 5.6 %collective-permute-start.18 = (f32[72,128]{1,0:T(8,128)S(1)}, f32[72,128]{1,0:T(8,128)S(1)}, u32[]{:S(2)}, u32[]{:S(2)}) collective-permute-start(f32[72,128]{1,0:T(8,128)S(1)} %add.21), channel_id=1, source_target_pairs={{0,32},{1,33},{2,34},{3,35},{4,36},{5,37},{6,38},{7,39},{8,40},{9,... | collective-permute-start | bytes 110600 | tf_op jit(solution)/shard_map/ppermute | solution.py:57
  89.0 5.5 %collective-permute-start.17 = (f32[72,128]{1,0:T(8,128)S(1)}, f32[72,128]{1,0:T(8,128)S(1)}, u32[]{:S(2)}, u32[]{:S(2)}) collective-permute-start(f32[72,128]{1,0:T(8,128)S(1)} %add.21), channel_id=1, source_target_pairs={{0,64},{1,65},{2,66},{3,67},{4,68},{5,69},{6,70},{7,71},{8,72},{9,... | collective-permute-start | bytes 110600 | tf_op jit(solution)/shard_map/ppermute | solution.py:57
  94.5 5.4 %collective-permute-start.22 = (f32[72,128]{1,0:T(8,128)S(1)}, f32[72,128]{1,0:T(8,128)S(1)}, u32[]{:S(2)}, u32[]{:S(2)}) collective-permute-start(f32[72,128]{1,0:T(8,128)S(1)} %add_add_fusion.1), channel_id=1, source_target_pairs={{0,24},{1,25},{2,26},{3,27},{4,28},{5,29},{6,30},{7,31},{8,0},{9,1... | collective-permute-start | bytes 110600 | tf_op jit(solution)/shard_map/ppermute | solution.py:57
  97.5 4.0 %collective-permute-start.21 = (f32[72,128]{1,0:T(8,128)S(1)}, f32[72,128]{1,0:T(8,128)S(1)}, u32[]{:S(2)}, u32[]{:S(2)}) collective-permute-start(f32[72,128]{1,0:T(8,128)S(1)} %add_add_fusion.1), channel_id=1, source_target_pairs={{0,8},{1,9},{2,10},{3,11},{4,12},{5,13},{6,14},{7,15},{8,16},{9,17... | collective-permute-start | bytes 110600 | tf_op jit(solution)/shard_map/ppermute | solution.py:57
  97.5 5.5 %collective-permute-start.20 = (f32[72,128]{1,0:T(8,128)S(1)}, f32[72,128]{1,0:T(8,128)S(1)}, u32[]{:S(2)}, u32[]{:S(2)}) collective-permute-start(f32[72,128]{1,0:T(8,128)S(1)} %add_add_fusion.1), channel_id=1, source_target_pairs={{0,16},{1,17},{2,18},{3,19},{4,20},{5,21},{6,22},{7,23},{8,24},{9,... | collective-permute-start | bytes 110600 | tf_op jit(solution)/shard_map/ppermute | solution.py:57
  103.0 9.2 %copy-start.4 = (f32[72,128]{1,0:T(8,128)}, f32[72,128]{1,0:T(8,128)S(1)}, u32[]{:S(2)}) copy-start(f32[72,128]{1,0:T(8,128)S(1)} %add_add_fusion.own_ref) | copy-start | bytes 110596
  103.0 4.3 %collective-permute-start.25 = (f32[72,128]{1,0:T(8,128)S(1)}, f32[72,128]{1,0:T(8,128)S(1)}, u32[]{:S(2)}, u32[]{:S(2)}) collective-permute-start(f32[72,128]{1,0:T(8,128)S(1)} %add_add_fusion.own_ref), channel_id=1, source_target_pairs={{0,5},{1,4},{2,7},{3,6},{4,0},{5,1},{6,2},{7,3},{8,13},{9,12},{10,... | collective-permute-start | bytes 110600 | tf_op jit(solution)/shard_map/ppermute | solution.py:57
  105.3 5.5 %collective-permute-start.24 = (f32[72,128]{1,0:T(8,128)S(1)}, f32[72,128]{1,0:T(8,128)S(1)}, u32[]{:S(2)}, u32[]{:S(2)}) collective-permute-start(f32[72,128]{1,0:T(8,128)S(1)} %add_add_fusion.own_ref), channel_id=1, source_target_pairs={{0,1},{1,0},{2,3},{3,2},{4,5},{5,4},{6,7},{7,6},{8,9},{9,8},{10,11... | collective-permute-start | bytes 110600 | tf_op jit(solution)/shard_map/ppermute | solution.py:57
  107.0 5.2 %collective-permute-start.23 = (f32[72,128]{1,0:T(8,128)S(1)}, f32[72,128]{1,0:T(8,128)S(1)}, u32[]{:S(2)}, u32[]{:S(2)}) collective-permute-start(f32[72,128]{1,0:T(8,128)S(1)} %add_add_fusion.own_ref), channel_id=1, source_target_pairs={{0,4},{1,5},{2,6},{3,7},{4,1},{5,0},{6,3},{7,2},{8,12},{9,13},{10,... | collective-permute-start | bytes 110600 | tf_op jit(solution)/shard_map/ppermute | solution.py:57
  107.3 4.9 %copy-start.8 = (f32[72,128]{1,0:T(8,128)}, f32[72,128]{1,0:T(8,128)S(1)}, u32[]{:S(2)}) copy-start(f32[72,128]{1,0:T(8,128)S(1)} %collective-permute-done.25.three_ref) | copy-start | bytes 110596
  110.8 1.4 %copy-start.9 = (f32[72,128]{1,0:T(8,128)}, f32[72,128]{1,0:T(8,128)S(1)}, u32[]{:S(2)}) copy-start(f32[72,128]{1,0:T(8,128)S(1)} %collective-permute-done.24.two_ref) | copy-start | bytes 110596
  (5 other events, 3.1 us)
